TPU v7x, 32 devices: a whole 2x2x4 slice. The times are simulated.
32 devices in a mesh: dp: 2 (over x), mp: 16 (over z, y, core).
Axes of the slice: x: 2, y: 2, z: 4, core: 2. Of those that a mesh axis runs over, the one named last changes fastest.
Arguments:
- inputs: bfloat16 [8192, 256], P('mp', 'dp'), may hold values from -6 to 6
- cotangent: bfloat16 [8192, 256], P('mp', 'dp'), may hold values from -6 to 6
- w_up: bfloat16 [4096, 4096], P('mp'), may hold values from -0.1875 to 0.1875
- w_down: bfloat16 [4096, 4096], P('mp'), may hold values from -0.125 to 0.125
- col_up: int32 [4096], P('mp'), may hold values from 0 to 15, as said below
- row_down: int32 [4096], P('mp'), may hold values from 0 to 15, as said below
- owner_up: int32 [4096, 1], P('mp'), may hold values from 0 to 1; in each aligned block of 256 rows (0 to 255, 256 to 511, ...) at most 160 rows name the same one
- owner_down: int32 [4096, 1], P('mp'), may hold values from 0 to 1; in each aligned block of 256 rows (0 to 255, 256 to 511, ...) at most 160 rows name the same one
Outputs:
- active: bfloat16 [16384, 256], P('mp', 'dp')
- input_grad: bfloat16 [8192, 256], P('mp', 'dp')
- grad_up: bfloat16 [5120, 4096], P(('dp', 'mp'))
- grad_down: bfloat16 [5120, 4096], P(('dp', 'mp'))
Inputs may be any that keep to these rules, and one draw needn't show every extreme that they name: `col_up`: within each list of 256 entries of one index of mp, the 2 entries of each block row r (positions 2 * r to 2 * r + 1) are different block columns. `row_down`: within each list of 256 entries of one index of mp, the 2 entries of each block column r are different block rows. `owner_up`: within the 256 entries of each index of mp no index of dp appears more than 160 times, and some index of dp appears exactly 160 times. `owner_down`: within the 256 entries of each index of mp no index of dp appears more than 160 times, and some index of dp appears exactly 160 times.
All inputs are finite; a program needn't handle non-finite values.
Results may differ from a plain program's by a relative error of at most 0.0059.
Values may be sent and summed in bfloat16 or wider, within the bound.
No kernel may reach another device: no remote copies, remote signals or barrier semaphores. Data moves between devices by JAX's collectives and lax.ppermute only.
A program may use at most 128 MiB of HBM per device.

v0:
```python
import functools
import jax
import jax.numpy as jnp
from jax import lax
from jax.experimental import pallas as pl
from jax.experimental.pallas import tpu as pltpu
from jax.sharding import PartitionSpec as P

BS = 64
FBLK = 16
KB = 2
GROUP = 16
RELAYOUT = 32
PITCH = BS + 1
VMEM = pltpu.VMEM
SMEM = pltpu.SMEM
ANY = pl.ANY
BF = jnp.bfloat16
F32 = jnp.float32


def swap(value, axis, mask):
    size = lax.axis_size(axis)
    return lax.ppermute(value, axis, [(i, i ^ mask) for i in range(size)])


def relayout_kernel(blocks, up_ref, down_ref, up_out, down_out, low, high):
    lane = lax.broadcasted_iota(jnp.int32, (BS, 2 * BS), 1) < BS
    for src, out in ((up_ref, up_out), (down_ref, down_out)):
        for a in range(BS // 2):
            tile = src[:, a * 2 * BS : (a + 1) * 2 * BS].astype(F32)
            turned = pltpu.roll(tile, BS, 1)
            low[pl.ds(2 * a, blocks, stride=PITCH), :] = tile
            low[pl.ds(2 * a + 1, blocks, stride=PITCH), :] = turned
            high[pl.ds(2 * a, blocks, stride=PITCH), :] = turned
            high[pl.ds(2 * a + 1, blocks, stride=PITCH), :] = tile
        for r in range(blocks // KB):
            first = low[2 * r * PITCH : 2 * r * PITCH + BS, :]
            second = high[(2 * r + 1) * PITCH : (2 * r + 1) * PITCH + BS, :]
            out[r * BS : (r + 1) * BS, :] = jnp.where(lane, first, second).astype(BF)


def relayout(w_up, w_down):
    total = w_up.shape[0]
    blocks = RELAYOUT
    row = pl.BlockSpec((blocks, BS * BS), lambda i: (i, 0))
    tiles = pl.BlockSpec((blocks * BS // KB, KB * BS), lambda i: (i, 0))
    shape = jax.ShapeDtypeStruct((total * BS // KB, KB * BS), BF)
    return pl.pallas_call(
        functools.partial(relayout_kernel, blocks),
        grid=(total // blocks,),
        in_specs=[row, row],
        out_specs=[tiles, tiles],
        out_shape=[shape, shape],
        scratch_shapes=[VMEM((blocks * PITCH, 2 * BS), F32)] * 2,
        cost_estimate=pl.CostEstimate(flops=0, bytes_accessed=14 << 20, transcendentals=0),
        name="relayout",
    )(w_up, w_down)


def slots_kernel(me_ref, up_ref, down_ref, up_tab, down_tab):
    group = me_ref[0]
    total = up_ref.shape[0]
    pad = up_tab.shape[0]

    def body(e, carry):
        a, b = carry
        up_tab[a] = e
        down_tab[b] = e
        a = a + (up_ref[e] == group).astype(jnp.int32)
        b = b + (down_ref[e] == group).astype(jnp.int32)
        return a, b

    a, b = lax.fori_loop(0, total, body, (jnp.int32(0), jnp.int32(0)))

    def rest_up(t, carry):
        up_tab[t] = -1
        return carry

    def rest_down(t, carry):
        down_tab[t] = -1
        return carry

    lax.fori_loop(a, pad, rest_up, 0)
    lax.fori_loop(b, pad, rest_down, 0)


def slots(group, owner_up, owner_down):
    total = owner_up.shape[0]
    shape = jax.ShapeDtypeStruct((total + 8,), jnp.int32)
    spec = pl.BlockSpec(memory_space=SMEM)
    return pl.pallas_call(
        slots_kernel,
        in_specs=[spec] * 3,
        out_specs=[spec] * 2,
        out_shape=[shape] * 2,
        cost_estimate=pl.CostEstimate(flops=0, bytes_accessed=1 << 20, transcendentals=0),
        name="slots",
    )(group, owner_up, owner_down)


def gelu_slope(value):
    scale = 0.7978845608028654
    cubic = 0.044715
    inner = scale * (value + cubic * value * value * value)
    tanh_part = jnp.tanh(inner)
    gate = 0.5 * (1.0 + tanh_part)
    slope = gate + 0.5 * value * (1.0 - tanh_part * tanh_part) * scale * (
        1.0 + 3.0 * cubic * value * value
    )
    return value * gate, slope


def add_blocks(place, where_ref, w_ref, x_refs, acc, rows, is_up):
    per = rows // BS
    zero = jnp.zeros((BS, acc.shape[1]), BF)
    width = acc.shape[1]
    done = 0
    for x_ref in x_refs:
        chunks = x_ref.shape[0] // rows

        def body(i, carry, x_ref=x_ref, done=done):
            start = place[done + i] * per
            for rr in range(per):
                r = start + rr
                w = w_ref[pl.ds(pl.multiple_of(r * BS, BS), BS), :]
                x = x_ref[pl.ds(pl.multiple_of(i * rows + rr * BS, BS), BS), :]
                if is_up:
                    t = lax.dot_general(
                        w, x, (((0,), (0,)), ((), ())), preferred_element_type=F32
                    )
                    parts = [t[q * BS : (q + 1) * BS, :] for q in range(KB)]
                else:
                    right = jnp.concatenate(
                        [
                            jnp.concatenate([x, zero], axis=1),
                            jnp.concatenate([zero, x], axis=1),
                        ],
                        axis=0,
                    )
                    t = jnp.dot(w, right, preferred_element_type=F32)
                    parts = [t[:, q * width : (q + 1) * width] for q in range(KB)]
                for q in range(KB):
                    to = pl.ds(pl.multiple_of(where_ref[KB * r + q] * BS, BS), BS)
                    acc[to, :] += parts[q]
            return carry

        lax.fori_loop(0, chunks, body, 0)
        done += chunks


def hidden_kernel(rows, is_up, count, first, last, *refs):
    place, where_ref, w_ref = refs[:3]
    x_refs = refs[3 : 3 + count]
    rest = list(refs[3 + count :])
    acc_in = None if first else rest.pop(0)
    hidden = rest.pop(0) if last else None
    if last:
        both, acc = rest
    else:
        (acc,) = rest
    acc[...] = jnp.zeros_like(acc) if first else acc_in[...]
    add_blocks(place, where_ref, w_ref, x_refs, acc, rows, is_up)
    if last:
        ff = acc.shape[0]

        def body(i, carry):
            at = pl.multiple_of(i * BS, BS)
            value, slope = gelu_slope(hidden[pl.ds(at, BS), :])
            both[pl.ds(at, BS), :] = value.astype(BF)
            both[pl.ds(ff + at, BS), :] = (acc[pl.ds(at, BS), :] * slope).astype(BF)
            return carry

        lax.fori_loop(0, ff // BS, body, 0)


def hidden_sum(rows, is_up, place, where, w, pieces, acc=None, hidden=None):
    ff, tokens = FBLK * BS, pieces[0].shape[1]
    smem = pl.BlockSpec(memory_space=SMEM)
    vmem = pl.BlockSpec(memory_space=VMEM)
    more = [x for x in (acc, hidden) if x is not None]
    if hidden is None:
        out, scratch = jax.ShapeDtypeStruct((ff, tokens), F32), []
    else:
        out, scratch = jax.ShapeDtypeStruct((2 * ff, tokens), BF), [VMEM((ff, tokens), F32)]
    return pl.pallas_call(
        functools.partial(
            hidden_kernel, rows, is_up, len(pieces), acc is None, hidden is not None
        ),
        in_specs=[smem, smem] + [vmem] * (1 + len(pieces) + len(more)),
        out_specs=vmem,
        out_shape=out,
        scratch_shapes=scratch,
        compiler_params=pltpu.CompilerParams(vmem_limit_bytes=24 << 20),
        cost_estimate=pl.CostEstimate(
            flops=1 << 29, bytes_accessed=6 << 20, transcendentals=0
        ),
        name=("hidden" if is_up else "upper") + ("" if hidden is None else "_last"),
    )(place, where, w, *pieces, *more)


def input_grad_kernel(rows, place, col_ref, w_ref, both_ref, out):
    per = rows // BS
    chunks = out.shape[0] // rows
    base = both_ref.shape[0] // 2

    def body(i, carry):
        start = place[i] * per
        for rr in range(per):
            r = start + rr
            w = w_ref[pl.ds(pl.multiple_of(r * BS, BS), BS), :]
            parts = [
                both_ref[pl.ds(pl.multiple_of(base + col_ref[KB * r + q] * BS, BS), BS), :]
                for q in range(KB)
            ]
            t = jnp.dot(w, jnp.concatenate(parts, axis=0), preferred_element_type=F32)
            out[pl.ds(pl.multiple_of(i * rows + rr * BS, BS), BS), :] = t.astype(out.dtype)
        return carry

    lax.fori_loop(0, chunks, body, 0)


def input_grad_part(rows, place, col, w, both, dtype):
    smem = pl.BlockSpec(memory_space=SMEM)
    vmem = pl.BlockSpec(memory_space=VMEM)
    return pl.pallas_call(
        functools.partial(input_grad_kernel, rows),
        in_specs=[smem, smem, vmem, vmem],
        out_specs=vmem,
        out_shape=jax.ShapeDtypeStruct((place.shape[0] * rows, both.shape[1]), dtype),
        compiler_params=pltpu.CompilerParams(vmem_limit_bytes=16 << 20),
        cost_estimate=pl.CostEstimate(flops=1 << 29, bytes_accessed=4 << 20, transcendentals=0),
        name="input_grad_part",
    )(place, col, w, both)


def grads_kernel(groups, pieces, capacity, batch, is_up, *refs):
    tab, order, place = refs[:3]
    feature_refs = refs[3 : 3 + groups * pieces]
    both_refs = refs[3 + groups * pieces : 3 + groups * pieces + groups]
    out = refs[3 + groups * pieces + groups]
    features, tiles, sem = refs[4 + groups * pieces + groups :]
    size = feature_refs[0].shape[0]
    base = both_refs[0].shape[0] // 2 if is_up else 0
    copies = []
    for g in range(groups):
        for p in range(pieces):
            n = g * pieces + p
            copies.append(
                pltpu.make_async_copy(
                    feature_refs[n], features.at[g, pl.ds(p * size, size), :], sem.at[n]
                )
            )
    for copy in copies:
        copy.start()
    for copy in copies:
        copy.wait()
    low = lax.broadcasted_iota(jnp.int32, (batch, 2 * BS), 1) < BS

    def body(b, carry):
        for u in range(batch):
            e = tab[b * batch + u]
            live = e >= 0
            e = jnp.maximum(e, 0)
            at = pl.multiple_of(place[e // KB], BS)
            to = pl.multiple_of(base + order[e] * BS, BS)
            f = jnp.concatenate([features[g, pl.ds(at, BS), :] for g in range(groups)], axis=1)
            h = jnp.concatenate([ref[pl.ds(to, BS), :] for ref in both_refs], axis=1)
            left, right = (f, h) if is_up else (h, f)
            right = jnp.concatenate([right, right], axis=0)
            t = lax.dot_general(
                left, right, (((1,), (1,)), ((), ())), preferred_element_type=F32
            )
            tiles[u * PITCH : u * PITCH + BS, :] = jnp.where(live, t, 0.0)
        for a in range(BS // 2):
            even = tiles[pl.ds(2 * a, batch, stride=PITCH), :]
            odd = tiles[pl.ds(2 * a + 1, batch, stride=PITCH), :]
            out[
                pl.ds(pl.multiple_of(b * batch, batch), batch), a * 2 * BS : (a + 1) * 2 * BS
            ] = jnp.where(low, even, odd).astype(BF)
        return carry

    lax.fori_loop(0, capacity // batch, body, 0)


def owned_grads(tab, order, place, features, boths, capacity, is_up):
    groups = len(boths)
    pieces = len(features[0])
    batch = GROUP if capacity % GROUP == 0 else 8
    flat = [piece for group in features for piece in group]
    tokens = boths[0].shape[1]
    total = sum(piece.shape[0] for piece in features[0])
    smem = pl.BlockSpec(memory_space=SMEM)
    vmem = pl.BlockSpec(memory_space=VMEM)
    return pl.pallas_call(
        functools.partial(grads_kernel, groups, pieces, capacity, batch, is_up),
        in_specs=[smem] * 3 + [pl.BlockSpec(memory_space=ANY)] * len(flat) + [vmem] * groups,
        out_specs=vmem,
        out_shape=jax.ShapeDtypeStruct((capacity, BS * BS), BF),
        scratch_shapes=[
            VMEM((groups, total, tokens), BF),
            VMEM((batch * PITCH, 2 * BS), F32),
            pltpu.SemaphoreType.DMA((groups * pieces,)),
        ],
        compiler_params=pltpu.CompilerParams(vmem_limit_bytes=48 << 20),
        cost_estimate=pl.CostEstimate(
            flops=2 * capacity * BS * BS * tokens * groups * 4,
            bytes_accessed=6 << 20,
            transcendentals=0,
        ),
        name="grads_up" if is_up else "grads_down",
    )(tab, order, place, *flat, *boths)


def per_device(inputs, cotangent, w_up, w_down, col_up, row_down, owner_up, owner_down):
    rows, tokens = inputs.shape
    blocks = w_up.shape[0]
    groups = lax.axis_size("dp")
    members = lax.axis_size("mp")
    capacity = 5 * blocks // (4 * groups)
    ff = FBLK * BS
    me = lax.axis_index("mp")
    far = members // 4
    half = members // 2

    step = jnp.arange(half, dtype=jnp.int32)
    masks = (step // far) * 2 + (step % far) * 4
    mine = jnp.bitwise_xor(me, masks).astype(jnp.int32)
    other = jnp.bitwise_xor(mine, 1)
    near_place = jnp.concatenate([mine[:far], other[:far]])
    after = lax.optimization_barrier

    others = range(1, groups)
    in_parts = [inputs] + [swap(inputs, "mp", 4 * z) for z in range(1, far)]
    up_w, down_w = relayout(w_up, w_down)
    in_parts, up_w, down_w = after((in_parts, up_w, down_w))
    in_near = jnp.concatenate(in_parts, axis=0)
    in_far = swap(in_near, "mp", 2)
    in_near_o = [swap(in_near, "dp", d) for d in others]
    in_near_b = swap(in_near, "mp", 1)
    in_near, cotangent = after((in_near, cotangent))
    cot_parts = [cotangent] + [swap(cotangent, "mp", 4 * z) for z in range(1, far)]
    up_tab, down_tab = slots(
        lax.axis_index("dp").reshape(1), owner_up[:, 0], owner_down[:, 0]
    )
    hidden = hidden_sum(rows, True, near_place, col_up, up_w, [in_near, in_near_b])
    cot_parts, hidden, up_tab, down_tab = after((cot_parts, hidden, up_tab, down_tab))
    cot_near = jnp.concatenate(cot_parts, axis=0)
    cot_far = swap(cot_near, "mp", 2)
    in_far_o = [swap(in_far, "dp", d) for d in others]
    in_far_b = swap(in_far, "mp", 1)
    cot_near_b = swap(cot_near, "mp", 1)
    cot_near_o = [swap(cot_near, "dp", d) for d in others]
    hidden = hidden_sum(
        rows, True, jnp.concatenate([mine[far:], other[far:]]), col_up, up_w,
        [in_far, in_far_b], hidden,
    )
    upper = hidden_sum(rows, False, near_place, row_down, down_w, [cot_near, cot_near_b])
    cot_far, hidden, upper, in_near_o = after((cot_far, hidden, upper, in_near_o))
    cot_far_b = swap(cot_far, "mp", 1)
    cot_far_o = [swap(cot_far, "dp", d) for d in others]
    upper = hidden_sum(rows, False, mine[far:], row_down, down_w, [cot_far], upper)
    cot_far_b, in_far_o = after((cot_far_b, in_far_o))
    both = hidden_sum(rows, False, other[far:], row_down, down_w, [cot_far_b], upper, hidden)
    both_o = [swap(both, "dp", d) for d in others]

    sent = input_grad_part(rows, other, col_up, up_w, both, BF)
    arrived = swap(sent, "mp", 1)
    terms = input_grad_part(rows, mine, col_up, up_w, both, F32)
    terms = terms + arrived.astype(F32)
    cut = far * rows
    arrived = swap(terms[cut:].astype(BF), "mp", 2)
    arrived, cot_near_o = after((arrived, cot_near_o))
    terms = terms[:cut] + arrived.astype(F32)
    total = terms[:rows]
    pieces = [
        swap(terms[z * rows : (z + 1) * rows].astype(BF), "mp", 4 * z) for z in range(1, far)
    ]

    in_all = [[in_near, in_far, in_near_b, in_far_b]]
    cot_all = [[cot_near, cot_far, cot_near_b, cot_far_b]]
    both_all = [both] + both_o
    for d in others:
        ours = [in_near_o[d - 1], in_far_o[d - 1]]
        in_all.append(ours + [swap(x, "mp", 1) for x in ours])
        ours = [cot_near_o[d - 1], cot_far_o[d - 1]]
        cot_all.append(ours + [swap(x, "mp", 1) for x in ours])

    row = jnp.arange(members * rows // BS, dtype=jnp.int32)
    apart = jnp.bitwise_xor(row // (rows // BS), me)
    spot = (apart & 1) * half + ((apart >> 1) & 1) * far + (apart >> 2)
    place = spot * rows + (row % (rows // BS)) * BS
    grad_up = owned_grads(up_tab, col_up, place, in_all, both_all, capacity, True)
    pieces, grad_up = after((pieces, grad_up))
    for piece in pieces:
        total = total + piece.astype(F32)
    input_grad = total.astype(BF)
    grad_down = owned_grads(down_tab, row_down, place, cot_all, both_all, capacity, False)
    return both[:ff], input_grad, grad_up, grad_down


def solution(mesh):
    placed = (
        P("mp", "dp"),
        P("mp", "dp"),
        P("mp", None),
        P("mp", None),
        P("mp"),
        P("mp"),
        P("mp", None),
        P("mp", None),
    )
    return jax.shard_map(
        per_device,
        mesh=mesh,
        in_specs=placed,
        out_specs=(P("mp", "dp"), P("mp", "dp"), P(("dp", "mp"), None), P(("dp", "mp"), None)),
        check_vma=False,
    )
```

profile of v0, /device:TPU:0, one launch (start us, length us, event | category | flops | bytes accessed | tf_op | source)
XLA Modules:
  0.0 124.1 jit_solution(756208663699546250)
XLA Ops:
  0.6 3.1 %collective-permute-start = (bf16[512,128]{1,0:T(8,128)(2,1)}, bf16[512,128]{1,0:T(8,128)(2,1)S(1)}, u32[]{:S(2)}, u32[]{:S(2)}) collective-permute-start(bf16[512,128]{1,0:T(8,128)(2,1)} %param.8), channel_id=1, source_target_pairs={{0,4},{1,5},{2,6},{3,7},{4,0},{5,1},{6,2},{7,3},{8,12},{9,13},{10,... | collective-permute-start | bytes 393224 | tf_op jit(solution)/shard_map/ppermute | solution.py:24
  3.7 2.6 %collective-permute-start.1 = (bf16[512,128]{1,0:T(8,128)(2,1)}, bf16[512,128]{1,0:T(8,128)(2,1)S(1)}, u32[]{:S(2)}, u32[]{:S(2)}) collective-permute-start(bf16[512,128]{1,0:T(8,128)(2,1)} %param.8), channel_id=1, source_target_pairs={{0,8},{1,9},{2,10},{3,11},{4,12},{5,13},{6,14},{7,15},{8,0},{9,1},... | collective-permute-start | bytes 393224 | tf_op jit(solution)/shard_map/ppermute | solution.py:24
  6.3 7.7 %relayout.1 = (bf16[8192,128]{1,0:T(8,128)(2,1)}, bf16[8192,128]{1,0:T(8,128)(2,1)}) custom-call(bf16[256,4096]{1,0:T(8,128)(2,1)} %up_ref.1, bf16[256,4096]{1,0:T(8,128)(2,1)} %down_ref.1), custom_call_target="tpu_custom_call" | custom-call | bytes 14680064 | tf_op jit(solution)/shard_map/relayout/pallas_call | solution.py:49
  14.1 0.0 collective-permute-done
  14.1 2.8 %collective-permute-done.1 = bf16[512,128]{1,0:T(8,128)(2,1)S(1)} collective-permute-done((bf16[512,128]{1,0:T(8,128)(2,1)}, bf16[512,128]{1,0:T(8,128)(2,1)S(1)}, u32[]{:S(2)}, u32[]{:S(2)}) %collective-permute-start.1) | collective-permute-done | bytes 131104 | tf_op jit(solution)/shard_map/ppermute | solution.py:24
  16.9 0.0 collective-permute-done.2
  17.0 0.1 collective-permute-start.6
  17.1 0.1 fusion.13
  17.1 1.5 %collective-permute-start.8 = (bf16[2048,128]{1,0:T(8,128)(2,1)S(1)}, bf16[2048,128]{1,0:T(8,128)(2,1)S(1)}, u32[]{:S(2)}, u32[]{:S(2)}) collective-permute-start(bf16[2048,128]{1,0:T(8,128)(2,1)S(1)} %constant_dynamic-update-slice_fusion.refs_3_), channel_id=1, source_target_pairs={{0,2},{1,3},{2,0},{3,1},{4,6},{5,7},{6,4},{7,5},{8,10},{9,11},{10,... | collective-permute-start | bytes 1572872 | tf_op jit(solution)/shard_map/ppermute | solution.py:24
  18.7 0.1 fusion.12
  18.7 5.0 %slots.1 = (s32[264]{0:T(512)}, s32[264]{0:T(512)}) custom-call(s32[1]{0:T(128)} %bitcast.me_ref, s32[256]{0:T(256)} %bitcast.3, s32[256]{0:T(256)} %bitcast.4), custom_call_target="tpu_custom_call" | custom-call | bytes 1048576 | tf_op jit(solution)/shard_map/slots/pallas_call | solution.py:92
  23.8 2.0 %collective-permute-start.3 = (bf16[512,128]{1,0:T(8,128)(2,1)S(1)}, bf16[512,128]{1,0:T(8,128)(2,1)S(1)}, u32[]{:S(2)}, u32[]{:S(2)}) collective-permute-start(bf16[512,128]{1,0:T(8,128)(2,1)S(1)} %copy-done.8), channel_id=1, source_target_pairs={{0,4},{1,5},{2,6},{3,7},{4,0},{5,1},{6,2},{7,3},{8,12},{9,13},{10,... | collective-permute-start | bytes 393224 | tf_op jit(solution)/shard_map/ppermute | solution.py:24
  25.8 1.1 collective-permute-start.4
  26.9 1.4 %collective-permute-start.5 = (bf16[512,128]{1,0:T(8,128)(2,1)S(1)}, bf16[512,128]{1,0:T(8,128)(2,1)S(1)}, u32[]{:S(2)}, u32[]{:S(2)}) collective-permute-start(bf16[512,128]{1,0:T(8,128)(2,1)S(1)} %copy-done.8), channel_id=1, source_target_pairs={{0,12},{1,13},{2,14},{3,15},{4,8},{5,9},{6,10},{7,11},{8,4},{9,5},... | collective-permute-start | bytes 393224 | tf_op jit(solution)/shard_map/ppermute | solution.py:24
  28.3 0.1 pad_add_fusion.refs_0_
  28.3 0.0 collective-permute-done.6.refs_4_.refs_5_
  28.3 1.6 %copy-done = bf16[8192,128]{1,0:T(8,128)(2,1)S(1)} copy-done((bf16[8192,128]{1,0:T(8,128)(2,1)S(1)}, bf16[8192,128]{1,0:T(8,128)(2,1)}, u32[]{:S(2)}) %copy-start) | copy-done | bytes 2097176
  29.9 2.9 %hidden.2.refs_5_ = f32[1024,128]{1,0:T(8,128)S(1)} custom-call(s32[8]{0:T(128)S(1)} %pad_add_fusion.refs_0_, s32[256]{0:T(256)S(1)} %copy-done.3, bf16[8192,128]{1,0:T(8,128)(2,1)S(1)} %copy-done, bf16[2048,128]{1,0:T(8,128)(2,1)S(1)} %constant_dynamic-update-slice_fusion.refs_3_, bf16[2048,128]{1,0:T(8,128)(2,1)S(1)} %collective-permute-done.6.refs_4_.refs_5_), custom_call_target="tpu_custom_call" | custom-call | flops 536870912 | bytes 6291456 | tf_op jit(solution)/shard_map/hidden/pallas_call | solution.py:186
  32.9 0.0 collective-permute-done.3
  32.9 5.8 %collective-permute-done.4 = bf16[512,128]{1,0:T(8,128)(2,1)S(1)} collective-permute-done((bf16[512,128]{1,0:T(8,128)(2,1)S(1)}, bf16[512,128]{1,0:T(8,128)(2,1)S(1)}, u32[]{:S(2)}, u32[]{:S(2)}) %collective-permute-start.4) | collective-permute-done | bytes 131104 | tf_op jit(solution)/shard_map/ppermute | solution.py:24
  38.7 0.0 collective-permute-done.5
  38.8 0.0 collective-permute-done.8.refs_3_.refs_4_
  38.8 0.1 collective-permute-start.9
  38.9 0.6 collective-permute-start.10
  39.4 1.5 %collective-permute-start.11 = (bf16[2048,128]{1,0:T(8,128)(2,1)S(1)}, bf16[2048,128]{1,0:T(8,128)(2,1)S(1)}, u32[]{:S(2)}, u32[]{:S(2)}) collective-permute-start(bf16[2048,128]{1,0:T(8,128)(2,1)S(1)} %constant_dynamic-update-slice_fusion.refs_3_), channel_id=1, source_target_pairs={{0,16},{16,0},{1,17},{17,1},{2,18},{18,2},{3,19},{19,3},{4,20},{20... | collective-permute-start | bytes 1572872 | tf_op jit(solution)/shard_map/ppermute | solution.py:24
  40.9 0.5 collective-permute-start.7
  41.4 0.1 pad_add_fusion.1.refs_0_
  41.5 0.5 collective-permute-start.13
  42.1 2.9 %hidden.3.refs_5_ = f32[1024,128]{1,0:T(8,128)S(1)} custom-call(s32[8]{0:T(128)S(1)} %pad_add_fusion.1.refs_0_, s32[256]{0:T(256)S(1)} %copy-done.3, bf16[8192,128]{1,0:T(8,128)(2,1)S(1)} %copy-done, bf16[2048,128]{1,0:T(8,128)(2,1)S(1)} %collective-permute-done.8.refs_3_.refs_4_, bf16[2048,128]{1,0:T(8,128)(2,1)S(1)} %collective-permute-done.9.refs_4_.refs_6_, ...), custom_call_target="tpu_custom_call" | custom-call | flops 536870912 | bytes 6291456 | tf_op jit(solution)/shard_map/hidden/pallas_call | solution.py:186
  45.0 2.6 %upper.2.refs_4_ = f32[1024,128]{1,0:T(8,128)S(1)} custom-call(s32[8]{0:T(128)S(1)} %pad_add_fusion.refs_0_, s32[256]{0:T(256)S(1)} %copy-done.4, bf16[8192,128]{1,0:T(8,128)(2,1)S(1)} %copy-done.2, bf16[2048,128]{1,0:T(8,128)(2,1)S(1)} %constant_dynamic-update-slice_fusion.4.refs_3_, bf16[2048,128]{1,0:T(8,128)(2,1)S(1)} %collective-permute-done.10.refs_4_.refs_5_), custom_call_target="tpu_custom_call" | custom-call | flops 536870912 | bytes 6291456 | tf_op jit(solution)/shard_map/upper/pallas_call | solution.py:186
  47.6 6.6 %collective-permute-done.11.refs_7_ = bf16[2048,128]{1,0:T(8,128)(2,1)S(1)} collective-permute-done((bf16[2048,128]{1,0:T(8,128)(2,1)S(1)}, bf16[2048,128]{1,0:T(8,128)(2,1)S(1)}, u32[]{:S(2)}, u32[]{:S(2)}) %collective-permute-start.11) | collective-permute-done | bytes 524320 | tf_op jit(solution)/shard_map/ppermute | solution.py:24
  54.2 0.3 collective-permute-done.7.refs_3_.refs_4_
  54.6 1.6 %upper.3.refs_4_ = f32[1024,128]{1,0:T(8,128)S(1)} custom-call(s32[4]{0:T(128)S(1)} %get-tuple-element.71.refs_0_, s32[256]{0:T(256)S(1)} %copy-done.4, bf16[8192,128]{1,0:T(8,128)(2,1)S(1)} %copy-done.2, bf16[2048,128]{1,0:T(8,128)(2,1)S(1)} %collective-permute-done.7.refs_3_.refs_4_, f32[1024,128]{1,0:T(8,128)S(1)} %upper.2.refs_4_), custom_call_target="tpu_custom_call" | custom-call | flops 536870912 | bytes 6291456 | tf_op jit(solution)/shard_map/upper/pallas_call | solution.py:186
  56.1 8.4 %collective-permute-done.13.refs_8_ = bf16[2048,128]{1,0:T(8,128)(2,1)S(1)} collective-permute-done((bf16[2048,128]{1,0:T(8,128)(2,1)S(1)}, bf16[2048,128]{1,0:T(8,128)(2,1)S(1)}, u32[]{:S(2)}, u32[]{:S(2)}) %collective-permute-start.13) | collective-permute-done | bytes 524320 | tf_op jit(solution)/shard_map/ppermute | solution.py:24
  64.6 0.0 collective-permute-done.12.refs_3_.refs_6_
  64.6 2.1 %upper_last.1.both_ref.refs_11_ = bf16[2048,128]{1,0:T(8,128)(2,1)S(1)} custom-call(s32[4]{0:T(128)S(1)} %get-tuple-element.74.refs_0_, s32[256]{0:T(256)S(1)} %copy-done.4, bf16[8192,128]{1,0:T(8,128)(2,1)S(1)} %copy-done.2, bf16[2048,128]{1,0:T(8,128)(2,1)S(1)} %collective-permute-done.12.refs_3_.refs_6_, f32[1024,128]{1,0:T(8,128)S(1)} %upper.3.refs_4_, ...), custom_call_target="tpu_custom_call" | custom-call | flops 536870912 | bytes 6291456 | tf_op jit(solution)/shard_map/upper_last/pallas_call | solution.py:186
  66.7 2.3 %input_grad_part.3 = bf16[4096,128]{1,0:T(8,128)(2,1)S(1)} custom-call(s32[8]{0:T(128)S(1)} %get-tuple-element.76.place, s32[256]{0:T(256)S(1)} %copy-done.3, bf16[8192,128]{1,0:T(8,128)(2,1)S(1)} %copy-done.1, bf16[2048,128]{1,0:T(8,128)(2,1)S(1)} %upper_last.1.both_ref.refs_11_), custom_call_target="tpu_custom_call" | custom-call | flops 536870912 | bytes 4194304 | tf_op jit(solution)/shard_map/input_grad_part/pallas_call | solution.py:226
  68.9 0.1 collective-permute-start.14
  69.0 1.6 %collective-permute-start.16 = (bf16[2048,128]{1,0:T(8,128)(2,1)S(1)}, bf16[2048,128]{1,0:T(8,128)(2,1)S(1)}, u32[]{:S(2)}, u32[]{:S(2)}) collective-permute-start(bf16[2048,128]{1,0:T(8,128)(2,1)S(1)} %constant_dynamic-update-slice_fusion.4.refs_3_), channel_id=1, source_target_pairs={{0,16},{16,0},{1,17},{17,1},{2,18},{18,2},{3,19},{19,3},{4,20},{20... | collective-permute-start | bytes 1572872 | tf_op jit(solution)/shard_map/ppermute | solution.py:24
  70.6 0.5 collective-permute-start.23
  71.1 2.2 %input_grad_part.2 = f32[4096,128]{1,0:T(8,128)S(1)} custom-call(s32[8]{0:T(128)S(1)} %get-tuple-element.75.place, s32[256]{0:T(256)S(1)} %copy-done.3, bf16[8192,128]{1,0:T(8,128)(2,1)S(1)} %copy-done.1, bf16[2048,128]{1,0:T(8,128)(2,1)S(1)} %upper_last.1.both_ref.refs_11_), custom_call_target="tpu_custom_call" | custom-call | flops 536870912 | bytes 4194304 | tf_op jit(solution)/shard_map/input_grad_part/pallas_call | solution.py:226
  73.3 0.0 collective-permute-done.14
  73.3 0.3 convert_add_fusion
  73.6 0.1 slice.66
  73.7 0.0 copy-start.6
  73.7 0.6 collective-permute-start.15
  74.3 0.0 collective-permute-start.20
  74.3 1.5 %collective-permute-start.22 = (bf16[2048,128]{1,0:T(8,128)(2,1)S(1)}, bf16[2048,128]{1,0:T(8,128)(2,1)S(1)}, u32[]{:S(2)}, u32[]{:S(2)}) collective-permute-start(bf16[2048,128]{1,0:T(8,128)(2,1)S(1)} %upper_last.1.both_ref.refs_11_), channel_id=1, source_target_pairs={{0,16},{16,0},{1,17},{17,1},{2,18},{18,2},{3,19},{19,3},{4,20},{20... | collective-permute-start | bytes 1572872 | tf_op jit(solution)/shard_map/ppermute | solution.py:24
  75.8 8.0 %collective-permute-done.16.refs_7_ = bf16[2048,128]{1,0:T(8,128)(2,1)S(1)} collective-permute-done((bf16[2048,128]{1,0:T(8,128)(2,1)S(1)}, bf16[2048,128]{1,0:T(8,128)(2,1)S(1)}, u32[]{:S(2)}, u32[]{:S(2)}) %collective-permute-start.16) | collective-permute-done | bytes 524320 | tf_op jit(solution)/shard_map/ppermute | solution.py:24
  83.8 0.0 collective-permute-start.21
  83.8 11.2 %collective-permute-done.23.refs_8_ = bf16[2048,128]{1,0:T(8,128)(2,1)S(1)} collective-permute-done((bf16[2048,128]{1,0:T(8,128)(2,1)S(1)}, bf16[2048,128]{1,0:T(8,128)(2,1)S(1)}, u32[]{:S(2)}, u32[]{:S(2)}) %collective-permute-start.23) | collective-permute-done | bytes 524320 | tf_op jit(solution)/shard_map/ppermute | solution.py:24
  95.0 0.0 collective-permute-start.25
  95.0 0.0 collective-permute-done.15
  95.0 0.5 collective-permute-start.24
  95.5 0.1 fusion.10
  95.7 0.0 collective-permute-done.20.refs_9_
  95.7 2.5 %collective-permute-start.17 = (bf16[512,128]{1,0:T(8,128)(2,1)S(1)}, bf16[512,128]{1,0:T(8,128)(2,1)S(1)}, u32[]{:S(2)}, u32[]{:S(2)}) collective-permute-start(bf16[512,128]{1,0:T(8,128)(2,1)S(1)} %get-tuple-element.70), channel_id=1, source_target_pairs={{0,4},{1,5},{2,6},{3,7},{4,0},{5,1},{6,2},{7,3},{8,12},{9,13},{10,... | collective-permute-start | bytes 393224 | tf_op jit(solution)/shard_map/ppermute | solution.py:24
  98.2 1.0 collective-permute-start.18
  99.2 6.6 %collective-permute-done.22.refs_12_ = bf16[2048,128]{1,0:T(8,128)(2,1)S(1)} collective-permute-done((bf16[2048,128]{1,0:T(8,128)(2,1)S(1)}, bf16[2048,128]{1,0:T(8,128)(2,1)S(1)}, u32[]{:S(2)}, u32[]{:S(2)}) %collective-permute-start.22) | collective-permute-done | bytes 524320 | tf_op jit(solution)/shard_map/ppermute | solution.py:24
  105.8 2.3 %collective-permute-start.19 = (bf16[512,128]{1,0:T(8,128)(2,1)S(1)}, bf16[512,128]{1,0:T(8,128)(2,1)S(1)}, u32[]{:S(2)}, u32[]{:S(2)}) collective-permute-start(bf16[512,128]{1,0:T(8,128)(2,1)S(1)} %get-tuple-element.68), channel_id=1, source_target_pairs={{0,12},{1,13},{2,14},{3,15},{4,8},{5,9},{6,10},{7,11},{8,4},{9,5},... | collective-permute-start | bytes 393224 | tf_op jit(solution)/shard_map/ppermute | solution.py:24
  108.2 0.7 slice.50
  108.9 7.1 %grads_up.1 = bf16[160,4096]{1,0:T(8,128)(2,1)} custom-call(s32[264]{0:T(512)S(1)} %copy-done.6, s32[256]{0:T(256)S(1)} %copy-done.3, s32[128]{0:T(128)S(1)} %fusion.6.refs_2_, bf16[2048,128]{1,0:T(8,128)(2,1)S(1)} %constant_dynamic-update-slice_fusion.refs_3_, bf16[2048,128]{1,0:T(8,128)(2,1)S(1)} %collective-permute-done.8.refs_3_.refs_4_, ...), custom_call_target="tpu_custom_call" | custom-call | flops 1342177280 | bytes 6291456 | tf_op jit(solution)/shard_map/grads_up/pallas_call | solution.py:295
  116.1 0.7 fusion.2
  116.8 7.2 %grads_down.1 = bf16[160,4096]{1,0:T(8,128)(2,1)} custom-call(s32[264]{0:T(512)S(1)} %copy-done.5, s32[256]{0:T(256)S(1)} %copy-done.4, s32[128]{0:T(128)S(1)} %fusion.6.refs_2_, bf16[2048,128]{1,0:T(8,128)(2,1)S(1)} %constant_dynamic-update-slice_fusion.4.refs_3_, bf16[2048,128]{1,0:T(8,128)(2,1)S(1)} %collective-permute-done.7.refs_3_.refs_4_, ...), custom_call_target="tpu_custom_call" | custom-call | flops 1342177280 | bytes 6291456 | tf_op jit(solution)/shard_map/grads_down/pallas_call | solution.py:295
  (37 shorter events, 0.2 us)
Async XLA Ops:
  0.6 13.4 %collective-permute-start = (bf16[512,128]{1,0:T(8,128)(2,1)}, bf16[512,128]{1,0:T(8,128)(2,1)S(1)}, u32[]{:S(2)}, u32[]{:S(2)}) collective-permute-start(bf16[512,128]{1,0:T(8,128)(2,1)} %param.8), channel_id=1, source_target_pairs={{0,4},{1,5},{2,6},{3,7},{4,0},{5,1},{6,2},{7,3},{8,12},{9,13},{10,... | collective-permute-start | bytes 393224 | tf_op jit(solution)/shard_map/ppermute | solution.py:24
  3.7 13.2 %collective-permute-start.1 = (bf16[512,128]{1,0:T(8,128)(2,1)}, bf16[512,128]{1,0:T(8,128)(2,1)S(1)}, u32[]{:S(2)}, u32[]{:S(2)}) collective-permute-start(bf16[512,128]{1,0:T(8,128)(2,1)} %param.8), channel_id=1, source_target_pairs={{0,8},{1,9},{2,10},{3,11},{4,12},{5,13},{6,14},{7,15},{8,0},{9,1},... | collective-permute-start | bytes 393224 | tf_op jit(solution)/shard_map/ppermute | solution.py:24
  6.3 10.6 %collective-permute-start.2 = (bf16[512,128]{1,0:T(8,128)(2,1)}, bf16[512,128]{1,0:T(8,128)(2,1)S(1)}, u32[]{:S(2)}, u32[]{:S(2)}) collective-permute-start(bf16[512,128]{1,0:T(8,128)(2,1)} %param.8), channel_id=1, source_target_pairs={{0,12},{1,13},{2,14},{3,15},{4,8},{5,9},{6,10},{7,11},{8,4},{9,5},... | collective-permute-start | bytes 393224 | tf_op jit(solution)/shard_map/ppermute | solution.py:24
  6.3 10.6 %copy-start.7 = (bf16[512,128]{1,0:T(8,128)(2,1)S(1)}, bf16[512,128]{1,0:T(8,128)(2,1)}, u32[]{:S(2)}) copy-start(bf16[512,128]{1,0:T(8,128)(2,1)} %param.8) | copy-start | bytes 393220
  6.3 17.4 %copy-start.8 = (bf16[512,128]{1,0:T(8,128)(2,1)S(1)}, bf16[512,128]{1,0:T(8,128)(2,1)}, u32[]{:S(2)}) copy-start(bf16[512,128]{1,0:T(8,128)(2,1)} %param.9) | copy-start | bytes 393220
  6.3 22.0 %copy-start.3 = (s32[256]{0:T(256)S(1)}, s32[256]{0:T(256)}, u32[]{:S(2)}) copy-start(s32[256]{0:T(256)} %refs_1_.12) | copy-start | bytes 3076
  17.0 11.4 %collective-permute-start.6 = (bf16[2048,128]{1,0:T(8,128)(2,1)S(1)}, bf16[2048,128]{1,0:T(8,128)(2,1)S(1)}, u32[]{:S(2)}, u32[]{:S(2)}) collective-permute-start(bf16[2048,128]{1,0:T(8,128)(2,1)S(1)} %constant_dynamic-update-slice_fusion.refs_3_), channel_id=1, source_target_pairs={{0,1},{1,0},{2,3},{3,2},{4,5},{5,4},{6,7},{7,6},{8,9},{9,8},{10,11... | collective-permute-start | bytes 1572872 | tf_op jit(solution)/shard_map/ppermute | solution.py:24
  17.1 21.6 %collective-permute-start.8 = (bf16[2048,128]{1,0:T(8,128)(2,1)S(1)}, bf16[2048,128]{1,0:T(8,128)(2,1)S(1)}, u32[]{:S(2)}, u32[]{:S(2)}) collective-permute-start(bf16[2048,128]{1,0:T(8,128)(2,1)S(1)} %constant_dynamic-update-slice_fusion.refs_3_), channel_id=1, source_target_pairs={{0,2},{1,3},{2,0},{3,1},{4,6},{5,7},{6,4},{7,5},{8,10},{9,11},{10,... | collective-permute-start | bytes 1572872 | tf_op jit(solution)/shard_map/ppermute | solution.py:24
  23.8 9.1 %collective-permute-start.3 = (bf16[512,128]{1,0:T(8,128)(2,1)S(1)}, bf16[512,128]{1,0:T(8,128)(2,1)S(1)}, u32[]{:S(2)}, u32[]{:S(2)}) collective-permute-start(bf16[512,128]{1,0:T(8,128)(2,1)S(1)} %copy-done.8), channel_id=1, source_target_pairs={{0,4},{1,5},{2,6},{3,7},{4,0},{5,1},{6,2},{7,3},{8,12},{9,13},{10,... | collective-permute-start | bytes 393224 | tf_op jit(solution)/shard_map/ppermute | solution.py:24
  25.8 12.9 %collective-permute-start.4 = (bf16[512,128]{1,0:T(8,128)(2,1)S(1)}, bf16[512,128]{1,0:T(8,128)(2,1)S(1)}, u32[]{:S(2)}, u32[]{:S(2)}) collective-permute-start(bf16[512,128]{1,0:T(8,128)(2,1)S(1)} %copy-done.8), channel_id=1, source_target_pairs={{0,8},{1,9},{2,10},{3,11},{4,12},{5,13},{6,14},{7,15},{8,0},{9,1},... | collective-permute-start | bytes 393224 | tf_op jit(solution)/shard_map/ppermute | solution.py:24
  26.9 11.8 %collective-permute-start.5 = (bf16[512,128]{1,0:T(8,128)(2,1)S(1)}, bf16[512,128]{1,0:T(8,128)(2,1)S(1)}, u32[]{:S(2)}, u32[]{:S(2)}) collective-permute-start(bf16[512,128]{1,0:T(8,128)(2,1)S(1)} %copy-done.8), channel_id=1, source_target_pairs={{0,12},{1,13},{2,14},{3,15},{4,8},{5,9},{6,10},{7,11},{8,4},{9,5},... | collective-permute-start | bytes 393224 | tf_op jit(solution)/shard_map/ppermute | solution.py:24
  28.3 1.6 %copy-start = (bf16[8192,128]{1,0:T(8,128)(2,1)S(1)}, bf16[8192,128]{1,0:T(8,128)(2,1)}, u32[]{:S(2)}) copy-start(bf16[8192,128]{1,0:T(8,128)(2,1)} %get-tuple-element.43.refs_2_.w_ref) | copy-start | bytes 6291460
  38.8 3.3 %collective-permute-start.9 = (bf16[2048,128]{1,0:T(8,128)(2,1)S(1)}, bf16[2048,128]{1,0:T(8,128)(2,1)S(1)}, u32[]{:S(2)}, u32[]{:S(2)}) collective-permute-start(bf16[2048,128]{1,0:T(8,128)(2,1)S(1)} %collective-permute-done.8.refs_3_.refs_4_), channel_id=1, source_target_pairs={{0,1},{1,0},{2,3},{3,2},{4,5},{5,4},{6,7},{7,6},{8,9},{9,8},{10,11... | collective-permute-start | bytes 1572872 | tf_op jit(solution)/shard_map/ppermute | solution.py:24
  38.9 6.1 %collective-permute-start.10 = (bf16[2048,128]{1,0:T(8,128)(2,1)S(1)}, bf16[2048,128]{1,0:T(8,128)(2,1)S(1)}, u32[]{:S(2)}, u32[]{:S(2)}) collective-permute-start(bf16[2048,128]{1,0:T(8,128)(2,1)S(1)} %constant_dynamic-update-slice_fusion.4.refs_3_), channel_id=1, source_target_pairs={{0,1},{1,0},{2,3},{3,2},{4,5},{5,4},{6,7},{7,6},{8,9},{9,8},{10,11... | collective-permute-start | bytes 1572872 | tf_op jit(solution)/shard_map/ppermute | solution.py:24
  39.4 14.8 %collective-permute-start.11 = (bf16[2048,128]{1,0:T(8,128)(2,1)S(1)}, bf16[2048,128]{1,0:T(8,128)(2,1)S(1)}, u32[]{:S(2)}, u32[]{:S(2)}) collective-permute-start(bf16[2048,128]{1,0:T(8,128)(2,1)S(1)} %constant_dynamic-update-slice_fusion.refs_3_), channel_id=1, source_target_pairs={{0,16},{16,0},{1,17},{17,1},{2,18},{18,2},{3,19},{19,3},{4,20},{20... | collective-permute-start | bytes 1572872 | tf_op jit(solution)/shard_map/ppermute | solution.py:24
  40.9 13.6 %collective-permute-start.7 = (bf16[2048,128]{1,0:T(8,128)(2,1)S(1)}, bf16[2048,128]{1,0:T(8,128)(2,1)S(1)}, u32[]{:S(2)}, u32[]{:S(2)}) collective-permute-start(bf16[2048,128]{1,0:T(8,128)(2,1)S(1)} %constant_dynamic-update-slice_fusion.4.refs_3_), channel_id=1, source_target_pairs={{0,2},{1,3},{2,0},{3,1},{4,6},{5,7},{6,4},{7,5},{8,10},{9,11},{10,... | collective-permute-start | bytes 1572872 | tf_op jit(solution)/shard_map/ppermute | solution.py:24
  41.5 3.5 %copy-start.2 = (bf16[8192,128]{1,0:T(8,128)(2,1)S(1)}, bf16[8192,128]{1,0:T(8,128)(2,1)}, u32[]{:S(2)}) copy-start(bf16[8192,128]{1,0:T(8,128)(2,1)} %get-tuple-element.37.refs_2_) | copy-start | bytes 6291460
  41.5 3.5 %copy-start.4 = (s32[256]{0:T(256)S(1)}, s32[256]{0:T(256)}, u32[]{:S(2)}) copy-start(s32[256]{0:T(256)} %refs_1_.13) | copy-start | bytes 3076
  41.5 23.1 %collective-permute-start.13 = (bf16[2048,128]{1,0:T(8,128)(2,1)S(1)}, bf16[2048,128]{1,0:T(8,128)(2,1)S(1)}, u32[]{:S(2)}, u32[]{:S(2)}) collective-permute-start(bf16[2048,128]{1,0:T(8,128)(2,1)S(1)} %collective-permute-done.8.refs_3_.refs_4_), channel_id=1, source_target_pairs={{0,16},{16,0},{1,17},{17,1},{2,18},{18,2},{3,19},{19,3},{4,20},{20... | collective-permute-start | bytes 1572872 | tf_op jit(solution)/shard_map/ppermute | solution.py:24
  54.6 10.0 %collective-permute-start.12 = (bf16[2048,128]{1,0:T(8,128)(2,1)S(1)}, bf16[2048,128]{1,0:T(8,128)(2,1)S(1)}, u32[]{:S(2)}, u32[]{:S(2)}) collective-permute-start(bf16[2048,128]{1,0:T(8,128)(2,1)S(1)} %collective-permute-done.7.refs_3_.refs_4_), channel_id=1, source_target_pairs={{0,1},{1,0},{2,3},{3,2},{4,5},{5,4},{6,7},{7,6},{8,9},{9,8},{10,11... | collective-permute-start | bytes 1572872 | tf_op jit(solution)/shard_map/ppermute | solution.py:24
  56.1 10.5 %copy-start.1 = (bf16[8192,128]{1,0:T(8,128)(2,1)S(1)}, bf16[8192,128]{1,0:T(8,128)(2,1)}, u32[]{:S(2)}) copy-start(bf16[8192,128]{1,0:T(8,128)(2,1)} %get-tuple-element.43.refs_2_.w_ref) | copy-start | bytes 6291460
  68.9 4.4 %collective-permute-start.14 = (bf16[4096,128]{1,0:T(8,128)(2,1)S(1)}, bf16[4096,128]{1,0:T(8,128)(2,1)S(1)}, u32[]{:S(2)}, u32[]{:S(2)}) collective-permute-start(bf16[4096,128]{1,0:T(8,128)(2,1)S(1)} %input_grad_part.3), channel_id=1, source_target_pairs={{0,1},{1,0},{2,3},{3,2},{4,5},{5,4},{6,7},{7,6},{8,9},{9,8},{10,11... | collective-permute-start | bytes 3145736 | tf_op jit(solution)/shard_map/ppermute | solution.py:24
  69.0 14.8 %collective-permute-start.16 = (bf16[2048,128]{1,0:T(8,128)(2,1)S(1)}, bf16[2048,128]{1,0:T(8,128)(2,1)S(1)}, u32[]{:S(2)}, u32[]{:S(2)}) collective-permute-start(bf16[2048,128]{1,0:T(8,128)(2,1)S(1)} %constant_dynamic-update-slice_fusion.4.refs_3_), channel_id=1, source_target_pairs={{0,16},{16,0},{1,17},{17,1},{2,18},{18,2},{3,19},{19,3},{4,20},{20... | collective-permute-start | bytes 1572872 | tf_op jit(solution)/shard_map/ppermute | solution.py:24
  70.6 24.5 %collective-permute-start.23 = (bf16[2048,128]{1,0:T(8,128)(2,1)S(1)}, bf16[2048,128]{1,0:T(8,128)(2,1)S(1)}, u32[]{:S(2)}, u32[]{:S(2)}) collective-permute-start(bf16[2048,128]{1,0:T(8,128)(2,1)S(1)} %collective-permute-done.7.refs_3_.refs_4_), channel_id=1, source_target_pairs={{0,16},{16,0},{1,17},{17,1},{2,18},{18,2},{3,19},{19,3},{4,20},{20... | collective-permute-start | bytes 1572872 | tf_op jit(solution)/shard_map/ppermute | solution.py:24
  73.7 35.2 %copy-start.6 = (s32[264]{0:T(512)S(1)}, s32[264]{0:T(512)}, u32[]{:S(2)}) copy-start(s32[264]{0:T(512)} %get-tuple-element.57.refs_0_) | copy-start | bytes 3172
  73.7 21.3 %collective-permute-start.15 = (bf16[2048,128]{1,0:T(8,128)(2,1)S(1)}, bf16[2048,128]{1,0:T(8,128)(2,1)S(1)}, u32[]{:S(2)}, u32[]{:S(2)}) collective-permute-start(bf16[2048,128]{1,0:T(8,128)(2,1)S(1)} %slice.66), channel_id=1, source_target_pairs={{0,2},{1,3},{2,0},{3,1},{4,6},{5,7},{6,4},{7,5},{8,10},{9,11},{10,... | collective-permute-start | bytes 1572872 | tf_op jit(solution)/shard_map/ppermute | solution.py:24
  74.3 21.5 %collective-permute-start.20 = (bf16[2048,128]{1,0:T(8,128)(2,1)S(1)}, bf16[2048,128]{1,0:T(8,128)(2,1)S(1)}, u32[]{:S(2)}, u32[]{:S(2)}) collective-permute-start(bf16[2048,128]{1,0:T(8,128)(2,1)S(1)} %collective-permute-done.11.refs_7_), channel_id=1, source_target_pairs={{0,1},{1,0},{2,3},{3,2},{4,5},{5,4},{6,7},{7,6},{8,9},{9,8},{10,11... | collective-permute-start | bytes 1572872 | tf_op jit(solution)/shard_map/ppermute | solution.py:24
  74.3 31.5 %collective-permute-start.22 = (bf16[2048,128]{1,0:T(8,128)(2,1)S(1)}, bf16[2048,128]{1,0:T(8,128)(2,1)S(1)}, u32[]{:S(2)}, u32[]{:S(2)}) collective-permute-start(bf16[2048,128]{1,0:T(8,128)(2,1)S(1)} %upper_last.1.both_ref.refs_11_), channel_id=1, source_target_pairs={{0,16},{16,0},{1,17},{17,1},{2,18},{18,2},{3,19},{19,3},{4,20},{20... | collective-permute-start | bytes 1572872 | tf_op jit(solution)/shard_map/ppermute | solution.py:24
  83.8 14.4 %collective-permute-start.21 = (bf16[2048,128]{1,0:T(8,128)(2,1)S(1)}, bf16[2048,128]{1,0:T(8,128)(2,1)S(1)}, u32[]{:S(2)}, u32[]{:S(2)}) collective-permute-start(bf16[2048,128]{1,0:T(8,128)(2,1)S(1)} %collective-permute-done.13.refs_8_), channel_id=1, source_target_pairs={{0,1},{1,0},{2,3},{3,2},{4,5},{5,4},{6,7},{7,6},{8,9},{9,8},{10,11... | collective-permute-start | bytes 1572872 | tf_op jit(solution)/shard_map/ppermute | solution.py:24
  95.0 21.8 %collective-permute-start.25 = (bf16[2048,128]{1,0:T(8,128)(2,1)S(1)}, bf16[2048,128]{1,0:T(8,128)(2,1)S(1)}, u32[]{:S(2)}, u32[]{:S(2)}) collective-permute-start(bf16[2048,128]{1,0:T(8,128)(2,1)S(1)} %collective-permute-done.23.refs_8_), channel_id=1, source_target_pairs={{0,1},{1,0},{2,3},{3,2},{4,5},{5,4},{6,7},{7,6},{8,9},{9,8},{10,11... | collective-permute-start | bytes 1572872 | tf_op jit(solution)/shard_map/ppermute | solution.py:24
  95.0 21.8 %collective-permute-start.24 = (bf16[2048,128]{1,0:T(8,128)(2,1)S(1)}, bf16[2048,128]{1,0:T(8,128)(2,1)S(1)}, u32[]{:S(2)}, u32[]{:S(2)}) collective-permute-start(bf16[2048,128]{1,0:T(8,128)(2,1)S(1)} %collective-permute-done.16.refs_7_), channel_id=1, source_target_pairs={{0,1},{1,0},{2,3},{3,2},{4,5},{5,4},{6,7},{7,6},{8,9},{9,8},{10,11... | collective-permute-start | bytes 1572872 | tf_op jit(solution)/shard_map/ppermute | solution.py:24
  95.7 20.3 %collective-permute-start.17 = (bf16[512,128]{1,0:T(8,128)(2,1)S(1)}, bf16[512,128]{1,0:T(8,128)(2,1)S(1)}, u32[]{:S(2)}, u32[]{:S(2)}) collective-permute-start(bf16[512,128]{1,0:T(8,128)(2,1)S(1)} %get-tuple-element.70), channel_id=1, source_target_pairs={{0,4},{1,5},{2,6},{3,7},{4,0},{5,1},{6,2},{7,3},{8,12},{9,13},{10,... | collective-permute-start | bytes 393224 | tf_op jit(solution)/shard_map/ppermute | solution.py:24
  98.2 17.9 %collective-permute-start.18 = (bf16[512,128]{1,0:T(8,128)(2,1)S(1)}, bf16[512,128]{1,0:T(8,128)(2,1)S(1)}, u32[]{:S(2)}, u32[]{:S(2)}) collective-permute-start(bf16[512,128]{1,0:T(8,128)(2,1)S(1)} %get-tuple-element.69), channel_id=1, source_target_pairs={{0,8},{1,9},{2,10},{3,11},{4,12},{5,13},{6,14},{7,15},{8,0},{9,1},... | collective-permute-start | bytes 393224 | tf_op jit(solution)/shard_map/ppermute | solution.py:24
  105.8 10.3 %collective-permute-start.19 = (bf16[512,128]{1,0:T(8,128)(2,1)S(1)}, bf16[512,128]{1,0:T(8,128)(2,1)S(1)}, u32[]{:S(2)}, u32[]{:S(2)}) collective-permute-start(bf16[512,128]{1,0:T(8,128)(2,1)S(1)} %get-tuple-element.68), channel_id=1, source_target_pairs={{0,12},{1,13},{2,14},{3,15},{4,8},{5,9},{6,10},{7,11},{8,4},{9,5},... | collective-permute-start | bytes 393224 | tf_op jit(solution)/shard_map/ppermute | solution.py:24
  108.9 7.9 %copy-start.5 = (s32[264]{0:T(512)S(1)}, s32[264]{0:T(512)}, u32[]{:S(2)}) copy-start(s32[264]{0:T(512)} %get-tuple-element.64.refs_0_) | copy-start | bytes 3172
where the time goes:
time: 124 us
  waiting for transfers between devices  49.9 us (40%)
  Pallas kernels  43.7 us (35%)
  starting transfers between devices  25.5 us (21%)
  local copies, waits for them, and re-layouts  2.71 us (2%)
  other arithmetic  1.3 us (1%)
    ppermute x26, waiting for transfers between devices, swap(): return lax.ppermute(value, axis, [(i, i ^ mask) for i in range(size)])  49.9 us
    ppermute x26, starting transfers between devices, swap(): return lax.ppermute(value, axis, [(i, i ^ mask) for i in range(size)])  25.5 us
    pallas_call x2, Pallas kernels, owned_grads(): pl.pallas_call(functools.partial(grads_kernel, groups, pieces, capacity,...  14.4 us
    pallas_call x5, Pallas kernels, hidden_sum(): pl.pallas_call(functools.partial(hidden_kernel, rows, is_up, len(pieces),...  12.1 us
    pallas_call x1, Pallas kernels, relayout(): pl.pallas_call(functools.partial(relayout_kernel, blocks), grid=(total //...  7.73 us
    pallas_call x1, Pallas kernels, slots(): pl.pallas_call(slots_kernel, in_specs=[spec] * 3, out_specs=[spec] * 2, o...  5.03 us
    pallas_call x2, Pallas kernels, input_grad_part(): pl.pallas_call(functools.partial(input_grad_kernel, rows), in_specs=[smem...  4.49 us
  transfers between devices with their start and end apart: 26, of which 8 were waited for; matrix products, arithmetic and copies ran while one was open for 2% of the time, Pallas kernels for 26%

commit v1 on v0

v1 whole, which is shorter than its diff:
```python
import functools
import jax
import jax.numpy as jnp
from jax import lax
from jax.experimental import pallas as pl
from jax.experimental.pallas import tpu as pltpu
from jax.sharding import PartitionSpec as P

BS = 64
FBLK = 16
KB = 2
GROUP = 16
RELAYOUT = 64
PITCH = BS + 1
VMEM = pltpu.VMEM
SMEM = pltpu.SMEM
ANY = pl.ANY
BF = jnp.bfloat16
F32 = jnp.float32
COST = pl.CostEstimate(flops=1 << 29, bytes_accessed=6 << 20, transcendentals=0)
SMALL = pl.CostEstimate(flops=1000, bytes_accessed=1 << 20, transcendentals=0)


def swap(value, axis, mask):
    size = lax.axis_size(axis)
    return lax.ppermute(value, axis, [(i, i ^ mask) for i in range(size)])


def swap_groups(value, group_mask, mask):
    groups, size = lax.axis_size("dp"), lax.axis_size("mp")
    pairs = [
        (g * size + i, (g ^ group_mask) * size + (i ^ mask))
        for g in range(groups)
        for i in range(size)
    ]
    return lax.ppermute(value, ("dp", "mp"), pairs)


def relayout_kernel(blocks, src, out, tall):
    lane = lax.broadcasted_iota(jnp.int32, (BS, 2 * BS), 1) < BS
    even = lax.broadcasted_iota(jnp.int32, (blocks, 2 * BS), 0) % 2 == 0

    def body(i, carry):
        rows = pl.ds(pl.multiple_of(i * blocks, blocks), blocks)
        for a in range(BS // 2):
            tile = src[rows, a * 2 * BS : (a + 1) * 2 * BS].astype(F32)
            turned = pltpu.roll(tile, BS, 1)
            tall[pl.ds(2 * a, blocks, stride=PITCH), :] = jnp.where(even, tile, turned)
            tall[pl.ds(2 * a + 1, blocks, stride=PITCH), :] = jnp.where(even, turned, tile)
        for r in range(blocks // KB):
            first = tall[2 * r * PITCH : 2 * r * PITCH + BS, :]
            second = tall[(2 * r + 1) * PITCH : (2 * r + 1) * PITCH + BS, :]
            at = pl.multiple_of(i * (blocks // KB) * BS + r * BS, BS)
            out[pl.ds(at, BS), :] = jnp.where(lane, first, second).astype(BF)
        return carry

    lax.fori_loop(0, src.shape[0] // blocks, body, 0)


def relayout(w):
    vmem = pl.BlockSpec(memory_space=VMEM)
    return pl.pallas_call(
        functools.partial(relayout_kernel, RELAYOUT),
        in_specs=[vmem],
        out_specs=vmem,
        out_shape=jax.ShapeDtypeStruct((w.shape[0] * BS // KB, KB * BS), BF),
        scratch_shapes=[VMEM((RELAYOUT * PITCH, 2 * BS), F32)],
        compiler_params=pltpu.CompilerParams(vmem_limit_bytes=16 << 20),
        cost_estimate=COST,
        name="relayout",
    )(w)


def slots_kernel(me_ref, up_ref, down_ref, up_tab, down_tab, counts):
    group = me_ref[0]
    total = up_ref.shape[0]

    def body(i, carry):
        a, b = carry
        for u in range(8):
            e = i * 8 + u
            up_tab[a] = e
            down_tab[b] = e
            a = a + (up_ref[e] == group).astype(jnp.int32)
            b = b + (down_ref[e] == group).astype(jnp.int32)
        return a, b

    a, b = lax.fori_loop(0, total // 8, body, (jnp.int32(0), jnp.int32(0)))
    counts[0] = a
    counts[1] = b


def slots(group, owner_up, owner_down):
    total = owner_up.shape[0]
    shape = jax.ShapeDtypeStruct((total + 8,), jnp.int32)
    spec = pl.BlockSpec(memory_space=SMEM)
    return pl.pallas_call(
        slots_kernel,
        in_specs=[spec] * 3,
        out_specs=[spec] * 3,
        out_shape=[shape, shape, jax.ShapeDtypeStruct((2,), jnp.int32)],
        cost_estimate=COST,
        name="slots",
    )(group, owner_up, owner_down)


def gelu_slope(value):
    scale = 0.7978845608028654
    cubic = 0.044715
    inner = scale * (value + cubic * value * value * value)
    tanh_part = jnp.tanh(inner)
    gate = 0.5 * (1.0 + tanh_part)
    slope = gate + 0.5 * value * (1.0 - tanh_part * tanh_part) * scale * (
        1.0 + 3.0 * cubic * value * value
    )
    return value * gate, slope


def source(me, i, far):
    return me ^ ((i // far) * 2 + (i % far) * 4)


def add_blocks(me_ref, where_ref, w_ref, x_refs, starts, acc, rows, is_up):
    far = w_ref.shape[0] // rows // 4
    per = rows // BS
    zero = jnp.zeros((BS, acc.shape[1]), BF)
    width = acc.shape[1]
    for x_ref, (bit, skip) in zip(x_refs, starts):

        def body(i, carry, x_ref=x_ref, bit=bit, skip=skip):
            start = source(me_ref[0] ^ bit, skip + i, far) * per
            for rr in range(per):
                r = start + rr
                w = w_ref[pl.ds(pl.multiple_of(r * BS, BS), BS), :]
                x = x_ref[pl.ds(pl.multiple_of(i * rows + rr * BS, BS), BS), :]
                if is_up:
                    t = lax.dot_general(
                        w, x, (((0,), (0,)), ((), ())), preferred_element_type=F32
                    )
                    parts = [t[q * BS : (q + 1) * BS, :] for q in range(KB)]
                else:
                    right = jnp.concatenate(
                        [
                            jnp.concatenate([x, zero], axis=1),
                            jnp.concatenate([zero, x], axis=1),
                        ],
                        axis=0,
                    )
                    t = jnp.dot(w, right, preferred_element_type=F32)
                    parts = [t[:, q * width : (q + 1) * width] for q in range(KB)]
                for q in range(KB):
                    to = pl.ds(pl.multiple_of(where_ref[KB * r + q] * BS, BS), BS)
                    acc[to, :] += parts[q]
            return carry

        lax.fori_loop(0, x_ref.shape[0] // rows, body, 0)


def hidden_kernel(rows, is_up, starts, first, last, *refs):
    me_ref, where_ref, w_ref = refs[:3]
    x_refs = refs[3 : 3 + len(starts)]
    rest = list(refs[3 + len(starts) :])
    acc_in = None if first else rest.pop(0)
    hidden = rest.pop(0) if last else None
    if last:
        both, active, acc = rest
    else:
        (acc,) = rest
    acc[...] = jnp.zeros_like(acc) if first else acc_in[...]
    add_blocks(me_ref, where_ref, w_ref, x_refs, starts, acc, rows, is_up)
    if last:
        ff = acc.shape[0]

        def body(i, carry):
            at = pl.multiple_of(i * BS, BS)
            value, slope = gelu_slope(hidden[pl.ds(at, BS), :])
            both[pl.ds(at, BS), :] = value.astype(BF)
            active[pl.ds(at, BS), :] = value.astype(BF)
            both[pl.ds(ff + at, BS), :] = (acc[pl.ds(at, BS), :] * slope).astype(BF)
            return carry

        lax.fori_loop(0, ff // BS, body, 0)


def hidden_sum(rows, is_up, me, where, w, pieces, starts, acc=None, hidden=None):
    ff, tokens = FBLK * BS, pieces[0].shape[1]
    smem = pl.BlockSpec(memory_space=SMEM)
    vmem = pl.BlockSpec(memory_space=VMEM)
    more = [x for x in (acc, hidden) if x is not None]
    if hidden is None:
        outs, scratch = [jax.ShapeDtypeStruct((ff, tokens), F32)], []
    else:
        outs = [jax.ShapeDtypeStruct((n * ff, tokens), BF) for n in (2, 1)]
        scratch = [VMEM((ff, tokens), F32)]
    return pl.pallas_call(
        functools.partial(
            hidden_kernel, rows, is_up, tuple(starts), acc is None, hidden is not None
        ),
        in_specs=[smem, smem] + [vmem] * (1 + len(pieces) + len(more)),
        out_specs=[vmem] * len(outs),
        out_shape=outs,
        scratch_shapes=scratch,
        compiler_params=pltpu.CompilerParams(vmem_limit_bytes=12 << 20),
        cost_estimate=COST,
        name=("hidden" if is_up else "upper") + ("" if hidden is None else "_last"),
    )(me, where, w, *pieces, *more)


def input_grad_kernel(rows, bit, me_ref, col_ref, w_ref, both_ref, out):
    per = rows // BS
    chunks = out.shape[0] // rows
    base = both_ref.shape[0] // 2

    def body(i, carry):
        start = source(me_ref[0] ^ bit, i, chunks // 2) * per
        for rr in range(per):
            r = start + rr
            w = w_ref[pl.ds(pl.multiple_of(r * BS, BS), BS), :]
            parts = [
                both_ref[pl.ds(pl.multiple_of(base + col_ref[KB * r + q] * BS, BS), BS), :]
                for q in range(KB)
            ]
            t = jnp.dot(w, jnp.concatenate(parts, axis=0), preferred_element_type=F32)
            out[pl.ds(pl.multiple_of(i * rows + rr * BS, BS), BS), :] = t.astype(out.dtype)
        return carry

    lax.fori_loop(0, chunks, body, 0)


def input_grad_part(rows, bit, me, col, w, both, dtype):
    smem = pl.BlockSpec(memory_space=SMEM)
    vmem = pl.BlockSpec(memory_space=VMEM)
    return pl.pallas_call(
        functools.partial(input_grad_kernel, rows, bit),
        in_specs=[smem, smem, vmem, vmem],
        out_specs=vmem,
        out_shape=jax.ShapeDtypeStruct((w.shape[0] // 2, both.shape[1]), dtype),
        compiler_params=pltpu.CompilerParams(vmem_limit_bytes=10 << 20),
        cost_estimate=COST,
        name="input_grad_part",
    )(me, col, w, both)


def in_vmem(kernel, outs, *args):
    vmem = pl.BlockSpec(memory_space=VMEM)
    return pl.pallas_call(
        kernel,
        in_specs=[vmem] * len(args),
        out_specs=[vmem] * len(outs),
        out_shape=[jax.ShapeDtypeStruct(*x) for x in outs],
        compiler_params=pltpu.CompilerParams(vmem_limit_bytes=10 << 20),
        cost_estimate=SMALL,
        name=kernel.__name__,
    )(*args)


def join(parts):
    def join_parts(*refs):
        row = 0
        for ref in refs[:-1]:
            refs[-1][row : row + ref.shape[0], :] = ref[...]
            row += ref.shape[0]

    shape = (sum(x.shape[0] for x in parts), parts[0].shape[1])
    return in_vmem(join_parts, [(shape, parts[0].dtype)], *parts)[0]


def add_and_split(terms, arrived, keep):
    rows, tokens = terms.shape
    sends = (rows - keep) // min(keep, rows - keep)
    size = (rows - keep) // sends

    def add_stage(terms_ref, arrived_ref, keep_ref, *send_refs):
        keep_ref[...] = terms_ref[:keep, :] + arrived_ref[:keep, :].astype(F32)
        for n, ref in enumerate(send_refs):
            at = pl.ds(keep + n * size, size)
            ref[...] = (terms_ref[at, :] + arrived_ref[at, :].astype(F32)).astype(BF)

    outs = [((keep, tokens), F32)] + [((size, tokens), BF)] * sends
    return in_vmem(add_stage, outs, terms, arrived)


def add_all(terms, arrived):
    def add_last(*refs):
        total = refs[0][...]
        for ref in refs[1:-1]:
            total = total + ref[...].astype(F32)
        refs[-1][...] = total.astype(BF)

    return in_vmem(add_last, [(terms.shape, BF)], terms, *arrived)[0]


def grads_kernel(groups, pieces, capacity, batch, rows, is_up, *refs):
    tab, count, order, me_ref = refs[:4]
    flat = refs[4 : 4 + sum(pieces)]
    both_refs = refs[4 + len(flat) : 4 + len(flat) + groups]
    out, features, tiles, *sem = refs[4 + len(flat) + groups :]
    base = both_refs[0].shape[0] // 2 if is_up else 0
    copies = []
    n = 0
    for g in range(groups):
        row = 0
        for _ in range(pieces[g]):
            size = flat[n].shape[0]
            if sem:
                copies.append(
                    pltpu.make_async_copy(
                        flat[n], features.at[g, pl.ds(row, size), :], sem[0].at[n]
                    )
                )
            else:
                features[g, row : row + size, :] = flat[n][...]
            row += size
            n += 1
    for copy in copies:
        copy.start()
    for copy in copies:
        copy.wait()
    low = lax.broadcasted_iota(jnp.int32, (batch, 2 * BS), 1) < BS
    slot = lax.broadcasted_iota(jnp.int32, (batch, 2 * BS), 0)
    live_slots = count[0 if is_up else 1]

    half = features.shape[1] // rows // 2
    far = half // 2
    per = rows // BS

    def place(row, y_first):
        apart = (row // per) ^ me_ref[0]
        core, y, z = apart & 1, (apart >> 1) & 1, apart >> 2
        spot = core * half + (z * 2 + y if y_first else y * far + z)
        return pl.multiple_of(spot * rows + (row % per) * BS, BS)

    def body(b, carry):
        live = slot + b * batch < live_slots
        for u in range(batch):
            e = jnp.where(b * batch + u < live_slots, tab[b * batch + u], 0)
            at = [place(e // KB, g > 0 and not is_up) for g in range(groups)]
            to = pl.multiple_of(base + order[e] * BS, BS)
            f = jnp.concatenate(
                [features[g, pl.ds(at[g], BS), :] for g in range(groups)], axis=1
            )
            h = jnp.concatenate([ref[pl.ds(to, BS), :] for ref in both_refs], axis=1)
            left, right = (f, h) if is_up else (h, f)
            t = lax.dot_general(
                left, right, (((1,), (1,)), ((), ())), preferred_element_type=F32
            )
            tiles[u * PITCH : u * PITCH + BS, :BS] = t
        for a in range(BS // 2):
            even = tiles[pl.ds(2 * a, batch, stride=PITCH), :]
            odd = pltpu.roll(tiles[pl.ds(2 * a + 1, batch, stride=PITCH), :], BS, 1)
            out[
                pl.ds(pl.multiple_of(b * batch, batch), batch), a * 2 * BS : (a + 1) * 2 * BS
            ] = jnp.where(live, jnp.where(low, even, odd), 0.0).astype(BF)
        return carry

    lax.fori_loop(0, capacity // batch, body, 0)


def owned_grads(tab, count, order, me, features, boths, capacity, rows, is_up):
    groups = len(boths)
    pieces = tuple(len(group) for group in features)
    batch = GROUP if capacity % GROUP == 0 else 8
    flat = [piece for group in features for piece in group]
    tokens = boths[0].shape[1]
    total = sum(piece.shape[0] for piece in features[0])
    small = groups * total * tokens <= 4 << 20
    smem = pl.BlockSpec(memory_space=SMEM)
    vmem = pl.BlockSpec(memory_space=VMEM)
    piece = vmem if small else pl.BlockSpec(memory_space=ANY)
    scratch = [VMEM((groups, total, tokens), BF), VMEM((batch * PITCH, 2 * BS), F32)]
    if not small:
        scratch.append(pltpu.SemaphoreType.DMA((len(flat),)))
    return pl.pallas_call(
        functools.partial(grads_kernel, groups, pieces, capacity, batch, rows, is_up),
        in_specs=[smem] * 4 + [piece] * len(flat) + [vmem] * groups,
        out_specs=vmem,
        out_shape=jax.ShapeDtypeStruct((capacity, BS * BS), BF),
        scratch_shapes=scratch,
        compiler_params=pltpu.CompilerParams(vmem_limit_bytes=(20 if small else 48) << 20),
        cost_estimate=COST,
        name="grads_up" if is_up else "grads_down",
    )(tab, count, order, me, *flat, *boths)


def per_device(inputs, cotangent, w_up, w_down, col_up, row_down, owner_up, owner_down):
    rows, tokens = inputs.shape
    blocks = w_up.shape[0]
    groups = lax.axis_size("dp")
    members = lax.axis_size("mp")
    capacity = 5 * blocks // (4 * groups)
    me = lax.axis_index("mp").reshape(1)
    far = members // 4
    half = members // 2
    after = lax.optimization_barrier
    others = range(1, groups)

    cot_x = [swap(cotangent, "dp", d) for d in others]
    cot_xy = [swap_groups(cotangent, d, 2) for d in others]
    in_parts = [inputs] + [swap(inputs, "mp", 4 * z) for z in range(1, far)]
    up_w = relayout(w_up)
    down_w = relayout(w_down)
    in_parts, up_w, down_w, cot_x, cot_xy, cotangent = after(
        (in_parts, up_w, down_w, cot_x, cot_xy, cotangent)
    )
    in_near = join(in_parts)
    in_far = swap(in_near, "mp", 2)
    in_near_o = [swap(in_near, "dp", d) for d in others]
    in_near_b = swap(in_near, "mp", 1)
    cot_parts = [cotangent] + [swap(cotangent, "mp", 4 * z) for z in range(1, far)]
    cot_o = [join([x, xy]) for x, xy in zip(cot_x, cot_xy)]
    (hidden,) = hidden_sum(
        rows, True, me, col_up, up_w, [in_near, in_near_b], [(0, 0), (1, 0)]
    )
    cot_parts, hidden, cot_o, in_far, in_near_o = after(
        (cot_parts, hidden, cot_o, in_far, in_near_o)
    )
    cot_near = join(cot_parts)
    cot_far = swap(cot_near, "mp", 2)
    cot_near_b = swap(cot_near, "mp", 1)
    in_far_b = swap(in_far, "mp", 1)
    in_far_o = [swap(in_far, "dp", d) for d in others]
    cot_o_z = [[swap(x, "mp", 4 * z) for z in range(1, far)] for x in cot_o]
    (upper,) = hidden_sum(
        rows, False, me, row_down, down_w, [cot_near, cot_near_b], [(0, 0), (1, 0)]
    )
    (hidden,) = hidden_sum(
        rows, True, me, col_up, up_w, [in_far, in_far_b], [(0, far), (1, far)], hidden
    )
    early = [x[: far // 2] for x in cot_o_z]
    cot_far, hidden, upper, in_far_o, early = after((cot_far, hidden, upper, in_far_o, early))
    cot_far_b = swap(cot_far, "mp", 1)
    (upper,) = hidden_sum(rows, False, me, row_down, down_w, [cot_far], [(0, far)], upper)
    both, active = hidden_sum(
        rows, False, me, row_down, down_w, [cot_far_b], [(1, far)], upper, hidden
    )
    both_o = [swap(both, "dp", d) for d in others]

    sent = input_grad_part(rows, 1, me, col_up, up_w, both, BF)
    arrived = swap(sent, "mp", 1)
    sent, both = after((sent, both))
    terms = input_grad_part(rows, 0, me, col_up, up_w, both, F32)
    terms, sent = add_and_split(terms, arrived, far * rows)
    arrived = swap(sent, "mp", 2)
    terms, owner_up, owner_down = after((terms, owner_up, owner_down))
    up_tab, down_tab, counts = slots(
        lax.axis_index("dp").reshape(1), owner_up[:, 0], owner_down[:, 0]
    )
    in_near_o_b = [swap(x, "mp", 1) for x in in_near_o]
    in_far_o_b = [swap(x, "mp", 1) for x in in_far_o]
    in_all = [[in_near, in_far, in_near_b, in_far_b]]
    in_all += [list(x) for x in zip(in_near_o, in_far_o, in_near_o_b, in_far_o_b)]
    both_all = [both] + both_o
    grad_up = owned_grads(up_tab, counts, col_up, me, in_all, both_all, capacity, rows, True)
    late = [x[far // 2 :] for x in cot_o_z]
    arrived, late, grad_up = after((arrived, late, grad_up))
    cot_o = [[x] + near + rest for x, near, rest in zip(cot_o, early, late)]
    terms, *sent = add_and_split(terms, arrived, rows)
    pieces = [swap(x, "mp", 4 * z + 4) for z, x in enumerate(sent)]
    cot_o_b = [[swap(piece, "mp", 1) for piece in x] for x in cot_o]
    cot_all = [[cot_near, cot_far, cot_near_b, cot_far_b]]
    cot_all += [x + x_b for x, x_b in zip(cot_o, cot_o_b)]
    grad_down = owned_grads(
        down_tab, counts, row_down, me, cot_all, both_all, capacity, rows, False
    )
    pieces, grad_down = after((pieces, grad_down))
    return active, add_all(terms, pieces), grad_up, grad_down


def solution(mesh):
    placed = (
        P("mp", "dp"),
        P("mp", "dp"),
        P("mp", None),
        P("mp", None),
        P("mp"),
        P("mp"),
        P("mp", None),
        P("mp", None),
    )
    return jax.shard_map(
        per_device,
        mesh=mesh,
        in_specs=placed,
        out_specs=(P("mp", "dp"), P("mp", "dp"), P(("dp", "mp"), None), P(("dp", "mp"), None)),
        check_vma=False,
    )
```

time: 124 us -> 103 us (0.83)
  waiting for transfers between devices: 49.9 us -> 18.8 us
  starting transfers between devices: 25.5 us -> 33 us
  local copies, waits for them, and re-layouts: 2.71 us -> 5.97 us
  other arithmetic: 1.3 us -> 0 us
    ppermute x26 -> x30, waiting for transfers between devices: 49.9 us -> 18.8 us  [swap(): return lax.ppermute(value, axis, [(i, i ^ mask) for i in range(size)])]
    ppermute x26 -> x30, starting transfers between devices: 25.5 us -> 31.5 us  [swap(): return lax.ppermute(value, axis, [(i, i ^ mask) for i in range(size)])]
    unnamed x24 -> x60, local copies, waits for them, and re-layouts: 1.72 us -> 5.97 us
    pallas_call x2, Pallas kernels: 14.4 us -> 16.7 us  [owned_grads(): pl.pallas_call(functools.partial(grads_kernel, groups, pieces, capacity,...]
    pallas_call x9 -> x16, Pallas kernels: 29.3 us -> 27.2 us  [the longest x5 13.3 us: hidden_sum(): pl.pallas_call(functools.partial(hidden_kernel, rows, is_up, tuple(starts...]
    ppermute x0 -> x1, starting transfers between devices: none -> 1.49 us  [swap_groups(): return lax.ppermute(value, ('dp', 'mp'), pairs)]
  transfers between devices with their start and end apart: 26 -> 31, of which waited for: 8 -> 7; matrix products, arithmetic and copies ran while one was open for 2% -> 0% of each run, Pallas kernels for 26% -> 37%
where the time goes in v1:
time: 103 us
  Pallas kernels  43.9 us (43%)
  starting transfers between devices  33 us (32%)
  waiting for transfers between devices  18.8 us (18%)
  local copies, waits for them, and re-layouts  5.97 us (6%)
  between operations  1.05 us (1%)
    ppermute x30, starting transfers between devices, swap(): return lax.ppermute(value, axis, [(i, i ^ mask) for i in range(size)])  31.5 us
    ppermute x30, waiting for transfers between devices, swap(): return lax.ppermute(value, axis, [(i, i ^ mask) for i in range(size)])  18.8 us
    pallas_call x2, Pallas kernels, owned_grads(): pl.pallas_call(functools.partial(grads_kernel, groups, pieces, capacity,...  16.7 us
    pallas_call x5, Pallas kernels, hidden_sum(): pl.pallas_call(functools.partial(hidden_kernel, rows, is_up, tuple(starts...  13.3 us
    unnamed x60, local copies, waits for them, and re-layouts  5.97 us
    pallas_call x2, Pallas kernels, input_grad_part(): pl.pallas_call(functools.partial(input_grad_kernel, rows, bit), in_specs=...  4.44 us
    pallas_call x6, Pallas kernels, in_vmem(): pl.pallas_call(kernel, in_specs=[vmem] * len(args), out_specs=[vmem] * le...  4 us
    pallas_call x2, Pallas kernels, relayout(): pl.pallas_call(functools.partial(relayout_kernel, RELAYOUT), in_specs=[vm...  2.93 us
  transfers between devices with their start and end apart: 31, of which 7 were waited for; matrix products, arithmetic and copies ran while one was open for 0% of the time, Pallas kernels for 37%

profile of v1, /device:TPU:0, one launch (start us, length us, event | category | flops | bytes accessed | tf_op | source)
XLA Modules:
  0.0 102.7 jit_solution(10648123388557124280)
XLA Ops:
  0.6 3.1 %collective-permute-start = (bf16[512,128]{1,0:T(8,128)(2,1)}, bf16[512,128]{1,0:T(8,128)(2,1)S(1)}, u32[]{:S(2)}, u32[]{:S(2)}) collective-permute-start(bf16[512,128]{1,0:T(8,128)(2,1)} %refs_0_), channel_id=1, source_target_pairs={{0,4},{1,5},{2,6},{3,7},{4,0},{5,1},{6,2},{7,3},{8,12},{9,13},{10,... | collective-permute-start | bytes 393224 | tf_op jit(solution)/shard_map/ppermute | solution.py:26
  3.7 2.6 %collective-permute-start.1 = (bf16[512,128]{1,0:T(8,128)(2,1)}, bf16[512,128]{1,0:T(8,128)(2,1)S(1)}, u32[]{:S(2)}, u32[]{:S(2)}) collective-permute-start(bf16[512,128]{1,0:T(8,128)(2,1)} %refs_0_), channel_id=1, source_target_pairs={{0,8},{1,9},{2,10},{3,11},{4,12},{5,13},{6,14},{7,15},{8,0},{9,1},... | collective-permute-start | bytes 393224 | tf_op jit(solution)/shard_map/ppermute | solution.py:26
  6.3 0.0 collective-permute-start.2
  6.3 1.7 %collective-permute-start.3 = (bf16[512,128]{1,0:T(8,128)(2,1)}, bf16[512,128]{1,0:T(8,128)(2,1)S(1)}, u32[]{:S(2)}, u32[]{:S(2)}) collective-permute-start(bf16[512,128]{1,0:T(8,128)(2,1)} %refs_0_.1), channel_id=1, source_target_pairs={{0,16},{16,0},{1,17},{17,1},{2,18},{18,2},{3,19},{19,3},{4,20},{20... | collective-permute-start | bytes 393224 | tf_op jit(solution)/shard_map/ppermute | solution.py:26
  8.0 1.5 %collective-permute-start.4 = (bf16[512,128]{1,0:T(8,128)(2,1)}, bf16[512,128]{1,0:T(8,128)(2,1)S(1)}, u32[]{:S(2)}, u32[]{:S(2)}) collective-permute-start(bf16[512,128]{1,0:T(8,128)(2,1)} %refs_0_.1), channel_id=1, source_target_pairs={{0,18},{1,19},{2,16},{3,17},{4,22},{5,23},{6,20},{7,21},{8,26},{9,... | collective-permute-start | bytes 393224 | tf_op jit(solution)/shard_map/ppermute | solution.py:36
  9.5 1.6 %copy-done.4 = bf16[256,4096]{1,0:T(8,128)(2,1)S(1)} copy-done((bf16[256,4096]{1,0:T(8,128)(2,1)S(1)}, bf16[256,4096]{1,0:T(8,128)(2,1)}, u32[]{:S(2)}) %copy-start.4) | copy-done | bytes 2097176
  11.1 1.5 %relayout.2.refs_2_.w_ref = bf16[8192,128]{1,0:T(8,128)(2,1)S(1)} custom-call(bf16[256,4096]{1,0:T(8,128)(2,1)S(1)} %copy-done.4), custom_call_target="tpu_custom_call" | custom-call | flops 536870912 | bytes 6291456 | tf_op jit(solution)/shard_map/relayout/pallas_call | solution.py:62
  12.6 0.1 copy-done.5
  12.7 1.5 %relayout.3.refs_2_ = bf16[8192,128]{1,0:T(8,128)(2,1)S(1)} custom-call(bf16[256,4096]{1,0:T(8,128)(2,1)S(1)} %copy-done.5), custom_call_target="tpu_custom_call" | custom-call | flops 536870912 | bytes 6291456 | tf_op jit(solution)/shard_map/relayout/pallas_call | solution.py:62
  14.2 1.3 %copy-done = bf16[8192,128]{1,0:T(8,128)(2,1)} copy-done((bf16[8192,128]{1,0:T(8,128)(2,1)}, bf16[8192,128]{1,0:T(8,128)(2,1)S(1)}, u32[]{:S(2)}) %copy-start) | copy-done | bytes 2097176
  15.5 1.3 %collective-permute-done.1.refs_2_ = bf16[512,128]{1,0:T(8,128)(2,1)S(1)} collective-permute-done((bf16[512,128]{1,0:T(8,128)(2,1)}, bf16[512,128]{1,0:T(8,128)(2,1)S(1)}, u32[]{:S(2)}, u32[]{:S(2)}) %collective-permute-start.1) | collective-permute-done | bytes 131104 | tf_op jit(solution)/shard_map/ppermute | solution.py:26
  16.9 0.0 collective-permute-done.2.refs_3_
  16.9 0.0 copy-start.22
  16.9 0.6 copy-done.22
  17.6 0.1 collective-permute-start.8
  17.7 1.6 %collective-permute-start.10 = (bf16[2048,128]{1,0:T(8,128)(2,1)S(1)}, bf16[2048,128]{1,0:T(8,128)(2,1)}, u32[]{:S(2)}, u32[]{:S(2)}) collective-permute-start(bf16[2048,128]{1,0:T(8,128)(2,1)S(1)} %join_parts.3.refs_3_.refs_4_), channel_id=1, source_target_pairs={{0,16},{16,0},{1,17},{17,1},{2,18},{18,2},{3,19},{19,3},{4,20},{20... | collective-permute-start | bytes 1572872 | tf_op jit(solution)/shard_map/ppermute | solution.py:26
  19.2 1.5 %collective-permute-start.9 = (bf16[2048,128]{1,0:T(8,128)(2,1)S(1)}, bf16[2048,128]{1,0:T(8,128)(2,1)}, u32[]{:S(2)}, u32[]{:S(2)}) collective-permute-start(bf16[2048,128]{1,0:T(8,128)(2,1)S(1)} %join_parts.3.refs_3_.refs_4_), channel_id=1, source_target_pairs={{0,2},{1,3},{2,0},{3,1},{4,6},{5,7},{6,4},{7,5},{8,10},{9,11},{10,... | collective-permute-start | bytes 1572872 | tf_op jit(solution)/shard_map/ppermute | solution.py:26
  20.7 2.0 %collective-permute-start.5 = (bf16[512,128]{1,0:T(8,128)(2,1)}, bf16[512,128]{1,0:T(8,128)(2,1)}, u32[]{:S(2)}, u32[]{:S(2)}) collective-permute-start(bf16[512,128]{1,0:T(8,128)(2,1)} %refs_0_.1), channel_id=1, source_target_pairs={{0,4},{1,5},{2,6},{3,7},{4,0},{5,1},{6,2},{7,3},{8,12},{9,13},{10,... | collective-permute-start | bytes 393224 | tf_op jit(solution)/shard_map/ppermute | solution.py:26
  22.7 1.0 collective-permute-start.6
  23.7 1.5 %collective-permute-start.7 = (bf16[512,128]{1,0:T(8,128)(2,1)}, bf16[512,128]{1,0:T(8,128)(2,1)}, u32[]{:S(2)}, u32[]{:S(2)}) collective-permute-start(bf16[512,128]{1,0:T(8,128)(2,1)} %refs_0_.1), channel_id=1, source_target_pairs={{0,12},{1,13},{2,14},{3,15},{4,8},{5,9},{6,10},{7,11},{8,4},{9,5},... | collective-permute-start | bytes 393224 | tf_op jit(solution)/shard_map/ppermute | solution.py:26
  25.2 0.9 copy-done.23
  26.2 3.0 %hidden.2.refs_5_ = f32[1024,128]{1,0:T(8,128)S(1)} custom-call(s32[1]{0:T(128)} %bitcast.refs_0_.me_ref.refs_3_, s32[256]{0:T(256)S(1)} %copy-done.25, bf16[8192,128]{1,0:T(8,128)(2,1)S(1)} %relayout.2.refs_2_.w_ref, bf16[2048,128]{1,0:T(8,128)(2,1)S(1)} %join_parts.3.refs_3_.refs_4_, bf16[2048,128]{1,0:T(8,128)(2,1)S(1)} %collective-permute-done.8.refs_4_.refs_6_), custom_call_target="tpu_custom_call" | custom-call | flops 536870912 | bytes 6291456 | tf_op jit(solution)/shard_map/hidden/pallas_call | solution.py:195
  29.2 6.8 %collective-permute-done.6.refs_2_ = bf16[512,128]{1,0:T(8,128)(2,1)} collective-permute-done((bf16[512,128]{1,0:T(8,128)(2,1)}, bf16[512,128]{1,0:T(8,128)(2,1)}, u32[]{:S(2)}, u32[]{:S(2)}) %collective-permute-start.6) | collective-permute-done | bytes 131104 | tf_op jit(solution)/shard_map/ppermute | solution.py:26
  36.0 0.1 collective-permute-start.12
  36.0 1.1 %join_parts.5.refs_3_.refs_4_ = bf16[2048,128]{1,0:T(8,128)(2,1)S(1)} custom-call(bf16[512,128]{1,0:T(8,128)(2,1)} %refs_0_.1, bf16[512,128]{1,0:T(8,128)(2,1)} %collective-permute-done.5.refs_1_, bf16[512,128]{1,0:T(8,128)(2,1)} %collective-permute-done.6.refs_2_, bf16[512,128]{1,0:T(8,128)(2,1)} %collective-permute-done.7.refs_3_), custom_call_target="tpu_custom_call" | custom-call | flops 1000 | bytes 1048576 | tf_op jit(solution)/shard_map/join_parts/pallas_call | solution.py:246
  37.2 0.0 copy-start.26
  37.2 0.6 collective-permute-start.13
  37.8 0.5 collective-permute-start.11
  38.3 0.5 collective-permute-start.14
  38.8 1.9 %collective-permute-start.15 = (bf16[1024,128]{1,0:T(8,128)(2,1)S(1)}, bf16[1024,128]{1,0:T(8,128)(2,1)S(1)}, u32[]{:S(2)}, u32[]{:S(2)}) collective-permute-start(bf16[1024,128]{1,0:T(8,128)(2,1)S(1)} %join_parts.4.refs_8_), channel_id=1, source_target_pairs={{0,4},{1,5},{2,6},{3,7},{4,0},{5,1},{6,2},{7,3},{8,12},{9,13},{10,... | collective-permute-start | bytes 786440 | tf_op jit(solution)/shard_map/ppermute | solution.py:26
  40.8 1.0 collective-permute-start.16
  41.8 3.4 %hidden.3.refs_5_ = f32[1024,128]{1,0:T(8,128)S(1)} custom-call(s32[1]{0:T(128)} %bitcast.refs_0_.me_ref.refs_3_, s32[256]{0:T(256)S(1)} %copy-done.25, bf16[8192,128]{1,0:T(8,128)(2,1)S(1)} %relayout.2.refs_2_.w_ref, bf16[2048,128]{1,0:T(8,128)(2,1)} %collective-permute-done.9.refs_3_.refs_5_, ...), custom_call_target="tpu_custom_call" | custom-call | flops 536870912 | bytes 6291456 | tf_op jit(solution)/shard_map/hidden/pallas_call | solution.py:195
  45.3 2.6 %upper.2.refs_4_ = f32[1024,128]{1,0:T(8,128)S(1)} custom-call(s32[1]{0:T(128)} %bitcast.refs_0_.me_ref.refs_3_, s32[256]{0:T(256)S(1)} %copy-done.26, bf16[8192,128]{1,0:T(8,128)(2,1)S(1)} %copy-done.1, bf16[2048,128]{1,0:T(8,128)(2,1)S(1)} %join_parts.5.refs_3_.refs_4_, bf16[2048,128]{1,0:T(8,128)(2,1)S(1)} %collective-permute-done.13.refs_4_.refs_6_), custom_call_target="tpu_custom_call" | custom-call | flops 536870912 | bytes 6291456 | tf_op jit(solution)/shard_map/upper/pallas_call | solution.py:195
  47.9 4.3 %collective-permute-done.15.refs_9_ = bf16[1024,128]{1,0:T(8,128)(2,1)S(1)} collective-permute-done((bf16[1024,128]{1,0:T(8,128)(2,1)S(1)}, bf16[1024,128]{1,0:T(8,128)(2,1)S(1)}, u32[]{:S(2)}, u32[]{:S(2)}) %collective-permute-start.15) | collective-permute-done | bytes 262176 | tf_op jit(solution)/shard_map/ppermute | solution.py:26
  52.2 2.6 %collective-permute-done.16.refs_10_ = bf16[1024,128]{1,0:T(8,128)(2,1)S(1)} collective-permute-done((bf16[1024,128]{1,0:T(8,128)(2,1)S(1)}, bf16[1024,128]{1,0:T(8,128)(2,1)S(1)}, u32[]{:S(2)}, u32[]{:S(2)}) %collective-permute-start.16) | collective-permute-done | bytes 262176 | tf_op jit(solution)/shard_map/ppermute | solution.py:26
  54.8 0.1 collective-permute-start.17
  54.9 1.6 %upper.3.refs_4_ = f32[1024,128]{1,0:T(8,128)S(1)} custom-call(s32[1]{0:T(128)} %bitcast.refs_0_.me_ref.refs_3_, s32[256]{0:T(256)S(1)} %copy-done.26, bf16[8192,128]{1,0:T(8,128)(2,1)S(1)} %copy-done.1, bf16[2048,128]{1,0:T(8,128)(2,1)S(1)} %collective-permute-done.11.refs_3_.refs_5_, f32[1024,128]{1,0:T(8,128)S(1)} %upper.2.refs_4_), custom_call_target="tpu_custom_call" | custom-call | flops 536870912 | bytes 6291456 | tf_op jit(solution)/shard_map/upper/pallas_call | solution.py:195
  56.5 0.3 collective-permute-done.17.refs_3_.refs_7_
  56.8 2.8 %upper_last.1 = (bf16[2048,128]{1,0:T(8,128)(2,1)S(1)}, bf16[1024,128]{1,0:T(8,128)(2,1)}) custom-call(s32[1]{0:T(128)} %bitcast.refs_0_.me_ref.refs_3_, s32[256]{0:T(256)S(1)} %copy-done.26, bf16[8192,128]{1,0:T(8,128)(2,1)S(1)} %copy-done.1, bf16[2048,128]{1,0:T(8,128)(2,1)S(1)} %collective-permute-done.17.refs_3_.refs_7_, f32[1024,128]{1,0:T(8,128)S(1)} %upper.3.refs_4_, ...), custom_call_target="tpu_custom_call" | custom-call | flops 536870912 | bytes 6291456 | tf_op jit(solution)/shard_map/upper_last/pallas_call | solution.py:195
  59.5 2.2 %input_grad_part.2 = bf16[4096,128]{1,0:T(8,128)(2,1)S(1)} custom-call(s32[1]{0:T(128)} %bitcast.refs_0_.me_ref.refs_3_, s32[256]{0:T(256)S(1)} %copy-done.25, bf16[8192,128]{1,0:T(8,128)(2,1)S(1)} %relayout.2.refs_2_.w_ref, bf16[2048,128]{1,0:T(8,128)(2,1)S(1)} %get-tuple-element.70.both_ref.refs_12_.refs_16_), custom_call_target="tpu_custom_call" | custom-call | flops 536870912 | bytes 6291456 | tf_op jit(solution)/shard_map/input_grad_part/pallas_call | solution.py:233
  61.8 0.3 collective-permute-start.18
  62.1 0.3 collective-permute-start.21
  62.4 0.2 collective-permute-start.22
  62.6 1.5 %collective-permute-start.23 = (bf16[2048,128]{1,0:T(8,128)(2,1)S(1)}, bf16[2048,128]{1,0:T(8,128)(2,1)}, u32[]{:S(2)}, u32[]{:S(2)}) collective-permute-start(bf16[2048,128]{1,0:T(8,128)(2,1)S(1)} %get-tuple-element.70.both_ref.refs_12_.refs_16_), channel_id=1, source_target_pairs={{0,16},{16,0},{1,17},{17,1},{2,18},{18,2},{3,19},{19,3},{4,20},{20... | collective-permute-start | bytes 1572872 | tf_op jit(solution)/shard_map/ppermute | solution.py:26
  64.1 2.2 %input_grad_part.3.terms_ref = f32[4096,128]{1,0:T(8,128)S(1)} custom-call(s32[1]{0:T(128)} %bitcast.refs_0_.me_ref.refs_3_, s32[256]{0:T(256)S(1)} %copy-done.25, bf16[8192,128]{1,0:T(8,128)(2,1)S(1)} %relayout.2.refs_2_.w_ref, bf16[2048,128]{1,0:T(8,128)(2,1)S(1)} %get-tuple-element.70.both_ref.refs_12_.refs_16_), custom_call_target="tpu_custom_call" | custom-call | flops 536870912 | bytes 6291456 | tf_op jit(solution)/shard_map/input_grad_part/pallas_call | solution.py:233
  66.3 0.0 copy-start.9
  66.3 1.0 add_stage.2
  67.3 1.5 %collective-permute-start.19 = (bf16[2048,128]{1,0:T(8,128)(2,1)}, bf16[2048,128]{1,0:T(8,128)(2,1)}, u32[]{:S(2)}, u32[]{:S(2)}) collective-permute-start(bf16[2048,128]{1,0:T(8,128)(2,1)} %get-tuple-element.73), channel_id=1, source_target_pairs={{0,2},{1,3},{2,0},{3,1},{4,6},{5,7},{6,4},{7,5},{8,10},{9,11},{10,... | collective-permute-start | bytes 1572872 | tf_op jit(solution)/shard_map/ppermute | solution.py:26
  68.8 2.4 %collective-permute-start.20 = (bf16[1024,128]{1,0:T(8,128)(2,1)S(1)}, bf16[1024,128]{1,0:T(8,128)(2,1)}, u32[]{:S(2)}, u32[]{:S(2)}) collective-permute-start(bf16[1024,128]{1,0:T(8,128)(2,1)S(1)} %join_parts.4.refs_8_), channel_id=1, source_target_pairs={{0,12},{1,13},{2,14},{3,15},{4,8},{5,9},{6,10},{7,11},{8,4},{9,5},... | collective-permute-start | bytes 786440 | tf_op jit(solution)/shard_map/ppermute | solution.py:26
  71.2 0.5 collective-permute-start.28
  71.7 2.5 %slots.1 = (s32[264]{0:T(512)}, s32[264]{0:T(512)}, s32[2]{0:T(128)}) custom-call(s32[1]{0:T(128)} %bitcast.1.me_ref, s32[256]{0:T(256)} %bitcast.4, s32[256]{0:T(256)} %bitcast.5), custom_call_target="tpu_custom_call" | custom-call | flops 536870912 | bytes 6291456 | tf_op jit(solution)/shard_map/slots/pallas_call | solution.py:97
  74.2 2.6 %collective-permute-done.23.refs_13_.refs_17_ = bf16[2048,128]{1,0:T(8,128)(2,1)} collective-permute-done((bf16[2048,128]{1,0:T(8,128)(2,1)S(1)}, bf16[2048,128]{1,0:T(8,128)(2,1)}, u32[]{:S(2)}, u32[]{:S(2)}) %collective-permute-start.23) | collective-permute-done | bytes 524320 | tf_op jit(solution)/shard_map/ppermute | solution.py:26
  76.8 0.0 copy-start.28
  76.8 0.7 copy-done.28
  77.5 0.6 copy-done.29
  78.2 8.7 %grads_up.1 = bf16[160,4096]{1,0:T(8,128)(2,1)} custom-call(s32[264]{0:T(512)S(1)} %copy-done.28, s32[2]{0:T(128)S(1)} %copy-done.29, s32[256]{0:T(256)S(1)} %copy-done.25, s32[1]{0:T(128)} %bitcast.refs_0_.me_ref.refs_3_, bf16[2048,128]{1,0:T(8,128)(2,1)S(1)} %join_parts.3.refs_3_.refs_4_, bf16[2048,128]{1,0:T(8,128)(2,1)} %collective-permute-done.9.refs_3_.refs_5_, ...), custom_call_target="tpu_custom_call" | custom-call | flops 536870912 | bytes 6291456 | tf_op jit(solution)/shard_map/grads_up/pallas_call | solution.py:373
  86.9 0.6 collective-permute-start.30
  87.5 1.1 %add_stage.3 = (f32[512,128]{1,0:T(8,128)S(1)}, bf16[512,128]{1,0:T(8,128)(2,1)S(1)}, bf16[512,128]{1,0:T(8,128)(2,1)S(1)}, bf16[512,128]{1,0:T(8,128)(2,1)S(1)}) custom-call(f32[2048,128]{1,0:T(8,128)S(1)} %copy-done.17, bf16[2048,128]{1,0:T(8,128)(2,1)} %collective-permute-done.19.arrived_ref), custom_call_target="tpu_custom_call" | custom-call | flops 1000 | bytes 1048576 | tf_op jit(solution)/shard_map/add_stage/pallas_call | solution.py:246
  88.6 0.5 collective-permute-start.24
  89.0 2.6 %collective-permute-start.25 = (bf16[512,128]{1,0:T(8,128)(2,1)S(1)}, bf16[512,128]{1,0:T(8,128)(2,1)S(1)}, u32[]{:S(2)}, u32[]{:S(2)}) collective-permute-start(bf16[512,128]{1,0:T(8,128)(2,1)S(1)} %get-tuple-element.83), channel_id=1, source_target_pairs={{0,8},{1,9},{2,10},{3,11},{4,12},{5,13},{6,14},{7,15},{8,0},{9,1},... | collective-permute-start | bytes 393224 | tf_op jit(solution)/shard_map/ppermute | solution.py:26
  91.6 1.4 %collective-permute-start.26 = (bf16[512,128]{1,0:T(8,128)(2,1)S(1)}, bf16[512,128]{1,0:T(8,128)(2,1)S(1)}, u32[]{:S(2)}, u32[]{:S(2)}) collective-permute-start(bf16[512,128]{1,0:T(8,128)(2,1)S(1)} %get-tuple-element.84), channel_id=1, source_target_pairs={{0,12},{1,13},{2,14},{3,15},{4,8},{5,9},{6,10},{7,11},{8,4},{9,5},... | collective-permute-start | bytes 393224 | tf_op jit(solution)/shard_map/ppermute | solution.py:26
  93.1 8.0 %grads_down.1 = bf16[160,4096]{1,0:T(8,128)(2,1)} custom-call(s32[264]{0:T(512)S(1)} %copy-done.27, s32[2]{0:T(128)S(1)} %copy-done.29, s32[256]{0:T(256)S(1)} %copy-done.26, s32[1]{0:T(128)} %bitcast.refs_0_.me_ref.refs_3_, bf16[2048,128]{1,0:T(8,128)(2,1)S(1)} %copy-done.3, bf16[2048,128]{1,0:T(8,128)(2,1)S(1)} %copy-done.13, ...), custom_call_target="tpu_custom_call" | custom-call | flops 536870912 | bytes 6291456 | tf_op jit(solution)/shard_map/grads_down/pallas_call | solution.py:373
  101.1 0.8 collective-permute-done.25.refs_2_
  102.0 0.7 add_last.1
  (76 shorter events, 0.2 us)
Async XLA Ops:
  0.6 14.9 %collective-permute-start = (bf16[512,128]{1,0:T(8,128)(2,1)}, bf16[512,128]{1,0:T(8,128)(2,1)S(1)}, u32[]{:S(2)}, u32[]{:S(2)}) collective-permute-start(bf16[512,128]{1,0:T(8,128)(2,1)} %refs_0_), channel_id=1, source_target_pairs={{0,4},{1,5},{2,6},{3,7},{4,0},{5,1},{6,2},{7,3},{8,12},{9,13},{10,... | collective-permute-start | bytes 393224 | tf_op jit(solution)/shard_map/ppermute | solution.py:26
  3.7 13.2 %collective-permute-start.1 = (bf16[512,128]{1,0:T(8,128)(2,1)}, bf16[512,128]{1,0:T(8,128)(2,1)S(1)}, u32[]{:S(2)}, u32[]{:S(2)}) collective-permute-start(bf16[512,128]{1,0:T(8,128)(2,1)} %refs_0_), channel_id=1, source_target_pairs={{0,8},{1,9},{2,10},{3,11},{4,12},{5,13},{6,14},{7,15},{8,0},{9,1},... | collective-permute-start | bytes 393224 | tf_op jit(solution)/shard_map/ppermute | solution.py:26
  6.3 10.6 %collective-permute-start.2 = (bf16[512,128]{1,0:T(8,128)(2,1)}, bf16[512,128]{1,0:T(8,128)(2,1)S(1)}, u32[]{:S(2)}, u32[]{:S(2)}) collective-permute-start(bf16[512,128]{1,0:T(8,128)(2,1)} %refs_0_), channel_id=1, source_target_pairs={{0,12},{1,13},{2,14},{3,15},{4,8},{5,9},{6,10},{7,11},{8,4},{9,5},... | collective-permute-start | bytes 393224 | tf_op jit(solution)/shard_map/ppermute | solution.py:26
  6.3 10.6 %collective-permute-start.3 = (bf16[512,128]{1,0:T(8,128)(2,1)}, bf16[512,128]{1,0:T(8,128)(2,1)S(1)}, u32[]{:S(2)}, u32[]{:S(2)}) collective-permute-start(bf16[512,128]{1,0:T(8,128)(2,1)} %refs_0_.1), channel_id=1, source_target_pairs={{0,16},{16,0},{1,17},{17,1},{2,18},{18,2},{3,19},{19,3},{4,20},{20... | collective-permute-start | bytes 393224 | tf_op jit(solution)/shard_map/ppermute | solution.py:26
  8.0 8.9 %collective-permute-start.4 = (bf16[512,128]{1,0:T(8,128)(2,1)}, bf16[512,128]{1,0:T(8,128)(2,1)S(1)}, u32[]{:S(2)}, u32[]{:S(2)}) collective-permute-start(bf16[512,128]{1,0:T(8,128)(2,1)} %refs_0_.1), channel_id=1, source_target_pairs={{0,18},{1,19},{2,16},{3,17},{4,22},{5,23},{6,20},{7,21},{8,26},{9,... | collective-permute-start | bytes 393224 | tf_op jit(solution)/shard_map/ppermute | solution.py:36
  9.5 1.6 %copy-start.4 = (bf16[256,4096]{1,0:T(8,128)(2,1)S(1)}, bf16[256,4096]{1,0:T(8,128)(2,1)}, u32[]{:S(2)}) copy-start(bf16[256,4096]{1,0:T(8,128)(2,1)} %src.2) | copy-start | bytes 6291460
  11.1 1.6 %copy-start.5 = (bf16[256,4096]{1,0:T(8,128)(2,1)S(1)}, bf16[256,4096]{1,0:T(8,128)(2,1)}, u32[]{:S(2)}) copy-start(bf16[256,4096]{1,0:T(8,128)(2,1)} %src.3) | copy-start | bytes 6291460
  12.7 4.8 %copy-start.24 = (bf16[512,128]{1,0:T(8,128)(2,1)S(1)}, bf16[512,128]{1,0:T(8,128)(2,1)}, u32[]{:S(2)}) copy-start(bf16[512,128]{1,0:T(8,128)(2,1)} %refs_0_) | copy-start | bytes 393220
  12.7 13.5 %copy-start.25 = (s32[256]{0:T(256)S(1)}, s32[256]{0:T(256)}, u32[]{:S(2)}) copy-start(s32[256]{0:T(256)} %refs_2_.2) | copy-start | bytes 3076
  14.2 1.3 %copy-start = (bf16[8192,128]{1,0:T(8,128)(2,1)}, bf16[8192,128]{1,0:T(8,128)(2,1)S(1)}, u32[]{:S(2)}) copy-start(bf16[8192,128]{1,0:T(8,128)(2,1)S(1)} %relayout.3.refs_2_) | copy-start | bytes 6291460
  16.9 0.7 copy-start.22
  17.6 6.1 %collective-permute-start.8 = (bf16[2048,128]{1,0:T(8,128)(2,1)S(1)}, bf16[2048,128]{1,0:T(8,128)(2,1)S(1)}, u32[]{:S(2)}, u32[]{:S(2)}) collective-permute-start(bf16[2048,128]{1,0:T(8,128)(2,1)S(1)} %join_parts.3.refs_3_.refs_4_), channel_id=1, source_target_pairs={{0,1},{1,0},{2,3},{3,2},{4,5},{5,4},{6,7},{7,6},{8,9},{9,8},{10,11... | collective-permute-start | bytes 1572872 | tf_op jit(solution)/shard_map/ppermute | solution.py:26
  17.7 18.3 %collective-permute-start.10 = (bf16[2048,128]{1,0:T(8,128)(2,1)S(1)}, bf16[2048,128]{1,0:T(8,128)(2,1)}, u32[]{:S(2)}, u32[]{:S(2)}) collective-permute-start(bf16[2048,128]{1,0:T(8,128)(2,1)S(1)} %join_parts.3.refs_3_.refs_4_), channel_id=1, source_target_pairs={{0,16},{16,0},{1,17},{17,1},{2,18},{18,2},{3,19},{19,3},{4,20},{20... | collective-permute-start | bytes 1572872 | tf_op jit(solution)/shard_map/ppermute | solution.py:26
  19.2 16.7 %collective-permute-start.9 = (bf16[2048,128]{1,0:T(8,128)(2,1)S(1)}, bf16[2048,128]{1,0:T(8,128)(2,1)}, u32[]{:S(2)}, u32[]{:S(2)}) collective-permute-start(bf16[2048,128]{1,0:T(8,128)(2,1)S(1)} %join_parts.3.refs_3_.refs_4_), channel_id=1, source_target_pairs={{0,2},{1,3},{2,0},{3,1},{4,6},{5,7},{6,4},{7,5},{8,10},{9,11},{10,... | collective-permute-start | bytes 1572872 | tf_op jit(solution)/shard_map/ppermute | solution.py:26
  20.7 8.4 %collective-permute-start.5 = (bf16[512,128]{1,0:T(8,128)(2,1)}, bf16[512,128]{1,0:T(8,128)(2,1)}, u32[]{:S(2)}, u32[]{:S(2)}) collective-permute-start(bf16[512,128]{1,0:T(8,128)(2,1)} %refs_0_.1), channel_id=1, source_target_pairs={{0,4},{1,5},{2,6},{3,7},{4,0},{5,1},{6,2},{7,3},{8,12},{9,13},{10,... | collective-permute-start | bytes 393224 | tf_op jit(solution)/shard_map/ppermute | solution.py:26
  22.7 13.3 %collective-permute-start.6 = (bf16[512,128]{1,0:T(8,128)(2,1)}, bf16[512,128]{1,0:T(8,128)(2,1)}, u32[]{:S(2)}, u32[]{:S(2)}) collective-permute-start(bf16[512,128]{1,0:T(8,128)(2,1)} %refs_0_.1), channel_id=1, source_target_pairs={{0,8},{1,9},{2,10},{3,11},{4,12},{5,13},{6,14},{7,15},{8,0},{9,1},... | collective-permute-start | bytes 393224 | tf_op jit(solution)/shard_map/ppermute | solution.py:26
  23.7 5.5 %copy-start.8 = (bf16[2048,128]{1,0:T(8,128)(2,1)}, bf16[2048,128]{1,0:T(8,128)(2,1)S(1)}, u32[]{:S(2)}) copy-start(bf16[2048,128]{1,0:T(8,128)(2,1)S(1)} %collective-permute-done.8.refs_4_.refs_6_) | copy-start | bytes 1572868
  23.7 12.3 %collective-permute-start.7 = (bf16[512,128]{1,0:T(8,128)(2,1)}, bf16[512,128]{1,0:T(8,128)(2,1)}, u32[]{:S(2)}, u32[]{:S(2)}) collective-permute-start(bf16[512,128]{1,0:T(8,128)(2,1)} %refs_0_.1), channel_id=1, source_target_pairs={{0,12},{1,13},{2,14},{3,15},{4,8},{5,9},{6,10},{7,11},{8,4},{9,5},... | collective-permute-start | bytes 393224 | tf_op jit(solution)/shard_map/ppermute | solution.py:26
  25.2 0.9 copy-start.23
  36.0 4.8 %collective-permute-start.12 = (bf16[2048,128]{1,0:T(8,128)(2,1)}, bf16[2048,128]{1,0:T(8,128)(2,1)S(1)}, u32[]{:S(2)}, u32[]{:S(2)}) collective-permute-start(bf16[2048,128]{1,0:T(8,128)(2,1)} %collective-permute-done.9.refs_3_.refs_5_), channel_id=1, source_target_pairs={{0,1},{1,0},{2,3},{3,2},{4,5},{5,4},{6,7},{7,6},{8,9},{9,8},{10,11... | collective-permute-start | bytes 1572872 | tf_op jit(solution)/shard_map/ppermute | solution.py:26
  37.2 8.1 %copy-start.2 = (bf16[2048,128]{1,0:T(8,128)(2,1)}, bf16[2048,128]{1,0:T(8,128)(2,1)S(1)}, u32[]{:S(2)}) copy-start(bf16[2048,128]{1,0:T(8,128)(2,1)S(1)} %join_parts.5.refs_3_.refs_4_) | copy-start | bytes 1572868
  37.2 8.1 %copy-start.1 = (bf16[8192,128]{1,0:T(8,128)(2,1)S(1)}, bf16[8192,128]{1,0:T(8,128)(2,1)}, u32[]{:S(2)}) copy-start(bf16[8192,128]{1,0:T(8,128)(2,1)} %copy-done) | copy-start | bytes 6291460
  37.2 8.1 %copy-start.26 = (s32[256]{0:T(256)S(1)}, s32[256]{0:T(256)}, u32[]{:S(2)}) copy-start(s32[256]{0:T(256)} %refs_2_.3) | copy-start | bytes 3076
  37.2 8.0 %collective-permute-start.13 = (bf16[2048,128]{1,0:T(8,128)(2,1)S(1)}, bf16[2048,128]{1,0:T(8,128)(2,1)S(1)}, u32[]{:S(2)}, u32[]{:S(2)}) collective-permute-start(bf16[2048,128]{1,0:T(8,128)(2,1)S(1)} %join_parts.5.refs_3_.refs_4_), channel_id=1, source_target_pairs={{0,1},{1,0},{2,3},{3,2},{4,5},{5,4},{6,7},{7,6},{8,9},{9,8},{10,11... | collective-permute-start | bytes 1572872 | tf_op jit(solution)/shard_map/ppermute | solution.py:26
  37.8 17.0 %collective-permute-start.11 = (bf16[2048,128]{1,0:T(8,128)(2,1)S(1)}, bf16[2048,128]{1,0:T(8,128)(2,1)S(1)}, u32[]{:S(2)}, u32[]{:S(2)}) collective-permute-start(bf16[2048,128]{1,0:T(8,128)(2,1)S(1)} %join_parts.5.refs_3_.refs_4_), channel_id=1, source_target_pairs={{0,2},{1,3},{2,0},{3,1},{4,6},{5,7},{6,4},{7,5},{8,10},{9,11},{10,... | collective-permute-start | bytes 1572872 | tf_op jit(solution)/shard_map/ppermute | solution.py:26
  38.3 16.5 %collective-permute-start.14 = (bf16[2048,128]{1,0:T(8,128)(2,1)}, bf16[2048,128]{1,0:T(8,128)(2,1)}, u32[]{:S(2)}, u32[]{:S(2)}) collective-permute-start(bf16[2048,128]{1,0:T(8,128)(2,1)} %collective-permute-done.9.refs_3_.refs_5_), channel_id=1, source_target_pairs={{0,16},{16,0},{1,17},{17,1},{2,18},{18,2},{3,19},{19,3},{4,20},{20... | collective-permute-start | bytes 1572872 | tf_op jit(solution)/shard_map/ppermute | solution.py:26
  38.8 13.4 %collective-permute-start.15 = (bf16[1024,128]{1,0:T(8,128)(2,1)S(1)}, bf16[1024,128]{1,0:T(8,128)(2,1)S(1)}, u32[]{:S(2)}, u32[]{:S(2)}) collective-permute-start(bf16[1024,128]{1,0:T(8,128)(2,1)S(1)} %join_parts.4.refs_8_), channel_id=1, source_target_pairs={{0,4},{1,5},{2,6},{3,7},{4,0},{5,1},{6,2},{7,3},{8,12},{9,13},{10,... | collective-permute-start | bytes 786440 | tf_op jit(solution)/shard_map/ppermute | solution.py:26
  40.8 4.5 %copy-start.6 = (bf16[2048,128]{1,0:T(8,128)(2,1)}, bf16[2048,128]{1,0:T(8,128)(2,1)S(1)}, u32[]{:S(2)}) copy-start(bf16[2048,128]{1,0:T(8,128)(2,1)S(1)} %collective-permute-done.12.refs_4_.refs_7_) | copy-start | bytes 1572868
  40.8 14.0 %collective-permute-start.16 = (bf16[1024,128]{1,0:T(8,128)(2,1)S(1)}, bf16[1024,128]{1,0:T(8,128)(2,1)S(1)}, u32[]{:S(2)}, u32[]{:S(2)}) collective-permute-start(bf16[1024,128]{1,0:T(8,128)(2,1)S(1)} %join_parts.4.refs_8_), channel_id=1, source_target_pairs={{0,8},{1,9},{2,10},{3,11},{4,12},{5,13},{6,14},{7,15},{8,0},{9,1},... | collective-permute-start | bytes 786440 | tf_op jit(solution)/shard_map/ppermute | solution.py:26
  45.3 11.2 %copy-start.10 = (bf16[2048,128]{1,0:T(8,128)(2,1)}, bf16[2048,128]{1,0:T(8,128)(2,1)S(1)}, u32[]{:S(2)}) copy-start(bf16[2048,128]{1,0:T(8,128)(2,1)S(1)} %collective-permute-done.13.refs_4_.refs_6_) | copy-start | bytes 1572868
  52.2 7.4 %copy-start.18 = (bf16[1024,128]{1,0:T(8,128)(2,1)}, bf16[1024,128]{1,0:T(8,128)(2,1)S(1)}, u32[]{:S(2)}) copy-start(bf16[1024,128]{1,0:T(8,128)(2,1)S(1)} %collective-permute-done.15.refs_9_) | copy-start | bytes 786436
  54.8 4.8 %copy-start.20 = (bf16[1024,128]{1,0:T(8,128)(2,1)}, bf16[1024,128]{1,0:T(8,128)(2,1)S(1)}, u32[]{:S(2)}) copy-start(bf16[1024,128]{1,0:T(8,128)(2,1)S(1)} %collective-permute-done.16.refs_10_) | copy-start | bytes 786436
  54.8 4.8 %copy-start.12 = (bf16[2048,128]{1,0:T(8,128)(2,1)}, bf16[2048,128]{1,0:T(8,128)(2,1)S(1)}, u32[]{:S(2)}) copy-start(bf16[2048,128]{1,0:T(8,128)(2,1)S(1)} %collective-permute-done.11.refs_3_.refs_5_) | copy-start | bytes 1572868
  54.8 2.0 %collective-permute-start.17 = (bf16[2048,128]{1,0:T(8,128)(2,1)S(1)}, bf16[2048,128]{1,0:T(8,128)(2,1)S(1)}, u32[]{:S(2)}, u32[]{:S(2)}) collective-permute-start(bf16[2048,128]{1,0:T(8,128)(2,1)S(1)} %collective-permute-done.11.refs_3_.refs_5_), channel_id=1, source_target_pairs={{0,1},{1,0},{2,3},{3,2},{4,5},{5,4},{6,7},{7,6},{8,9},{9,8},{10,11... | collective-permute-start | bytes 1572872 | tf_op jit(solution)/shard_map/ppermute | solution.py:26
  56.8 5.0 %copy-start.14 = (bf16[2048,128]{1,0:T(8,128)(2,1)}, bf16[2048,128]{1,0:T(8,128)(2,1)S(1)}, u32[]{:S(2)}) copy-start(bf16[2048,128]{1,0:T(8,128)(2,1)S(1)} %collective-permute-done.17.refs_3_.refs_7_) | copy-start | bytes 1572868
  61.8 4.5 %collective-permute-start.18 = (bf16[4096,128]{1,0:T(8,128)(2,1)S(1)}, bf16[4096,128]{1,0:T(8,128)(2,1)S(1)}, u32[]{:S(2)}, u32[]{:S(2)}) collective-permute-start(bf16[4096,128]{1,0:T(8,128)(2,1)S(1)} %input_grad_part.2), channel_id=1, source_target_pairs={{0,1},{1,0},{2,3},{3,2},{4,5},{5,4},{6,7},{7,6},{8,9},{9,8},{10,11... | collective-permute-start | bytes 3145736 | tf_op jit(solution)/shard_map/ppermute | solution.py:26
  62.1 9.2 %collective-permute-start.21 = (bf16[2048,128]{1,0:T(8,128)(2,1)}, bf16[2048,128]{1,0:T(8,128)(2,1)}, u32[]{:S(2)}, u32[]{:S(2)}) collective-permute-start(bf16[2048,128]{1,0:T(8,128)(2,1)} %collective-permute-done.10.refs_8_), channel_id=1, source_target_pairs={{0,1},{1,0},{2,3},{3,2},{4,5},{5,4},{6,7},{7,6},{8,9},{9,8},{10,11... | collective-permute-start | bytes 1572872 | tf_op jit(solution)/shard_map/ppermute | solution.py:26
  62.4 8.9 %collective-permute-start.22 = (bf16[2048,128]{1,0:T(8,128)(2,1)}, bf16[2048,128]{1,0:T(8,128)(2,1)}, u32[]{:S(2)}, u32[]{:S(2)}) collective-permute-start(bf16[2048,128]{1,0:T(8,128)(2,1)} %collective-permute-done.14.refs_9_), channel_id=1, source_target_pairs={{0,1},{1,0},{2,3},{3,2},{4,5},{5,4},{6,7},{7,6},{8,9},{9,8},{10,11... | collective-permute-start | bytes 1572872 | tf_op jit(solution)/shard_map/ppermute | solution.py:26
  62.6 14.2 %collective-permute-start.23 = (bf16[2048,128]{1,0:T(8,128)(2,1)S(1)}, bf16[2048,128]{1,0:T(8,128)(2,1)}, u32[]{:S(2)}, u32[]{:S(2)}) collective-permute-start(bf16[2048,128]{1,0:T(8,128)(2,1)S(1)} %get-tuple-element.70.both_ref.refs_12_.refs_16_), channel_id=1, source_target_pairs={{0,16},{16,0},{1,17},{17,1},{2,18},{18,2},{3,19},{19,3},{4,20},{20... | collective-permute-start | bytes 1572872 | tf_op jit(solution)/shard_map/ppermute | solution.py:26
  66.3 10.5 %copy-start.7 = (bf16[2048,128]{1,0:T(8,128)(2,1)S(1)}, bf16[2048,128]{1,0:T(8,128)(2,1)}, u32[]{:S(2)}) copy-start(bf16[2048,128]{1,0:T(8,128)(2,1)} %copy-done.6) | copy-start | bytes 1572868
  66.3 10.5 %copy-start.9 = (bf16[2048,128]{1,0:T(8,128)(2,1)S(1)}, bf16[2048,128]{1,0:T(8,128)(2,1)}, u32[]{:S(2)}) copy-start(bf16[2048,128]{1,0:T(8,128)(2,1)} %copy-done.8) | copy-start | bytes 1572868
  67.3 9.5 %copy-start.16 = (f32[2048,128]{1,0:T(8,128)}, f32[2048,128]{1,0:T(8,128)S(1)}, u32[]{:S(2)}) copy-start(f32[2048,128]{1,0:T(8,128)S(1)} %get-tuple-element.72.terms_ref) | copy-start | bytes 3145732
  67.3 19.6 %collective-permute-start.19 = (bf16[2048,128]{1,0:T(8,128)(2,1)}, bf16[2048,128]{1,0:T(8,128)(2,1)}, u32[]{:S(2)}, u32[]{:S(2)}) collective-permute-start(bf16[2048,128]{1,0:T(8,128)(2,1)} %get-tuple-element.73), channel_id=1, source_target_pairs={{0,2},{1,3},{2,0},{3,1},{4,6},{5,7},{6,4},{7,5},{8,10},{9,11},{10,... | collective-permute-start | bytes 1572872 | tf_op jit(solution)/shard_map/ppermute | solution.py:26
  68.8 18.1 %collective-permute-start.20 = (bf16[1024,128]{1,0:T(8,128)(2,1)S(1)}, bf16[1024,128]{1,0:T(8,128)(2,1)}, u32[]{:S(2)}, u32[]{:S(2)}) collective-permute-start(bf16[1024,128]{1,0:T(8,128)(2,1)S(1)} %join_parts.4.refs_8_), channel_id=1, source_target_pairs={{0,12},{1,13},{2,14},{3,15},{4,8},{5,9},{6,10},{7,11},{8,4},{9,5},... | collective-permute-start | bytes 786440 | tf_op jit(solution)/shard_map/ppermute | solution.py:26
  71.2 17.8 %collective-permute-start.27 = (bf16[1024,128]{1,0:T(8,128)(2,1)S(1)}, bf16[1024,128]{1,0:T(8,128)(2,1)}, u32[]{:S(2)}, u32[]{:S(2)}) collective-permute-start(bf16[1024,128]{1,0:T(8,128)(2,1)S(1)} %join_parts.4.refs_8_), channel_id=1, source_target_pairs={{0,1},{1,0},{2,3},{3,2},{4,5},{5,4},{6,7},{7,6},{8,9},{9,8},{10,11... | collective-permute-start | bytes 786440 | tf_op jit(solution)/shard_map/ppermute | solution.py:26
  71.2 20.4 %collective-permute-start.28 = (bf16[1024,128]{1,0:T(8,128)(2,1)}, bf16[1024,128]{1,0:T(8,128)(2,1)}, u32[]{:S(2)}, u32[]{:S(2)}) collective-permute-start(bf16[1024,128]{1,0:T(8,128)(2,1)} %copy-done.18), channel_id=1, source_target_pairs={{0,1},{1,0},{2,3},{3,2},{4,5},{5,4},{6,7},{7,6},{8,9},{9,8},{10,11... | collective-permute-start | bytes 786440 | tf_op jit(solution)/shard_map/ppermute | solution.py:26
  76.8 16.2 %collective-permute-start.29 = (bf16[1024,128]{1,0:T(8,128)(2,1)}, bf16[1024,128]{1,0:T(8,128)(2,1)S(1)}, u32[]{:S(2)}, u32[]{:S(2)}) collective-permute-start(bf16[1024,128]{1,0:T(8,128)(2,1)} %copy-done.20), channel_id=1, source_target_pairs={{0,1},{1,0},{2,3},{3,2},{4,5},{5,4},{6,7},{7,6},{8,9},{9,8},{10,11... | collective-permute-start | bytes 786440 | tf_op jit(solution)/shard_map/ppermute | solution.py:26
  76.8 0.7 copy-start.28
  77.5 0.6 copy-start.29
  78.1 9.3 %copy-start.17 = (f32[2048,128]{1,0:T(8,128)S(1)}, f32[2048,128]{1,0:T(8,128)}, u32[]{:S(2)}) copy-start(f32[2048,128]{1,0:T(8,128)} %copy-done.16) | copy-start | bytes 3145732
  78.1 14.9 %copy-start.3 = (bf16[2048,128]{1,0:T(8,128)(2,1)S(1)}, bf16[2048,128]{1,0:T(8,128)(2,1)}, u32[]{:S(2)}) copy-start(bf16[2048,128]{1,0:T(8,128)(2,1)} %copy-done.2) | copy-start | bytes 1572868
  78.1 14.9 %copy-start.11 = (bf16[2048,128]{1,0:T(8,128)(2,1)S(1)}, bf16[2048,128]{1,0:T(8,128)(2,1)}, u32[]{:S(2)}) copy-start(bf16[2048,128]{1,0:T(8,128)(2,1)} %copy-done.10) | copy-start | bytes 1572868
  78.1 15.0 %copy-start.13 = (bf16[2048,128]{1,0:T(8,128)(2,1)S(1)}, bf16[2048,128]{1,0:T(8,128)(2,1)}, u32[]{:S(2)}) copy-start(bf16[2048,128]{1,0:T(8,128)(2,1)} %copy-done.12) | copy-start | bytes 1572868
  78.1 15.0 %copy-start.15 = (bf16[2048,128]{1,0:T(8,128)(2,1)S(1)}, bf16[2048,128]{1,0:T(8,128)(2,1)}, u32[]{:S(2)}) copy-start(bf16[2048,128]{1,0:T(8,128)(2,1)} %copy-done.14) | copy-start | bytes 1572868
  78.1 15.0 %copy-start.19 = (bf16[1024,128]{1,0:T(8,128)(2,1)S(1)}, bf16[1024,128]{1,0:T(8,128)(2,1)}, u32[]{:S(2)}) copy-start(bf16[1024,128]{1,0:T(8,128)(2,1)} %copy-done.18) | copy-start | bytes 786436
  78.1 15.0 %copy-start.21 = (bf16[1024,128]{1,0:T(8,128)(2,1)S(1)}, bf16[1024,128]{1,0:T(8,128)(2,1)}, u32[]{:S(2)}) copy-start(bf16[1024,128]{1,0:T(8,128)(2,1)} %copy-done.20) | copy-start | bytes 786436
  78.2 15.0 %copy-start.27 = (s32[264]{0:T(512)S(1)}, s32[264]{0:T(512)}, u32[]{:S(2)}) copy-start(s32[264]{0:T(512)} %get-tuple-element.85.refs_0_) | copy-start | bytes 3172
  86.9 6.2 %collective-permute-start.30 = (bf16[1024,128]{1,0:T(8,128)(2,1)}, bf16[1024,128]{1,0:T(8,128)(2,1)S(1)}, u32[]{:S(2)}, u32[]{:S(2)}) collective-permute-start(bf16[1024,128]{1,0:T(8,128)(2,1)} %collective-permute-done.20.refs_11_), channel_id=1, source_target_pairs={{0,1},{1,0},{2,3},{3,2},{4,5},{5,4},{6,7},{7,6},{8,9},{9,8},{10,11... | collective-permute-start | bytes 786440 | tf_op jit(solution)/shard_map/ppermute | solution.py:26
  88.6 12.5 %collective-permute-start.24 = (bf16[512,128]{1,0:T(8,128)(2,1)S(1)}, bf16[512,128]{1,0:T(8,128)(2,1)S(1)}, u32[]{:S(2)}, u32[]{:S(2)}) collective-permute-start(bf16[512,128]{1,0:T(8,128)(2,1)S(1)} %get-tuple-element.82), channel_id=1, source_target_pairs={{0,4},{1,5},{2,6},{3,7},{4,0},{5,1},{6,2},{7,3},{8,12},{9,13},{10,... | collective-permute-start | bytes 393224 | tf_op jit(solution)/shard_map/ppermute | solution.py:26
  89.0 12.9 %collective-permute-start.25 = (bf16[512,128]{1,0:T(8,128)(2,1)S(1)}, bf16[512,128]{1,0:T(8,128)(2,1)S(1)}, u32[]{:S(2)}, u32[]{:S(2)}) collective-permute-start(bf16[512,128]{1,0:T(8,128)(2,1)S(1)} %get-tuple-element.83), channel_id=1, source_target_pairs={{0,8},{1,9},{2,10},{3,11},{4,12},{5,13},{6,14},{7,15},{8,0},{9,1},... | collective-permute-start | bytes 393224 | tf_op jit(solution)/shard_map/ppermute | solution.py:26
  91.6 10.3 %collective-permute-start.26 = (bf16[512,128]{1,0:T(8,128)(2,1)S(1)}, bf16[512,128]{1,0:T(8,128)(2,1)S(1)}, u32[]{:S(2)}, u32[]{:S(2)}) collective-permute-start(bf16[512,128]{1,0:T(8,128)(2,1)S(1)} %get-tuple-element.84), channel_id=1, source_target_pairs={{0,12},{1,13},{2,14},{3,15},{4,8},{5,9},{6,10},{7,11},{8,4},{9,5},... | collective-permute-start | bytes 393224 | tf_op jit(solution)/shard_map/ppermute | solution.py:26

commit v2 on v1

--- a/solution.py
+++ b/solution.py
@@ -161,84 +161,91 @@
     x_refs = refs[3 : 3 + len(starts)]
     rest = list(refs[3 + len(starts) :])
     acc_in = None if first else rest.pop(0)
-    hidden = rest.pop(0) if last else None
-    if last:
-        both, active, acc = rest
+    if not last:
+        (acc,) = rest
+    elif is_up:
+        active, slope_ref, acc = rest
     else:
-        (acc,) = rest
+        slope_ref, slope_grad, acc = rest
     acc[...] = jnp.zeros_like(acc) if first else acc_in[...]
     add_blocks(me_ref, where_ref, w_ref, x_refs, starts, acc, rows, is_up)
     if last:
         ff = acc.shape[0]
 
         def body(i, carry):
-            at = pl.multiple_of(i * BS, BS)
-            value, slope = gelu_slope(hidden[pl.ds(at, BS), :])
-            both[pl.ds(at, BS), :] = value.astype(BF)
-            active[pl.ds(at, BS), :] = value.astype(BF)
-            both[pl.ds(ff + at, BS), :] = (acc[pl.ds(at, BS), :] * slope).astype(BF)
+            here = pl.ds(pl.multiple_of(i * BS, BS), BS)
+            if is_up:
+                value, slope = gelu_slope(acc[here, :])
+                active[here, :] = value.astype(BF)
+                slope_ref[here, :] = slope
+            else:
+                slope_grad[here, :] = (acc[here, :] * slope_ref[here, :]).astype(BF)
             return carry
 
         lax.fori_loop(0, ff // BS, body, 0)
 
 
-def hidden_sum(rows, is_up, me, where, w, pieces, starts, acc=None, hidden=None):
+def hidden_sum(rows, is_up, me, where, w, pieces, starts, acc=None, last=False, slope=None):
     ff, tokens = FBLK * BS, pieces[0].shape[1]
     smem = pl.BlockSpec(memory_space=SMEM)
     vmem = pl.BlockSpec(memory_space=VMEM)
-    more = [x for x in (acc, hidden) if x is not None]
-    if hidden is None:
-        outs, scratch = [jax.ShapeDtypeStruct((ff, tokens), F32)], []
+    more = [x for x in (acc, slope) if x is not None]
+    whole, kept = jax.ShapeDtypeStruct((ff, tokens), F32), jax.ShapeDtypeStruct((ff, tokens), BF)
+    if not last:
+        outs = [whole]
+    elif is_up:
+        outs = [kept, whole]
     else:
-        outs = [jax.ShapeDtypeStruct((n * ff, tokens), BF) for n in (2, 1)]
-        scratch = [VMEM((ff, tokens), F32)]
+        outs = [kept]
     return pl.pallas_call(
-        functools.partial(
-            hidden_kernel, rows, is_up, tuple(starts), acc is None, hidden is not None
-        ),
+        functools.partial(hidden_kernel, rows, is_up, tuple(starts), acc is None, last),
         in_specs=[smem, smem] + [vmem] * (1 + len(pieces) + len(more)),
         out_specs=[vmem] * len(outs),
         out_shape=outs,
-        scratch_shapes=scratch,
+        scratch_shapes=[VMEM((ff, tokens), F32)] if last else [],
         compiler_params=pltpu.CompilerParams(vmem_limit_bytes=12 << 20),
         cost_estimate=COST,
-        name=("hidden" if is_up else "upper") + ("" if hidden is None else "_last"),
+        name=("hidden" if is_up else "upper") + ("_last" if last else ""),
     )(me, where, w, *pieces, *more)
 
 
-def input_grad_kernel(rows, bit, me_ref, col_ref, w_ref, both_ref, out):
+def input_grad_kernel(rows, skip, bits, me_ref, col_ref, w_ref, s_ref, *outs):
     per = rows // BS
-    chunks = out.shape[0] // rows
-    base = both_ref.shape[0] // 2
-
-    def body(i, carry):
-        start = source(me_ref[0] ^ bit, i, chunks // 2) * per
+    chunks = outs[0].shape[0] // rows
+
+    def one(i, bit, out):
+        start = source(me_ref[0] ^ bit, skip + i, chunks) * per
         for rr in range(per):
             r = start + rr
             w = w_ref[pl.ds(pl.multiple_of(r * BS, BS), BS), :]
             parts = [
-                both_ref[pl.ds(pl.multiple_of(base + col_ref[KB * r + q] * BS, BS), BS), :]
+                s_ref[pl.ds(pl.multiple_of(col_ref[KB * r + q] * BS, BS), BS), :]
                 for q in range(KB)
             ]
             t = jnp.dot(w, jnp.concatenate(parts, axis=0), preferred_element_type=F32)
             out[pl.ds(pl.multiple_of(i * rows + rr * BS, BS), BS), :] = t.astype(out.dtype)
+
+    def body(i, carry):
+        for bit, out in zip(bits, outs):
+            one(i, bit, out)
         return carry
 
     lax.fori_loop(0, chunks, body, 0)
 
 
-def input_grad_part(rows, bit, me, col, w, both, dtype):
+def input_grad_part(rows, skip, bits, me, col, w, slope_grad):
     smem = pl.BlockSpec(memory_space=SMEM)
     vmem = pl.BlockSpec(memory_space=VMEM)
+    shape = (w.shape[0] // 4, slope_grad.shape[1])
     return pl.pallas_call(
-        functools.partial(input_grad_kernel, rows, bit),
+        functools.partial(input_grad_kernel, rows, skip, bits),
         in_specs=[smem, smem, vmem, vmem],
-        out_specs=vmem,
-        out_shape=jax.ShapeDtypeStruct((w.shape[0] // 2, both.shape[1]), dtype),
+        out_specs=[vmem] * len(bits),
+        out_shape=[jax.ShapeDtypeStruct(shape, BF if bit else F32) for bit in bits],
         compiler_params=pltpu.CompilerParams(vmem_limit_bytes=10 << 20),
         cost_estimate=COST,
         name="input_grad_part",
-    )(me, col, w, both)
+    )(me, col, w, slope_grad)
 
 
 def in_vmem(kernel, outs, *args):
@@ -267,17 +274,21 @@
 
 def add_and_split(terms, arrived, keep):
     rows, tokens = terms.shape
-    sends = (rows - keep) // min(keep, rows - keep)
-    size = (rows - keep) // sends
-
-    def add_stage(terms_ref, arrived_ref, keep_ref, *send_refs):
-        keep_ref[...] = terms_ref[:keep, :] + arrived_ref[:keep, :].astype(F32)
-        for n, ref in enumerate(send_refs):
-            at = pl.ds(keep + n * size, size)
-            ref[...] = (terms_ref[at, :] + arrived_ref[at, :].astype(F32)).astype(BF)
-
-    outs = [((keep, tokens), F32)] + [((size, tokens), BF)] * sends
-    return in_vmem(add_stage, outs, terms, arrived)
+    size = keep if keep else rows
+    sends = (rows - keep) // size
+
+    def add_stage(terms_ref, *refs):
+        arrived_refs, outs = refs[: len(arrived)], refs[len(arrived) :]
+        for n, ref in enumerate(outs):
+            at = pl.ds(n * size, size)
+            total = terms_ref[at, :]
+            for more in arrived_refs:
+                total = total + more[at, :].astype(F32)
+            ref[...] = total.astype(ref.dtype)
+
+    outs = [((keep, tokens), F32)] if keep else []
+    outs += [((size, tokens), BF)] * sends
+    return in_vmem(add_stage, outs, terms, *arrived)
 
 
 def add_all(terms, arrived):
@@ -293,9 +304,8 @@
 def grads_kernel(groups, pieces, capacity, batch, rows, is_up, *refs):
     tab, count, order, me_ref = refs[:4]
     flat = refs[4 : 4 + sum(pieces)]
-    both_refs = refs[4 + len(flat) : 4 + len(flat) + groups]
-    out, features, tiles, *sem = refs[4 + len(flat) + groups :]
-    base = both_refs[0].shape[0] // 2 if is_up else 0
+    hidden_refs = refs[4 + len(flat) : 4 + len(flat) + groups]
+    out, features, tiles_a, tiles_b, *sem = refs[4 + len(flat) + groups :]
     copies = []
     n = 0
     for g in range(groups):
@@ -321,53 +331,71 @@
     live_slots = count[0 if is_up else 1]
 
     half = features.shape[1] // rows // 2
-    far = half // 2
+    far_bits = (half // 2).bit_length() - 1
     per = rows // BS
+    per_bits = per.bit_length() - 1
 
     def place(row, y_first):
-        apart = (row // per) ^ me_ref[0]
-        core, y, z = apart & 1, (apart >> 1) & 1, apart >> 2
-        spot = core * half + (z * 2 + y if y_first else y * far + z)
-        return pl.multiple_of(spot * rows + (row % per) * BS, BS)
-
-    def body(b, carry):
-        live = slot + b * batch < live_slots
+        apart = lax.shift_right_logical(row, per_bits) ^ me_ref[0]
+        core, y = apart & 1, lax.shift_right_logical(apart, 1) & 1
+        z = lax.shift_right_logical(apart, 2)
+        spot = core * half + (z * 2 + y if y_first else (y << far_bits) + z)
+        return pl.multiple_of(spot * rows + (row & (per - 1)) * BS, BS)
+
+    def multiply(first, tiles):
         for u in range(batch):
-            e = jnp.where(b * batch + u < live_slots, tab[b * batch + u], 0)
-            at = [place(e // KB, g > 0 and not is_up) for g in range(groups)]
-            to = pl.multiple_of(base + order[e] * BS, BS)
+            e = jnp.where(first + u < live_slots, tab[first + u], 0)
+            row = lax.shift_right_logical(e, KB.bit_length() - 1)
+            at = [place(row, False)]
+            at += [at[0] if is_up else place(row, True)] * (groups - 1)
+            to = pl.multiple_of(order[e] * BS, BS)
             f = jnp.concatenate(
                 [features[g, pl.ds(at[g], BS), :] for g in range(groups)], axis=1
             )
-            h = jnp.concatenate([ref[pl.ds(to, BS), :] for ref in both_refs], axis=1)
+            h = jnp.concatenate([ref[pl.ds(to, BS), :] for ref in hidden_refs], axis=1)
             left, right = (f, h) if is_up else (h, f)
             t = lax.dot_general(
                 left, right, (((1,), (1,)), ((), ())), preferred_element_type=F32
             )
             tiles[u * PITCH : u * PITCH + BS, :BS] = t
+
+    def flush(first, tiles):
+        live = slot + first < live_slots
         for a in range(BS // 2):
             even = tiles[pl.ds(2 * a, batch, stride=PITCH), :]
             odd = pltpu.roll(tiles[pl.ds(2 * a + 1, batch, stride=PITCH), :], BS, 1)
             out[
-                pl.ds(pl.multiple_of(b * batch, batch), batch), a * 2 * BS : (a + 1) * 2 * BS
+                pl.ds(pl.multiple_of(first, batch), batch), a * 2 * BS : (a + 1) * 2 * BS
             ] = jnp.where(live, jnp.where(low, even, odd), 0.0).astype(BF)
+
+    steps = capacity // batch
+
+    def body(i, carry):
+        first = i * 2 * batch
+        multiply(first, tiles_a)
+        multiply(first + batch, tiles_b)
+        flush(first, tiles_a)
+        flush(first + batch, tiles_b)
         return carry
 
-    lax.fori_loop(0, capacity // batch, body, 0)
-
-
-def owned_grads(tab, count, order, me, features, boths, capacity, rows, is_up):
-    groups = len(boths)
+    lax.fori_loop(0, steps // 2, body, 0)
+    if steps % 2:
+        multiply(capacity - batch, tiles_a)
+        flush(capacity - batch, tiles_a)
+
+
+def owned_grads(tab, count, order, me, features, hiddens, capacity, rows, is_up):
+    groups = len(hiddens)
     pieces = tuple(len(group) for group in features)
     batch = GROUP if capacity % GROUP == 0 else 8
     flat = [piece for group in features for piece in group]
-    tokens = boths[0].shape[1]
+    tokens = hiddens[0].shape[1]
     total = sum(piece.shape[0] for piece in features[0])
     small = groups * total * tokens <= 4 << 20
     smem = pl.BlockSpec(memory_space=SMEM)
     vmem = pl.BlockSpec(memory_space=VMEM)
     piece = vmem if small else pl.BlockSpec(memory_space=ANY)
-    scratch = [VMEM((groups, total, tokens), BF), VMEM((batch * PITCH, 2 * BS), F32)]
+    scratch = [VMEM((groups, total, tokens), BF)] + [VMEM((batch * PITCH, 2 * BS), F32)] * 2
     if not small:
         scratch.append(pltpu.SemaphoreType.DMA((len(flat),)))
     return pl.pallas_call(
@@ -379,7 +407,7 @@
         compiler_params=pltpu.CompilerParams(vmem_limit_bytes=(20 if small else 48) << 20),
         cost_estimate=COST,
         name="grads_up" if is_up else "grads_down",
-    )(tab, count, order, me, *flat, *boths)
+    )(tab, count, order, me, *flat, *hiddens)
 
 
 def per_device(inputs, cotangent, w_up, w_down, col_up, row_down, owner_up, owner_down):
@@ -390,7 +418,6 @@
     capacity = 5 * blocks // (4 * groups)
     me = lax.axis_index("mp").reshape(1)
     far = members // 4
-    half = members // 2
     after = lax.optimization_barrier
     others = range(1, groups)
 
@@ -398,71 +425,82 @@
     cot_xy = [swap_groups(cotangent, d, 2) for d in others]
     in_parts = [inputs] + [swap(inputs, "mp", 4 * z) for z in range(1, far)]
     up_w = relayout(w_up)
-    down_w = relayout(w_down)
-    in_parts, up_w, down_w, cot_x, cot_xy, cotangent = after(
-        (in_parts, up_w, down_w, cot_x, cot_xy, cotangent)
+    cot_parts = [cotangent, swap(cotangent, "mp", 4)]
+    in_parts, up_w, cot_x, cot_xy, cot_parts, cotangent = after(
+        (in_parts, up_w, cot_x, cot_xy, cot_parts, cotangent)
     )
     in_near = join(in_parts)
     in_far = swap(in_near, "mp", 2)
     in_near_o = [swap(in_near, "dp", d) for d in others]
     in_near_b = swap(in_near, "mp", 1)
-    cot_parts = [cotangent] + [swap(cotangent, "mp", 4 * z) for z in range(1, far)]
+    cot_parts += [swap(cotangent, "mp", 4 * z) for z in range(2, far)]
     cot_o = [join([x, xy]) for x, xy in zip(cot_x, cot_xy)]
+    in_near_b, cot_o = after((in_near_b, cot_o))
+    cot_o_1 = [swap(x, "mp", 4) for x in cot_o]
     (hidden,) = hidden_sum(
         rows, True, me, col_up, up_w, [in_near, in_near_b], [(0, 0), (1, 0)]
     )
-    cot_parts, hidden, cot_o, in_far, in_near_o = after(
-        (cot_parts, hidden, cot_o, in_far, in_near_o)
+    hidden, w_down, owner_up, owner_down = after((hidden, w_down, owner_up, owner_down))
+    down_w = relayout(w_down)
+    up_tab, down_tab, counts = slots(
+        lax.axis_index("dp").reshape(1), owner_up[:, 0], owner_down[:, 0]
+    )
+    cot_o, cot_o_1, in_near_o, cot_parts, in_far, hidden, down_w, up_tab = after(
+        (cot_o, cot_o_1, in_near_o, cot_parts, in_far, hidden, down_w, up_tab)
     )
     cot_near = join(cot_parts)
     cot_far = swap(cot_near, "mp", 2)
     cot_near_b = swap(cot_near, "mp", 1)
     in_far_b = swap(in_far, "mp", 1)
     in_far_o = [swap(in_far, "dp", d) for d in others]
-    cot_o_z = [[swap(x, "mp", 4 * z) for z in range(1, far)] for x in cot_o]
+    cot_o_z = [[swap(x, "mp", 4 * z) for z in range(2, far)] for x in cot_o]
     (upper,) = hidden_sum(
         rows, False, me, row_down, down_w, [cot_near, cot_near_b], [(0, 0), (1, 0)]
     )
-    (hidden,) = hidden_sum(
-        rows, True, me, col_up, up_w, [in_far, in_far_b], [(0, far), (1, far)], hidden
-    )
-    early = [x[: far // 2] for x in cot_o_z]
-    cot_far, hidden, upper, in_far_o, early = after((cot_far, hidden, upper, in_far_o, early))
+    active, slope = hidden_sum(
+        rows, True, me, col_up, up_w, [in_far, in_far_b], [(0, far), (1, far)], hidden, True
+    )
+    early = [x[: far // 2 - 1] for x in cot_o_z]
+    cot_far, slope, upper, in_far_o, early = after((cot_far, slope, upper, in_far_o, early))
     cot_far_b = swap(cot_far, "mp", 1)
     (upper,) = hidden_sum(rows, False, me, row_down, down_w, [cot_far], [(0, far)], upper)
-    both, active = hidden_sum(
-        rows, False, me, row_down, down_w, [cot_far_b], [(1, far)], upper, hidden
-    )
-    both_o = [swap(both, "dp", d) for d in others]
-
-    sent = input_grad_part(rows, 1, me, col_up, up_w, both, BF)
+    (slope_grad,) = hidden_sum(
+        rows, False, me, row_down, down_w, [cot_far_b], [(1, far)], upper, True,
+        slope,
+    )
+    slope_grad_o = [swap(slope_grad, "dp", d) for d in others]
+
+    part = functools.partial(input_grad_part, rows)
+    (sent,) = part(far, (1,), me, col_up, up_w, slope_grad)
     arrived = swap(sent, "mp", 1)
-    sent, both = after((sent, both))
-    terms = input_grad_part(rows, 0, me, col_up, up_w, both, F32)
-    terms, sent = add_and_split(terms, arrived, far * rows)
+    (terms,) = part(far, (0,), me, col_up, up_w, slope_grad)
+    (sent,) = add_and_split(terms, [arrived], 0)
     arrived = swap(sent, "mp", 2)
-    terms, owner_up, owner_down = after((terms, owner_up, owner_down))
-    up_tab, down_tab, counts = slots(
-        lax.axis_index("dp").reshape(1), owner_up[:, 0], owner_down[:, 0]
-    )
+    sent, near_slope_grad, near_active = after((sent, slope_grad, active))
+    active_o = [swap(near_active, "dp", d) for d in others]
+    sent_b, terms = part(0, (1, 0), me, col_up, up_w, near_slope_grad)
+    arrived_b = swap(sent_b, "mp", 1)
     in_near_o_b = [swap(x, "mp", 1) for x in in_near_o]
     in_far_o_b = [swap(x, "mp", 1) for x in in_far_o]
     in_all = [[in_near, in_far, in_near_b, in_far_b]]
     in_all += [list(x) for x in zip(in_near_o, in_far_o, in_near_o_b, in_far_o_b)]
-    both_all = [both] + both_o
-    grad_up = owned_grads(up_tab, counts, col_up, me, in_all, both_all, capacity, rows, True)
-    late = [x[far // 2 :] for x in cot_o_z]
-    arrived, late, grad_up = after((arrived, late, grad_up))
-    cot_o = [[x] + near + rest for x, near, rest in zip(cot_o, early, late)]
-    terms, *sent = add_and_split(terms, arrived, rows)
+    late = [x[far // 2 - 1 :] for x in cot_o_z]
+    arrived, late, slope_grad_o, terms = after((arrived, late, slope_grad_o, terms))
+    cot_o = [
+        [x, x_1] + near + rest for x, x_1, near, rest in zip(cot_o, cot_o_1, early, late)
+    ]
+    terms, *sent = add_and_split(terms, [arrived, arrived_b], rows)
     pieces = [swap(x, "mp", 4 * z + 4) for z, x in enumerate(sent)]
     cot_o_b = [[swap(piece, "mp", 1) for piece in x] for x in cot_o]
     cot_all = [[cot_near, cot_far, cot_near_b, cot_far_b]]
     cot_all += [x + x_b for x, x_b in zip(cot_o, cot_o_b)]
+    grad_up = owned_grads(
+        up_tab, counts, col_up, me, in_all, [slope_grad] + slope_grad_o, capacity, rows, True
+    )
     grad_down = owned_grads(
-        down_tab, counts, row_down, me, cot_all, both_all, capacity, rows, False
-    )
-    pieces, grad_down = after((pieces, grad_down))
+        down_tab, counts, row_down, me, cot_all, [active] + active_o, capacity, rows, False
+    )
+    pieces, grad_up, grad_down = after((pieces, grad_up, grad_down))
     return active, add_all(terms, pieces), grad_up, grad_down
 
 

time: 103 us -> 95.2 us (0.924)
  Pallas kernels: 43.9 us -> 35.8 us
    pallas_call x2, Pallas kernels: 16.7 us -> 10.6 us  [owned_grads(): pl.pallas_call(functools.partial(grads_kernel, groups, pieces, capacity,...]
    pallas_call x6, Pallas kernels: 4 us -> 2.05 us  [in_vmem(): pl.pallas_call(kernel, in_specs=[vmem] * len(args), out_specs=[vmem] * le...]
    unnamed x60 -> x32, local copies, waits for them, and re-layouts: 5.97 us -> 6.34 us
    ppermute x30 -> x32, starting transfers between devices: 31.5 us -> 31.6 us  [swap(): return lax.ppermute(value, axis, [(i, i ^ mask) for i in range(size)])]
    ppermute x30 -> x32, waiting for transfers between devices: 18.8 us -> 18.7 us  [swap(): return lax.ppermute(value, axis, [(i, i ^ mask) for i in range(size)])]
    pallas_call x2 -> x3, Pallas kernels: 4.44 us -> 4.42 us  [input_grad_part(): pl.pallas_call(functools.partial(input_grad_kernel, rows, skip, bits), in...]
  transfers between devices with their start and end apart: 31 -> 33, of which waited for: 7 -> 9; matrix products, arithmetic and copies ran while one was open for 0% -> 0% of each run, Pallas kernels for 37% -> 34%
where the time goes in v2:
time: 95.2 us; the launch traced here: 94.9 us
  Pallas kernels  35.8 us (38%)
  starting transfers between devices  33.1 us (35%)
  waiting for transfers between devices  18.7 us (20%)
  local copies, waits for them, and re-layouts  6.34 us (7%)
    ppermute x32, starting transfers between devices, swap(): return lax.ppermute(value, axis, [(i, i ^ mask) for i in range(size)])  31.6 us
    ppermute x32, waiting for transfers between devices, swap(): return lax.ppermute(value, axis, [(i, i ^ mask) for i in range(size)])  18.7 us
    pallas_call x5, Pallas kernels, hidden_sum(): pl.pallas_call(functools.partial(hidden_kernel, rows, is_up, tuple(starts...  13.4 us
    pallas_call x2, Pallas kernels, owned_grads(): pl.pallas_call(functools.partial(grads_kernel, groups, pieces, capacity,...  10.6 us
    unnamed x32, local copies, waits for them, and re-layouts  6.34 us
    pallas_call x3, Pallas kernels, input_grad_part(): pl.pallas_call(functools.partial(input_grad_kernel, rows, skip, bits), in...  4.42 us
    pallas_call x2, Pallas kernels, relayout(): pl.pallas_call(functools.partial(relayout_kernel, RELAYOUT), in_specs=[vm...  2.93 us
    pallas_call x1, Pallas kernels, slots(): pl.pallas_call(slots_kernel, in_specs=[spec] * 3, out_specs=[spec] * 3, o...  2.46 us
  transfers between devices with their start and end apart: 33, of which 9 were waited for; matrix products, arithmetic and copies ran while one was open for 0% of the time, Pallas kernels for 34%

profile of v2, /device:TPU:0, one launch (start us, length us, event | category | flops | bytes accessed | tf_op | source)
XLA Modules:
  0.0 94.9 jit_solution(10484250631165559582)
XLA Ops:
  0.6 3.1 %collective-permute-start = (bf16[512,128]{1,0:T(8,128)(2,1)}, bf16[512,128]{1,0:T(8,128)(2,1)S(1)}, u32[]{:S(2)}, u32[]{:S(2)}) collective-permute-start(bf16[512,128]{1,0:T(8,128)(2,1)} %refs_0_), channel_id=1, source_target_pairs={{0,4},{1,5},{2,6},{3,7},{4,0},{5,1},{6,2},{7,3},{8,12},{9,13},{10,... | collective-permute-start | bytes 393224 | tf_op jit(solution)/shard_map/ppermute | solution.py:26
  3.7 2.6 %collective-permute-start.1 = (bf16[512,128]{1,0:T(8,128)(2,1)}, bf16[512,128]{1,0:T(8,128)(2,1)S(1)}, u32[]{:S(2)}, u32[]{:S(2)}) collective-permute-start(bf16[512,128]{1,0:T(8,128)(2,1)} %refs_0_), channel_id=1, source_target_pairs={{0,8},{1,9},{2,10},{3,11},{4,12},{5,13},{6,14},{7,15},{8,0},{9,1},... | collective-permute-start | bytes 393224 | tf_op jit(solution)/shard_map/ppermute | solution.py:26
  6.3 1.7 %collective-permute-start.3 = (bf16[512,128]{1,0:T(8,128)(2,1)}, bf16[512,128]{1,0:T(8,128)(2,1)S(1)}, u32[]{:S(2)}, u32[]{:S(2)}) collective-permute-start(bf16[512,128]{1,0:T(8,128)(2,1)} %refs_0_.1), channel_id=1, source_target_pairs={{0,16},{16,0},{1,17},{17,1},{2,18},{18,2},{3,19},{19,3},{4,20},{20... | collective-permute-start | bytes 393224 | tf_op jit(solution)/shard_map/ppermute | solution.py:26
  8.0 1.5 %collective-permute-start.4 = (bf16[512,128]{1,0:T(8,128)(2,1)}, bf16[512,128]{1,0:T(8,128)(2,1)S(1)}, u32[]{:S(2)}, u32[]{:S(2)}) collective-permute-start(bf16[512,128]{1,0:T(8,128)(2,1)} %refs_0_.1), channel_id=1, source_target_pairs={{0,18},{1,19},{2,16},{3,17},{4,22},{5,23},{6,20},{7,21},{8,26},{9,... | collective-permute-start | bytes 393224 | tf_op jit(solution)/shard_map/ppermute | solution.py:36
  9.5 0.7 collective-permute-start.5
  10.2 1.6 %copy-done.2 = bf16[256,4096]{1,0:T(8,128)(2,1)S(1)} copy-done((bf16[256,4096]{1,0:T(8,128)(2,1)S(1)}, bf16[256,4096]{1,0:T(8,128)(2,1)}, u32[]{:S(2)}) %copy-start.2) | copy-done | bytes 2097176
  11.8 1.5 %relayout.2.refs_2_.w_ref = bf16[8192,128]{1,0:T(8,128)(2,1)S(1)} custom-call(bf16[256,4096]{1,0:T(8,128)(2,1)S(1)} %copy-done.2), custom_call_target="tpu_custom_call" | custom-call | flops 536870912 | bytes 6291456 | tf_op jit(solution)/shard_map/relayout/pallas_call | solution.py:62
  13.3 3.6 %collective-permute-done.1.refs_2_ = bf16[512,128]{1,0:T(8,128)(2,1)S(1)} collective-permute-done((bf16[512,128]{1,0:T(8,128)(2,1)}, bf16[512,128]{1,0:T(8,128)(2,1)S(1)}, u32[]{:S(2)}, u32[]{:S(2)}) %collective-permute-start.1) | collective-permute-done | bytes 131104 | tf_op jit(solution)/shard_map/ppermute | solution.py:26
  16.9 0.0 collective-permute-done.2.refs_3_
  16.9 0.4 collective-permute-done.5.refs_1_
  17.3 0.7 copy-done.9
  18.0 0.1 collective-permute-start.6
  18.1 1.4 %collective-permute-start.11 = (bf16[2048,128]{1,0:T(8,128)(2,1)S(1)}, bf16[2048,128]{1,0:T(8,128)(2,1)}, u32[]{:S(2)}, u32[]{:S(2)}) collective-permute-start(bf16[2048,128]{1,0:T(8,128)(2,1)S(1)} %join_parts.3.refs_3_.refs_4_), channel_id=1, source_target_pairs={{0,2},{1,3},{2,0},{3,1},{4,6},{5,7},{6,4},{7,5},{8,10},{9,11},{10,... | collective-permute-start | bytes 1572872 | tf_op jit(solution)/shard_map/ppermute | solution.py:26
  19.5 1.5 %collective-permute-start.8 = (bf16[2048,128]{1,0:T(8,128)(2,1)S(1)}, bf16[2048,128]{1,0:T(8,128)(2,1)}, u32[]{:S(2)}, u32[]{:S(2)}) collective-permute-start(bf16[2048,128]{1,0:T(8,128)(2,1)S(1)} %join_parts.3.refs_3_.refs_4_), channel_id=1, source_target_pairs={{0,16},{16,0},{1,17},{17,1},{2,18},{18,2},{3,19},{19,3},{4,20},{20... | collective-permute-start | bytes 1572872 | tf_op jit(solution)/shard_map/ppermute | solution.py:26
  21.0 0.0 collective-permute-done.6.refs_4_.refs_6_
  21.0 1.8 %collective-permute-start.7 = (bf16[1024,128]{1,0:T(8,128)(2,1)S(1)}, bf16[1024,128]{1,0:T(8,128)(2,1)}, u32[]{:S(2)}, u32[]{:S(2)}) collective-permute-start(bf16[1024,128]{1,0:T(8,128)(2,1)S(1)} %join_parts.4.refs_8_), channel_id=1, source_target_pairs={{0,4},{1,5},{2,6},{3,7},{4,0},{5,1},{6,2},{7,3},{8,12},{9,13},{10,... | collective-permute-start | bytes 786440 | tf_op jit(solution)/shard_map/ppermute | solution.py:26
  22.8 2.5 %collective-permute-start.10 = (bf16[512,128]{1,0:T(8,128)(2,1)S(1)}, bf16[512,128]{1,0:T(8,128)(2,1)}, u32[]{:S(2)}, u32[]{:S(2)}) collective-permute-start(bf16[512,128]{1,0:T(8,128)(2,1)S(1)} %copy-done.8), channel_id=1, source_target_pairs={{0,12},{1,13},{2,14},{3,15},{4,8},{5,9},{6,10},{7,11},{8,4},{9,5},... | collective-permute-start | bytes 393224 | tf_op jit(solution)/shard_map/ppermute | solution.py:26
  25.3 0.0 collective-permute-start.9
  25.3 3.0 %hidden.1.refs_5_ = f32[1024,128]{1,0:T(8,128)S(1)} custom-call(s32[1]{0:T(128)} %bitcast.refs_0_.me_ref.refs_3_, s32[256]{0:T(256)S(1)} %copy-done.11, bf16[8192,128]{1,0:T(8,128)(2,1)S(1)} %relayout.2.refs_2_.w_ref, bf16[2048,128]{1,0:T(8,128)(2,1)S(1)} %join_parts.3.refs_3_.refs_4_, bf16[2048,128]{1,0:T(8,128)(2,1)S(1)} %collective-permute-done.6.refs_4_.refs_6_), custom_call_target="tpu_custom_call" | custom-call | flops 536870912 | bytes 6291456 | tf_op jit(solution)/shard_map/hidden/pallas_call | solution.py:200
  28.3 0.0 copy-start.4
  28.3 0.8 copy-done.4
  29.1 1.5 %relayout.3.refs_2_ = bf16[8192,128]{1,0:T(8,128)(2,1)S(1)} custom-call(bf16[256,4096]{1,0:T(8,128)(2,1)S(1)} %copy-done.3), custom_call_target="tpu_custom_call" | custom-call | flops 536870912 | bytes 6291456 | tf_op jit(solution)/shard_map/relayout/pallas_call | solution.py:62
  30.6 1.3 %copy-done = bf16[8192,128]{1,0:T(8,128)(2,1)} copy-done((bf16[8192,128]{1,0:T(8,128)(2,1)}, bf16[8192,128]{1,0:T(8,128)(2,1)S(1)}, u32[]{:S(2)}) %copy-start) | copy-done | bytes 2097176
  31.9 2.5 %slots.1 = (s32[264]{0:T(512)}, s32[264]{0:T(512)}, s32[2]{0:T(128)}) custom-call(s32[1]{0:T(128)} %bitcast.1.me_ref, s32[256]{0:T(256)} %bitcast.4, s32[256]{0:T(256)} %bitcast.5), custom_call_target="tpu_custom_call" | custom-call | flops 536870912 | bytes 6291456 | tf_op jit(solution)/shard_map/slots/pallas_call | solution.py:97
  34.3 1.0 %collective-permute-done.10.refs_3_ = bf16[512,128]{1,0:T(8,128)(2,1)} collective-permute-done((bf16[512,128]{1,0:T(8,128)(2,1)S(1)}, bf16[512,128]{1,0:T(8,128)(2,1)}, u32[]{:S(2)}, u32[]{:S(2)}) %collective-permute-start.10) | collective-permute-done | bytes 131104 | tf_op jit(solution)/shard_map/ppermute | solution.py:26
  35.4 0.1 collective-permute-start.12
  35.5 0.0 copy-start.10
  35.5 0.9 copy-done.10
  36.4 1.0 %join_parts.5.refs_3_.refs_4_ = bf16[2048,128]{1,0:T(8,128)(2,1)S(1)} custom-call(bf16[512,128]{1,0:T(8,128)(2,1)S(1)} %copy-done.8, bf16[512,128]{1,0:T(8,128)(2,1)S(1)} %copy-done.10, bf16[512,128]{1,0:T(8,128)(2,1)} %collective-permute-done.9.refs_2_, bf16[512,128]{1,0:T(8,128)(2,1)} %collective-permute-done.10.refs_3_), custom_call_target="tpu_custom_call" | custom-call | flops 1000 | bytes 1048576 | tf_op jit(solution)/shard_map/join_parts/pallas_call | solution.py:253
  37.4 0.6 collective-permute-start.14
  38.0 0.5 collective-permute-start.13
  38.5 1.2 %collective-permute-start.15 = (bf16[2048,128]{1,0:T(8,128)(2,1)}, bf16[2048,128]{1,0:T(8,128)(2,1)S(1)}, u32[]{:S(2)}, u32[]{:S(2)}) collective-permute-start(bf16[2048,128]{1,0:T(8,128)(2,1)} %collective-permute-done.11.refs_3_.refs_5_), channel_id=1, source_target_pairs={{0,16},{16,0},{1,17},{17,1},{2,18},{18,2},{3,19},{19,3},{4,20},{20... | collective-permute-start | bytes 1572872 | tf_op jit(solution)/shard_map/ppermute | solution.py:26
  39.7 2.5 %collective-permute-start.16 = (bf16[1024,128]{1,0:T(8,128)(2,1)S(1)}, bf16[1024,128]{1,0:T(8,128)(2,1)S(1)}, u32[]{:S(2)}, u32[]{:S(2)}) collective-permute-start(bf16[1024,128]{1,0:T(8,128)(2,1)S(1)} %join_parts.4.refs_8_), channel_id=1, source_target_pairs={{0,8},{1,9},{2,10},{3,11},{4,12},{5,13},{6,14},{7,15},{8,0},{9,1},... | collective-permute-start | bytes 786440 | tf_op jit(solution)/shard_map/ppermute | solution.py:26
  42.2 1.0 %copy-done.5 = f32[1024,128]{1,0:T(8,128)S(1)} copy-done((f32[1024,128]{1,0:T(8,128)S(1)}, f32[1024,128]{1,0:T(8,128)}, u32[]{:S(2)}) %copy-start.5) | copy-done | bytes 524312
  43.2 4.6 %hidden_last.1 = (bf16[1024,128]{1,0:T(8,128)(2,1)}, f32[1024,128]{1,0:T(8,128)S(1)}) custom-call(s32[1]{0:T(128)} %bitcast.refs_0_.me_ref.refs_3_, s32[256]{0:T(256)S(1)} %copy-done.11, bf16[8192,128]{1,0:T(8,128)(2,1)S(1)} %relayout.2.refs_2_.w_ref, bf16[2048,128]{1,0:T(8,128)(2,1)} %collective-permute-done.11.refs_3_.refs_5_, ...), custom_call_target="tpu_custom_call" | custom-call | flops 536870912 | bytes 6291456 | tf_op jit(solution)/shard_map/hidden_last/pallas_call | solution.py:200
  47.9 2.6 %upper.2.refs_4_ = f32[1024,128]{1,0:T(8,128)S(1)} custom-call(s32[1]{0:T(128)} %bitcast.refs_0_.me_ref.refs_3_, s32[256]{0:T(256)S(1)} %copy-done.12, bf16[8192,128]{1,0:T(8,128)(2,1)S(1)} %copy-done.1, bf16[2048,128]{1,0:T(8,128)(2,1)S(1)} %join_parts.5.refs_3_.refs_4_, bf16[2048,128]{1,0:T(8,128)(2,1)S(1)} %collective-permute-done.14.refs_4_.refs_6_), custom_call_target="tpu_custom_call" | custom-call | flops 536870912 | bytes 6291456 | tf_op jit(solution)/shard_map/upper/pallas_call | solution.py:200
  50.4 3.5 %collective-permute-done.16.refs_10_ = bf16[1024,128]{1,0:T(8,128)(2,1)S(1)} collective-permute-done((bf16[1024,128]{1,0:T(8,128)(2,1)S(1)}, bf16[1024,128]{1,0:T(8,128)(2,1)S(1)}, u32[]{:S(2)}, u32[]{:S(2)}) %collective-permute-start.16) | collective-permute-done | bytes 262176 | tf_op jit(solution)/shard_map/ppermute | solution.py:26
  53.9 1.6 %upper.3.refs_4_ = f32[1024,128]{1,0:T(8,128)S(1)} custom-call(s32[1]{0:T(128)} %bitcast.refs_0_.me_ref.refs_3_, s32[256]{0:T(256)S(1)} %copy-done.12, bf16[8192,128]{1,0:T(8,128)(2,1)S(1)} %copy-done.1, bf16[2048,128]{1,0:T(8,128)(2,1)S(1)} %collective-permute-done.13.refs_3_.refs_5_, f32[1024,128]{1,0:T(8,128)S(1)} %upper.2.refs_4_), custom_call_target="tpu_custom_call" | custom-call | flops 536870912 | bytes 6291456 | tf_op jit(solution)/shard_map/upper/pallas_call | solution.py:200
  55.5 0.3 collective-permute-done.17.refs_3_.refs_7_
  55.8 1.7 %upper_last.1.s_ref.refs_12_ = bf16[1024,128]{1,0:T(8,128)(2,1)S(1)} custom-call(s32[1]{0:T(128)} %bitcast.refs_0_.me_ref.refs_3_, s32[256]{0:T(256)S(1)} %copy-done.12, bf16[8192,128]{1,0:T(8,128)(2,1)S(1)} %copy-done.1, bf16[2048,128]{1,0:T(8,128)(2,1)S(1)} %collective-permute-done.17.refs_3_.refs_7_, f32[1024,128]{1,0:T(8,128)S(1)} %upper.3.refs_4_, ...), custom_call_target="tpu_custom_call" | custom-call | flops 536870912 | bytes 6291456 | tf_op jit(solution)/shard_map/upper_last/pallas_call | solution.py:200
  57.5 1.4 %input_grad_part.4 = bf16[2048,128]{1,0:T(8,128)(2,1)S(1)} custom-call(s32[1]{0:T(128)} %bitcast.refs_0_.me_ref.refs_3_, s32[256]{0:T(256)S(1)} %copy-done.11, bf16[8192,128]{1,0:T(8,128)(2,1)S(1)} %relayout.2.refs_2_.w_ref, bf16[1024,128]{1,0:T(8,128)(2,1)S(1)} %upper_last.1.s_ref.refs_12_), custom_call_target="tpu_custom_call" | custom-call | flops 536870912 | bytes 6291456 | tf_op jit(solution)/shard_map/input_grad_part/pallas_call | solution.py:240
  58.9 0.3 collective-permute-start.18
  59.2 3.4 %collective-permute-start.20 = (bf16[1024,128]{1,0:T(8,128)(2,1)S(1)}, bf16[1024,128]{1,0:T(8,128)(2,1)S(1)}, u32[]{:S(2)}, u32[]{:S(2)}) collective-permute-start(bf16[1024,128]{1,0:T(8,128)(2,1)S(1)} %join_parts.4.refs_8_), channel_id=1, source_target_pairs={{0,12},{1,13},{2,14},{3,15},{4,8},{5,9},{6,10},{7,11},{8,4},{9,5},... | collective-permute-start | bytes 786440 | tf_op jit(solution)/shard_map/ppermute | solution.py:26
  62.6 1.4 %input_grad_part.3.terms_ref = f32[2048,128]{1,0:T(8,128)S(1)} custom-call(s32[1]{0:T(128)} %bitcast.refs_0_.me_ref.refs_3_, s32[256]{0:T(256)S(1)} %copy-done.11, bf16[8192,128]{1,0:T(8,128)(2,1)S(1)} %relayout.2.refs_2_.w_ref, bf16[1024,128]{1,0:T(8,128)(2,1)S(1)} %upper_last.1.s_ref.refs_12_), custom_call_target="tpu_custom_call" | custom-call | flops 536870912 | bytes 6291456 | tf_op jit(solution)/shard_map/input_grad_part/pallas_call | solution.py:240
  64.0 0.0 copy-start.6
  64.0 0.1 add_stage.2
  64.1 0.7 collective-permute-start.19
  64.9 1.4 %collective-permute-start.21 = (bf16[1024,128]{1,0:T(8,128)(2,1)S(1)}, bf16[1024,128]{1,0:T(8,128)(2,1)S(1)}, u32[]{:S(2)}, u32[]{:S(2)}) collective-permute-start(bf16[1024,128]{1,0:T(8,128)(2,1)S(1)} %upper_last.1.s_ref.refs_12_), channel_id=1, source_target_pairs={{0,16},{16,0},{1,17},{17,1},{2,18},{18,2},{3,19},{19,3},{4,20},{20... | collective-permute-start | bytes 786440 | tf_op jit(solution)/shard_map/ppermute | solution.py:26
  66.3 1.6 %input_grad_part.5 = (bf16[2048,128]{1,0:T(8,128)(2,1)S(1)}, f32[2048,128]{1,0:T(8,128)S(1)}) custom-call(s32[1]{0:T(128)} %bitcast.refs_0_.me_ref.refs_3_, s32[256]{0:T(256)S(1)} %copy-done.11, bf16[8192,128]{1,0:T(8,128)(2,1)S(1)} %relayout.2.refs_2_.w_ref, bf16[1024,128]{1,0:T(8,128)(2,1)S(1)} %upper_last.1.s_ref.refs_12_), custom_call_target="tpu_custom_call" | custom-call | flops 536870912 | bytes 6291456 | tf_op jit(solution)/shard_map/input_grad_part/pallas_call | solution.py:240
  67.9 0.3 collective-permute-start.22
  68.2 1.4 %collective-permute-done.20.refs_11_ = bf16[1024,128]{1,0:T(8,128)(2,1)S(1)} collective-permute-done((bf16[1024,128]{1,0:T(8,128)(2,1)S(1)}, bf16[1024,128]{1,0:T(8,128)(2,1)S(1)}, u32[]{:S(2)}, u32[]{:S(2)}) %collective-permute-start.20) | collective-permute-done | bytes 262176 | tf_op jit(solution)/shard_map/ppermute | solution.py:26
  69.6 0.5 collective-permute-start.27
  70.1 3.4 %collective-permute-done.21.refs_13_ = bf16[1024,128]{1,0:T(8,128)(2,1)S(1)} collective-permute-done((bf16[1024,128]{1,0:T(8,128)(2,1)S(1)}, bf16[1024,128]{1,0:T(8,128)(2,1)S(1)}, u32[]{:S(2)}, u32[]{:S(2)}) %collective-permute-start.21) | collective-permute-done | bytes 262176 | tf_op jit(solution)/shard_map/ppermute | solution.py:26
  73.6 4.5 %collective-permute-done.19.refs_0_ = bf16[2048,128]{1,0:T(8,128)(2,1)S(1)} collective-permute-done((bf16[2048,128]{1,0:T(8,128)(2,1)S(1)}, bf16[2048,128]{1,0:T(8,128)(2,1)S(1)}, u32[]{:S(2)}, u32[]{:S(2)}) %collective-permute-start.19) | collective-permute-done | bytes 524320 | tf_op jit(solution)/shard_map/ppermute | solution.py:26
  78.1 0.7 collective-permute-start.32
  78.7 0.2 collective-permute-start.31
  78.9 0.2 add_stage.3
  79.1 0.1 collective-permute-start.23
  79.2 0.4 collective-permute-done.30.refs_14_
  79.6 0.7 collective-permute-start.24
  80.3 3.2 %collective-permute-start.25 = (bf16[512,128]{1,0:T(8,128)(2,1)S(1)}, bf16[512,128]{1,0:T(8,128)(2,1)S(1)}, u32[]{:S(2)}, u32[]{:S(2)}) collective-permute-start(bf16[512,128]{1,0:T(8,128)(2,1)S(1)} %get-tuple-element.96), channel_id=1, source_target_pairs={{0,12},{1,13},{2,14},{3,15},{4,8},{5,9},{6,10},{7,11},{8,4},{9,5},... | collective-permute-start | bytes 393224 | tf_op jit(solution)/shard_map/ppermute | solution.py:26
  83.5 5.3 %grads_up.1 = bf16[160,4096]{1,0:T(8,128)(2,1)} custom-call(s32[264]{0:T(512)S(1)} %copy-done.14, s32[2]{0:T(128)S(1)} %copy-done.15, s32[256]{0:T(256)S(1)} %copy-done.11, s32[1]{0:T(128)} %bitcast.refs_0_.me_ref.refs_3_, bf16[2048,128]{1,0:T(8,128)(2,1)S(1)} %join_parts.3.refs_3_.refs_4_, bf16[2048,128]{1,0:T(8,128)(2,1)} %collective-permute-done.11.refs_3_.refs_5_, ...), custom_call_target="tpu_custom_call" | custom-call | flops 536870912 | bytes 6291456 | tf_op jit(solution)/shard_map/grads_up/pallas_call | solution.py:401
  88.8 5.3 %grads_down.1 = bf16[160,4096]{1,0:T(8,128)(2,1)} custom-call(s32[264]{0:T(512)S(1)} %copy-done.13, s32[2]{0:T(128)S(1)} %copy-done.15, s32[256]{0:T(256)S(1)} %copy-done.12, s32[1]{0:T(128)} %bitcast.refs_0_.me_ref.refs_3_, bf16[2048,128]{1,0:T(8,128)(2,1)S(1)} %join_parts.5.refs_3_.refs_4_, bf16[2048,128]{1,0:T(8,128)(2,1)S(1)} %collective-permute-done.13.refs_3_.refs_5_, ...), custom_call_target="tpu_custom_call" | custom-call | flops 536870912 | bytes 6291456 | tf_op jit(solution)/shard_map/grads_down/pallas_call | solution.py:401
  94.2 0.7 add_last.1
  (53 shorter events, 0.2 us)
Async XLA Ops:
  0.6 8.9 %collective-permute-start = (bf16[512,128]{1,0:T(8,128)(2,1)}, bf16[512,128]{1,0:T(8,128)(2,1)S(1)}, u32[]{:S(2)}, u32[]{:S(2)}) collective-permute-start(bf16[512,128]{1,0:T(8,128)(2,1)} %refs_0_), channel_id=1, source_target_pairs={{0,4},{1,5},{2,6},{3,7},{4,0},{5,1},{6,2},{7,3},{8,12},{9,13},{10,... | collective-permute-start | bytes 393224 | tf_op jit(solution)/shard_map/ppermute | solution.py:26
  3.7 13.2 %collective-permute-start.1 = (bf16[512,128]{1,0:T(8,128)(2,1)}, bf16[512,128]{1,0:T(8,128)(2,1)S(1)}, u32[]{:S(2)}, u32[]{:S(2)}) collective-permute-start(bf16[512,128]{1,0:T(8,128)(2,1)} %refs_0_), channel_id=1, source_target_pairs={{0,8},{1,9},{2,10},{3,11},{4,12},{5,13},{6,14},{7,15},{8,0},{9,1},... | collective-permute-start | bytes 393224 | tf_op jit(solution)/shard_map/ppermute | solution.py:26
  6.3 10.6 %collective-permute-start.2 = (bf16[512,128]{1,0:T(8,128)(2,1)}, bf16[512,128]{1,0:T(8,128)(2,1)S(1)}, u32[]{:S(2)}, u32[]{:S(2)}) collective-permute-start(bf16[512,128]{1,0:T(8,128)(2,1)} %refs_0_), channel_id=1, source_target_pairs={{0,12},{1,13},{2,14},{3,15},{4,8},{5,9},{6,10},{7,11},{8,4},{9,5},... | collective-permute-start | bytes 393224 | tf_op jit(solution)/shard_map/ppermute | solution.py:26
  6.3 10.6 %collective-permute-start.3 = (bf16[512,128]{1,0:T(8,128)(2,1)}, bf16[512,128]{1,0:T(8,128)(2,1)S(1)}, u32[]{:S(2)}, u32[]{:S(2)}) collective-permute-start(bf16[512,128]{1,0:T(8,128)(2,1)} %refs_0_.1), channel_id=1, source_target_pairs={{0,16},{16,0},{1,17},{17,1},{2,18},{18,2},{3,19},{19,3},{4,20},{20... | collective-permute-start | bytes 393224 | tf_op jit(solution)/shard_map/ppermute | solution.py:26
  8.0 8.9 %collective-permute-start.4 = (bf16[512,128]{1,0:T(8,128)(2,1)}, bf16[512,128]{1,0:T(8,128)(2,1)S(1)}, u32[]{:S(2)}, u32[]{:S(2)}) collective-permute-start(bf16[512,128]{1,0:T(8,128)(2,1)} %refs_0_.1), channel_id=1, source_target_pairs={{0,18},{1,19},{2,16},{3,17},{4,22},{5,23},{6,20},{7,21},{8,26},{9,... | collective-permute-start | bytes 393224 | tf_op jit(solution)/shard_map/ppermute | solution.py:36
  9.5 7.8 %collective-permute-start.5 = (bf16[512,128]{1,0:T(8,128)(2,1)}, bf16[512,128]{1,0:T(8,128)(2,1)S(1)}, u32[]{:S(2)}, u32[]{:S(2)}) collective-permute-start(bf16[512,128]{1,0:T(8,128)(2,1)} %refs_0_.1), channel_id=1, source_target_pairs={{0,4},{1,5},{2,6},{3,7},{4,0},{5,1},{6,2},{7,3},{8,12},{9,13},{10,... | collective-permute-start | bytes 393224 | tf_op jit(solution)/shard_map/ppermute | solution.py:26
  10.2 1.6 %copy-start.2 = (bf16[256,4096]{1,0:T(8,128)(2,1)S(1)}, bf16[256,4096]{1,0:T(8,128)(2,1)}, u32[]{:S(2)}) copy-start(bf16[256,4096]{1,0:T(8,128)(2,1)} %src.1) | copy-start | bytes 6291460
  11.8 6.2 %copy-start.7 = (bf16[512,128]{1,0:T(8,128)(2,1)S(1)}, bf16[512,128]{1,0:T(8,128)(2,1)}, u32[]{:S(2)}) copy-start(bf16[512,128]{1,0:T(8,128)(2,1)} %refs_0_) | copy-start | bytes 393220
  11.8 11.0 %copy-start.8 = (bf16[512,128]{1,0:T(8,128)(2,1)S(1)}, bf16[512,128]{1,0:T(8,128)(2,1)}, u32[]{:S(2)}) copy-start(bf16[512,128]{1,0:T(8,128)(2,1)} %refs_0_.1) | copy-start | bytes 393220
  11.8 13.5 %copy-start.11 = (s32[256]{0:T(256)S(1)}, s32[256]{0:T(256)}, u32[]{:S(2)}) copy-start(s32[256]{0:T(256)} %refs_2_.2) | copy-start | bytes 3076
  17.3 0.7 copy-start.9
  18.0 3.0 %collective-permute-start.6 = (bf16[2048,128]{1,0:T(8,128)(2,1)S(1)}, bf16[2048,128]{1,0:T(8,128)(2,1)S(1)}, u32[]{:S(2)}, u32[]{:S(2)}) collective-permute-start(bf16[2048,128]{1,0:T(8,128)(2,1)S(1)} %join_parts.3.refs_3_.refs_4_), channel_id=1, source_target_pairs={{0,1},{1,0},{2,3},{3,2},{4,5},{5,4},{6,7},{7,6},{8,9},{9,8},{10,11... | collective-permute-start | bytes 1572872 | tf_op jit(solution)/shard_map/ppermute | solution.py:26
  18.1 17.3 %collective-permute-start.11 = (bf16[2048,128]{1,0:T(8,128)(2,1)S(1)}, bf16[2048,128]{1,0:T(8,128)(2,1)}, u32[]{:S(2)}, u32[]{:S(2)}) collective-permute-start(bf16[2048,128]{1,0:T(8,128)(2,1)S(1)} %join_parts.3.refs_3_.refs_4_), channel_id=1, source_target_pairs={{0,2},{1,3},{2,0},{3,1},{4,6},{5,7},{6,4},{7,5},{8,10},{9,11},{10,... | collective-permute-start | bytes 1572872 | tf_op jit(solution)/shard_map/ppermute | solution.py:26
  19.5 15.9 %collective-permute-start.8 = (bf16[2048,128]{1,0:T(8,128)(2,1)S(1)}, bf16[2048,128]{1,0:T(8,128)(2,1)}, u32[]{:S(2)}, u32[]{:S(2)}) collective-permute-start(bf16[2048,128]{1,0:T(8,128)(2,1)S(1)} %join_parts.3.refs_3_.refs_4_), channel_id=1, source_target_pairs={{0,16},{16,0},{1,17},{17,1},{2,18},{18,2},{3,19},{19,3},{4,20},{20... | collective-permute-start | bytes 1572872 | tf_op jit(solution)/shard_map/ppermute | solution.py:26
  21.0 14.4 %collective-permute-start.7 = (bf16[1024,128]{1,0:T(8,128)(2,1)S(1)}, bf16[1024,128]{1,0:T(8,128)(2,1)}, u32[]{:S(2)}, u32[]{:S(2)}) collective-permute-start(bf16[1024,128]{1,0:T(8,128)(2,1)S(1)} %join_parts.4.refs_8_), channel_id=1, source_target_pairs={{0,4},{1,5},{2,6},{3,7},{4,0},{5,1},{6,2},{7,3},{8,12},{9,13},{10,... | collective-permute-start | bytes 786440 | tf_op jit(solution)/shard_map/ppermute | solution.py:26
  22.8 6.3 %copy-start.3 = (bf16[256,4096]{1,0:T(8,128)(2,1)S(1)}, bf16[256,4096]{1,0:T(8,128)(2,1)}, u32[]{:S(2)}) copy-start(bf16[256,4096]{1,0:T(8,128)(2,1)} %src.2) | copy-start | bytes 6291460
  22.8 12.6 %collective-permute-start.10 = (bf16[512,128]{1,0:T(8,128)(2,1)S(1)}, bf16[512,128]{1,0:T(8,128)(2,1)}, u32[]{:S(2)}, u32[]{:S(2)}) collective-permute-start(bf16[512,128]{1,0:T(8,128)(2,1)S(1)} %copy-done.8), channel_id=1, source_target_pairs={{0,12},{1,13},{2,14},{3,15},{4,8},{5,9},{6,10},{7,11},{8,4},{9,5},... | collective-permute-start | bytes 393224 | tf_op jit(solution)/shard_map/ppermute | solution.py:26
  25.3 10.1 %collective-permute-start.9 = (bf16[512,128]{1,0:T(8,128)(2,1)S(1)}, bf16[512,128]{1,0:T(8,128)(2,1)}, u32[]{:S(2)}, u32[]{:S(2)}) collective-permute-start(bf16[512,128]{1,0:T(8,128)(2,1)S(1)} %copy-done.8), channel_id=1, source_target_pairs={{0,8},{1,9},{2,10},{3,11},{4,12},{5,13},{6,14},{7,15},{8,0},{9,1},... | collective-permute-start | bytes 393224 | tf_op jit(solution)/shard_map/ppermute | solution.py:26
  28.3 0.8 copy-start.4
  30.5 1.3 %copy-start = (bf16[8192,128]{1,0:T(8,128)(2,1)}, bf16[8192,128]{1,0:T(8,128)(2,1)S(1)}, u32[]{:S(2)}) copy-start(bf16[8192,128]{1,0:T(8,128)(2,1)S(1)} %relayout.3.refs_2_) | copy-start | bytes 6291460
  35.4 6.8 %collective-permute-start.12 = (bf16[2048,128]{1,0:T(8,128)(2,1)}, bf16[2048,128]{1,0:T(8,128)(2,1)S(1)}, u32[]{:S(2)}, u32[]{:S(2)}) collective-permute-start(bf16[2048,128]{1,0:T(8,128)(2,1)} %collective-permute-done.11.refs_3_.refs_5_), channel_id=1, source_target_pairs={{0,1},{1,0},{2,3},{3,2},{4,5},{5,4},{6,7},{7,6},{8,9},{9,8},{10,11... | collective-permute-start | bytes 1572872 | tf_op jit(solution)/shard_map/ppermute | solution.py:26
  35.5 0.9 copy-start.10
  36.4 11.5 %copy-start.12 = (s32[256]{0:T(256)S(1)}, s32[256]{0:T(256)}, u32[]{:S(2)}) copy-start(s32[256]{0:T(256)} %refs_2_.3) | copy-start | bytes 3076
  37.4 10.5 %copy-start.1 = (bf16[8192,128]{1,0:T(8,128)(2,1)S(1)}, bf16[8192,128]{1,0:T(8,128)(2,1)}, u32[]{:S(2)}) copy-start(bf16[8192,128]{1,0:T(8,128)(2,1)} %copy-done) | copy-start | bytes 6291460
  37.4 10.5 %collective-permute-start.14 = (bf16[2048,128]{1,0:T(8,128)(2,1)S(1)}, bf16[2048,128]{1,0:T(8,128)(2,1)S(1)}, u32[]{:S(2)}, u32[]{:S(2)}) collective-permute-start(bf16[2048,128]{1,0:T(8,128)(2,1)S(1)} %join_parts.5.refs_3_.refs_4_), channel_id=1, source_target_pairs={{0,1},{1,0},{2,3},{3,2},{4,5},{5,4},{6,7},{7,6},{8,9},{9,8},{10,11... | collective-permute-start | bytes 1572872 | tf_op jit(solution)/shard_map/ppermute | solution.py:26
  38.0 15.9 %collective-permute-start.13 = (bf16[2048,128]{1,0:T(8,128)(2,1)S(1)}, bf16[2048,128]{1,0:T(8,128)(2,1)S(1)}, u32[]{:S(2)}, u32[]{:S(2)}) collective-permute-start(bf16[2048,128]{1,0:T(8,128)(2,1)S(1)} %join_parts.5.refs_3_.refs_4_), channel_id=1, source_target_pairs={{0,2},{1,3},{2,0},{3,1},{4,6},{5,7},{6,4},{7,5},{8,10},{9,11},{10,... | collective-permute-start | bytes 1572872 | tf_op jit(solution)/shard_map/ppermute | solution.py:26
  38.5 15.4 %collective-permute-start.15 = (bf16[2048,128]{1,0:T(8,128)(2,1)}, bf16[2048,128]{1,0:T(8,128)(2,1)S(1)}, u32[]{:S(2)}, u32[]{:S(2)}) collective-permute-start(bf16[2048,128]{1,0:T(8,128)(2,1)} %collective-permute-done.11.refs_3_.refs_5_), channel_id=1, source_target_pairs={{0,16},{16,0},{1,17},{17,1},{2,18},{18,2},{3,19},{19,3},{4,20},{20... | collective-permute-start | bytes 1572872 | tf_op jit(solution)/shard_map/ppermute | solution.py:26
  39.7 14.2 %collective-permute-start.16 = (bf16[1024,128]{1,0:T(8,128)(2,1)S(1)}, bf16[1024,128]{1,0:T(8,128)(2,1)S(1)}, u32[]{:S(2)}, u32[]{:S(2)}) collective-permute-start(bf16[1024,128]{1,0:T(8,128)(2,1)S(1)} %join_parts.4.refs_8_), channel_id=1, source_target_pairs={{0,8},{1,9},{2,10},{3,11},{4,12},{5,13},{6,14},{7,15},{8,0},{9,1},... | collective-permute-start | bytes 786440 | tf_op jit(solution)/shard_map/ppermute | solution.py:26
  42.2 1.0 %copy-start.5 = (f32[1024,128]{1,0:T(8,128)S(1)}, f32[1024,128]{1,0:T(8,128)}, u32[]{:S(2)}) copy-start(f32[1024,128]{1,0:T(8,128)} %copy-done.4) | copy-start | bytes 1572868
  53.9 1.9 %collective-permute-start.17 = (bf16[2048,128]{1,0:T(8,128)(2,1)S(1)}, bf16[2048,128]{1,0:T(8,128)(2,1)S(1)}, u32[]{:S(2)}, u32[]{:S(2)}) collective-permute-start(bf16[2048,128]{1,0:T(8,128)(2,1)S(1)} %collective-permute-done.13.refs_3_.refs_5_), channel_id=1, source_target_pairs={{0,1},{1,0},{2,3},{3,2},{4,5},{5,4},{6,7},{7,6},{8,9},{9,8},{10,11... | collective-permute-start | bytes 1572872 | tf_op jit(solution)/shard_map/ppermute | solution.py:26
  58.9 5.1 %collective-permute-start.18 = (bf16[2048,128]{1,0:T(8,128)(2,1)S(1)}, bf16[2048,128]{1,0:T(8,128)(2,1)S(1)}, u32[]{:S(2)}, u32[]{:S(2)}) collective-permute-start(bf16[2048,128]{1,0:T(8,128)(2,1)S(1)} %input_grad_part.4), channel_id=1, source_target_pairs={{0,1},{1,0},{2,3},{3,2},{4,5},{5,4},{6,7},{7,6},{8,9},{9,8},{10,11... | collective-permute-start | bytes 1572872 | tf_op jit(solution)/shard_map/ppermute | solution.py:26
  59.2 10.4 %collective-permute-start.20 = (bf16[1024,128]{1,0:T(8,128)(2,1)S(1)}, bf16[1024,128]{1,0:T(8,128)(2,1)S(1)}, u32[]{:S(2)}, u32[]{:S(2)}) collective-permute-start(bf16[1024,128]{1,0:T(8,128)(2,1)S(1)} %join_parts.4.refs_8_), channel_id=1, source_target_pairs={{0,12},{1,13},{2,14},{3,15},{4,8},{5,9},{6,10},{7,11},{8,4},{9,5},... | collective-permute-start | bytes 786440 | tf_op jit(solution)/shard_map/ppermute | solution.py:26
  64.0 14.1 %copy-start.6 = (bf16[1024,128]{1,0:T(8,128)(2,1)S(1)}, bf16[1024,128]{1,0:T(8,128)(2,1)}, u32[]{:S(2)}) copy-start(bf16[1024,128]{1,0:T(8,128)(2,1)} %get-tuple-element.106.refs_16_) | copy-start | bytes 786436
  64.1 13.9 %collective-permute-start.19 = (bf16[2048,128]{1,0:T(8,128)(2,1)S(1)}, bf16[2048,128]{1,0:T(8,128)(2,1)S(1)}, u32[]{:S(2)}, u32[]{:S(2)}) collective-permute-start(bf16[2048,128]{1,0:T(8,128)(2,1)S(1)} %add_stage.2), channel_id=1, source_target_pairs={{0,2},{1,3},{2,0},{3,1},{4,6},{5,7},{6,4},{7,5},{8,10},{9,11},{10,... | collective-permute-start | bytes 1572872 | tf_op jit(solution)/shard_map/ppermute | solution.py:26
  64.9 4.8 %collective-permute-start.28 = (bf16[1024,128]{1,0:T(8,128)(2,1)S(1)}, bf16[1024,128]{1,0:T(8,128)(2,1)S(1)}, u32[]{:S(2)}, u32[]{:S(2)}) collective-permute-start(bf16[1024,128]{1,0:T(8,128)(2,1)S(1)} %join_parts.4.refs_8_), channel_id=1, source_target_pairs={{0,1},{1,0},{2,3},{3,2},{4,5},{5,4},{6,7},{7,6},{8,9},{9,8},{10,11... | collective-permute-start | bytes 786440 | tf_op jit(solution)/shard_map/ppermute | solution.py:26
  64.9 8.7 %collective-permute-start.21 = (bf16[1024,128]{1,0:T(8,128)(2,1)S(1)}, bf16[1024,128]{1,0:T(8,128)(2,1)S(1)}, u32[]{:S(2)}, u32[]{:S(2)}) collective-permute-start(bf16[1024,128]{1,0:T(8,128)(2,1)S(1)} %upper_last.1.s_ref.refs_12_), channel_id=1, source_target_pairs={{0,16},{16,0},{1,17},{17,1},{2,18},{18,2},{3,19},{19,3},{4,20},{20... | collective-permute-start | bytes 786440 | tf_op jit(solution)/shard_map/ppermute | solution.py:26
  66.3 17.3 %copy-start.14 = (s32[264]{0:T(512)S(1)}, s32[264]{0:T(512)}, u32[]{:S(2)}) copy-start(s32[264]{0:T(512)} %get-tuple-element.97.refs_0_) | copy-start | bytes 3172
  66.3 17.3 %copy-start.15 = (s32[2]{0:T(128)S(1)}, s32[2]{0:T(128)}, u32[]{:S(2)}) copy-start(s32[2]{0:T(128)} %get-tuple-element.98.refs_1_) | copy-start | bytes 28
  67.9 10.8 %collective-permute-start.22 = (bf16[2048,128]{1,0:T(8,128)(2,1)S(1)}, bf16[2048,128]{1,0:T(8,128)(2,1)S(1)}, u32[]{:S(2)}, u32[]{:S(2)}) collective-permute-start(bf16[2048,128]{1,0:T(8,128)(2,1)S(1)} %get-tuple-element.92), channel_id=1, source_target_pairs={{0,1},{1,0},{2,3},{3,2},{4,5},{5,4},{6,7},{7,6},{8,9},{9,8},{10,11... | collective-permute-start | bytes 1572872 | tf_op jit(solution)/shard_map/ppermute | solution.py:26
  69.6 9.4 %collective-permute-start.26 = (bf16[2048,128]{1,0:T(8,128)(2,1)}, bf16[2048,128]{1,0:T(8,128)(2,1)S(1)}, u32[]{:S(2)}, u32[]{:S(2)}) collective-permute-start(bf16[2048,128]{1,0:T(8,128)(2,1)} %collective-permute-done.8.refs_8_), channel_id=1, source_target_pairs={{0,1},{1,0},{2,3},{3,2},{4,5},{5,4},{6,7},{7,6},{8,9},{9,8},{10,11... | collective-permute-start | bytes 1572872 | tf_op jit(solution)/shard_map/ppermute | solution.py:26
  69.6 10.7 %collective-permute-start.27 = (bf16[2048,128]{1,0:T(8,128)(2,1)S(1)}, bf16[2048,128]{1,0:T(8,128)(2,1)S(1)}, u32[]{:S(2)}, u32[]{:S(2)}) collective-permute-start(bf16[2048,128]{1,0:T(8,128)(2,1)S(1)} %collective-permute-done.15.refs_9_), channel_id=1, source_target_pairs={{0,1},{1,0},{2,3},{3,2},{4,5},{5,4},{6,7},{7,6},{8,9},{9,8},{10,11... | collective-permute-start | bytes 1572872 | tf_op jit(solution)/shard_map/ppermute | solution.py:26
  73.6 4.5 %collective-permute-start.29 = (bf16[1024,128]{1,0:T(8,128)(2,1)}, bf16[1024,128]{1,0:T(8,128)(2,1)S(1)}, u32[]{:S(2)}, u32[]{:S(2)}) collective-permute-start(bf16[1024,128]{1,0:T(8,128)(2,1)} %collective-permute-done.7.refs_9_), channel_id=1, source_target_pairs={{0,1},{1,0},{2,3},{3,2},{4,5},{5,4},{6,7},{7,6},{8,9},{9,8},{10,11... | collective-permute-start | bytes 786440 | tf_op jit(solution)/shard_map/ppermute | solution.py:26
  78.1 1.5 %collective-permute-start.30 = (bf16[1024,128]{1,0:T(8,128)(2,1)S(1)}, bf16[1024,128]{1,0:T(8,128)(2,1)S(1)}, u32[]{:S(2)}, u32[]{:S(2)}) collective-permute-start(bf16[1024,128]{1,0:T(8,128)(2,1)S(1)} %collective-permute-done.16.refs_10_), channel_id=1, source_target_pairs={{0,1},{1,0},{2,3},{3,2},{4,5},{5,4},{6,7},{7,6},{8,9},{9,8},{10,11... | collective-permute-start | bytes 786440 | tf_op jit(solution)/shard_map/ppermute | solution.py:26
  78.1 10.8 %collective-permute-start.32 = (bf16[1024,128]{1,0:T(8,128)(2,1)S(1)}, bf16[1024,128]{1,0:T(8,128)(2,1)S(1)}, u32[]{:S(2)}, u32[]{:S(2)}) collective-permute-start(bf16[1024,128]{1,0:T(8,128)(2,1)S(1)} %copy-done.6), channel_id=1, source_target_pairs={{0,16},{16,0},{1,17},{17,1},{2,18},{18,2},{3,19},{19,3},{4,20},{20... | collective-permute-start | bytes 786440 | tf_op jit(solution)/shard_map/ppermute | solution.py:26
  78.7 10.1 %collective-permute-start.31 = (bf16[1024,128]{1,0:T(8,128)(2,1)S(1)}, bf16[1024,128]{1,0:T(8,128)(2,1)S(1)}, u32[]{:S(2)}, u32[]{:S(2)}) collective-permute-start(bf16[1024,128]{1,0:T(8,128)(2,1)S(1)} %collective-permute-done.20.refs_11_), channel_id=1, source_target_pairs={{0,1},{1,0},{2,3},{3,2},{4,5},{5,4},{6,7},{7,6},{8,9},{9,8},{10,11... | collective-permute-start | bytes 786440 | tf_op jit(solution)/shard_map/ppermute | solution.py:26
  79.1 15.1 %collective-permute-start.23 = (bf16[512,128]{1,0:T(8,128)(2,1)S(1)}, bf16[512,128]{1,0:T(8,128)(2,1)S(1)}, u32[]{:S(2)}, u32[]{:S(2)}) collective-permute-start(bf16[512,128]{1,0:T(8,128)(2,1)S(1)} %get-tuple-element.94), channel_id=1, source_target_pairs={{0,4},{1,5},{2,6},{3,7},{4,0},{5,1},{6,2},{7,3},{8,12},{9,13},{10,... | collective-permute-start | bytes 393224 | tf_op jit(solution)/shard_map/ppermute | solution.py:26
  79.6 14.6 %collective-permute-start.24 = (bf16[512,128]{1,0:T(8,128)(2,1)S(1)}, bf16[512,128]{1,0:T(8,128)(2,1)S(1)}, u32[]{:S(2)}, u32[]{:S(2)}) collective-permute-start(bf16[512,128]{1,0:T(8,128)(2,1)S(1)} %get-tuple-element.95), channel_id=1, source_target_pairs={{0,8},{1,9},{2,10},{3,11},{4,12},{5,13},{6,14},{7,15},{8,0},{9,1},... | collective-permute-start | bytes 393224 | tf_op jit(solution)/shard_map/ppermute | solution.py:26
  80.3 13.8 %collective-permute-start.25 = (bf16[512,128]{1,0:T(8,128)(2,1)S(1)}, bf16[512,128]{1,0:T(8,128)(2,1)S(1)}, u32[]{:S(2)}, u32[]{:S(2)}) collective-permute-start(bf16[512,128]{1,0:T(8,128)(2,1)S(1)} %get-tuple-element.96), channel_id=1, source_target_pairs={{0,12},{1,13},{2,14},{3,15},{4,8},{5,9},{6,10},{7,11},{8,4},{9,5},... | collective-permute-start | bytes 393224 | tf_op jit(solution)/shard_map/ppermute | solution.py:26
  83.5 5.3 %copy-start.13 = (s32[264]{0:T(512)S(1)}, s32[264]{0:T(512)}, u32[]{:S(2)}) copy-start(s32[264]{0:T(512)} %get-tuple-element.102.refs_0_) | copy-start | bytes 3172

commit v3 on v2

--- a/solution.py
+++ b/solution.py
@@ -166,7 +166,7 @@
     elif is_up:
         active, slope_ref, acc = rest
     else:
-        slope_ref, slope_grad, acc = rest
+        slope_ref, col_ref, up_ref, slope_grad, sent, acc = rest
     acc[...] = jnp.zeros_like(acc) if first else acc_in[...]
     add_blocks(me_ref, where_ref, w_ref, x_refs, starts, acc, rows, is_up)
     if last:
@@ -183,9 +183,12 @@
             return carry
 
         lax.fori_loop(0, ff // BS, body, 0)
-
-
-def hidden_sum(rows, is_up, me, where, w, pieces, starts, acc=None, last=False, slope=None):
+        if not is_up:
+            skip = up_ref.shape[0] // rows // 4
+            input_grad_kernel(rows, skip, (1,), me_ref, col_ref, up_ref, slope_grad, sent)
+
+
+def hidden_sum(rows, is_up, me, where, w, pieces, starts, acc=None, last=False, slope=None, up=()):
     ff, tokens = FBLK * BS, pieces[0].shape[1]
     smem = pl.BlockSpec(memory_space=SMEM)
     vmem = pl.BlockSpec(memory_space=VMEM)
@@ -196,17 +199,17 @@
     elif is_up:
         outs = [kept, whole]
     else:
-        outs = [kept]
+        outs = [kept, jax.ShapeDtypeStruct((w.shape[0] // 4, tokens), BF)]
     return pl.pallas_call(
         functools.partial(hidden_kernel, rows, is_up, tuple(starts), acc is None, last),
-        in_specs=[smem, smem] + [vmem] * (1 + len(pieces) + len(more)),
+        in_specs=[smem, smem] + [vmem] * (1 + len(pieces) + len(more)) + [smem, vmem][: len(up)],
         out_specs=[vmem] * len(outs),
         out_shape=outs,
         scratch_shapes=[VMEM((ff, tokens), F32)] if last else [],
         compiler_params=pltpu.CompilerParams(vmem_limit_bytes=12 << 20),
         cost_estimate=COST,
         name=("hidden" if is_up else "upper") + ("_last" if last else ""),
-    )(me, where, w, *pieces, *more)
+    )(me, where, w, *pieces, *more, *up)
 
 
 def input_grad_kernel(rows, skip, bits, me_ref, col_ref, w_ref, s_ref, *outs):
@@ -464,14 +467,13 @@
     cot_far, slope, upper, in_far_o, early = after((cot_far, slope, upper, in_far_o, early))
     cot_far_b = swap(cot_far, "mp", 1)
     (upper,) = hidden_sum(rows, False, me, row_down, down_w, [cot_far], [(0, far)], upper)
-    (slope_grad,) = hidden_sum(
+    slope_grad, sent = hidden_sum(
         rows, False, me, row_down, down_w, [cot_far_b], [(1, far)], upper, True,
-        slope,
+        slope, (col_up, up_w),
     )
     slope_grad_o = [swap(slope_grad, "dp", d) for d in others]
 
     part = functools.partial(input_grad_part, rows)
-    (sent,) = part(far, (1,), me, col_up, up_w, slope_grad)
     arrived = swap(sent, "mp", 1)
     (terms,) = part(far, (0,), me, col_up, up_w, slope_grad)
     (sent,) = add_and_split(terms, [arrived], 0)

time: 95.2 us -> 94.7 us (level)
  starting transfers between devices: 33.1 us -> 30.7 us
  waiting for transfers between devices: 18.7 us -> 21.1 us
    ppermute x32, starting transfers between devices: 31.6 us -> 29.2 us  [swap(): return lax.ppermute(value, axis, [(i, i ^ mask) for i in range(size)])]
    ppermute x32, waiting for transfers between devices: 18.7 us -> 21.1 us  [swap(): return lax.ppermute(value, axis, [(i, i ^ mask) for i in range(size)])]
    pallas_call x3 -> x2, Pallas kernels: 4.42 us -> 3.03 us  [input_grad_part(): pl.pallas_call(functools.partial(input_grad_kernel, rows, skip, bits), in...]
where the time goes in v3:
time: 94.7 us; the launch traced here: 94.3 us
  Pallas kernels  35.3 us (37%)
  starting transfers between devices  30.7 us (32%)
  waiting for transfers between devices  21.1 us (22%)
  local copies, waits for them, and re-layouts  6.34 us (7%)
    ppermute x32, starting transfers between devices, swap(): return lax.ppermute(value, axis, [(i, i ^ mask) for i in range(size)])  29.2 us
    ppermute x32, waiting for transfers between devices, swap(): return lax.ppermute(value, axis, [(i, i ^ mask) for i in range(size)])  21.1 us
    pallas_call x5, Pallas kernels, hidden_sum(): pl.pallas_call(functools.partial(hidden_kernel, rows, is_up, tuple(starts...  14.3 us
    pallas_call x2, Pallas kernels, owned_grads(): pl.pallas_call(functools.partial(grads_kernel, groups, pieces, capacity,...  10.6 us
    unnamed x32, local copies, waits for them, and re-layouts  6.34 us
    pallas_call x2, Pallas kernels, input_grad_part(): pl.pallas_call(functools.partial(input_grad_kernel, rows, skip, bits), in...  3.03 us
    pallas_call x2, Pallas kernels, relayout(): pl.pallas_call(functools.partial(relayout_kernel, RELAYOUT), in_specs=[vm...  2.93 us
    pallas_call x1, Pallas kernels, slots(): pl.pallas_call(slots_kernel, in_specs=[spec] * 3, out_specs=[spec] * 3, o...  2.46 us
  transfers between devices with their start and end apart: 33, of which 9 were waited for; matrix products, arithmetic and copies ran while one was open for 0% of the time, Pallas kernels for 34%

profile of v3, /device:TPU:0, one launch (start us, length us, event | category | flops | bytes accessed | tf_op | source)
XLA Modules:
  0.0 94.3 jit_solution(13581031312183349050)
XLA Ops:
  0.6 3.1 %collective-permute-start = (bf16[512,128]{1,0:T(8,128)(2,1)}, bf16[512,128]{1,0:T(8,128)(2,1)S(1)}, u32[]{:S(2)}, u32[]{:S(2)}) collective-permute-start(bf16[512,128]{1,0:T(8,128)(2,1)} %refs_0_), channel_id=1, source_target_pairs={{0,4},{1,5},{2,6},{3,7},{4,0},{5,1},{6,2},{7,3},{8,12},{9,13},{10,... | collective-permute-start | bytes 393224 | tf_op jit(solution)/shard_map/ppermute | solution.py:26
  3.7 2.6 %collective-permute-start.1 = (bf16[512,128]{1,0:T(8,128)(2,1)}, bf16[512,128]{1,0:T(8,128)(2,1)S(1)}, u32[]{:S(2)}, u32[]{:S(2)}) collective-permute-start(bf16[512,128]{1,0:T(8,128)(2,1)} %refs_0_), channel_id=1, source_target_pairs={{0,8},{1,9},{2,10},{3,11},{4,12},{5,13},{6,14},{7,15},{8,0},{9,1},... | collective-permute-start | bytes 393224 | tf_op jit(solution)/shard_map/ppermute | solution.py:26
  6.3 0.0 collective-permute-start.2
  6.3 1.7 %collective-permute-start.3 = (bf16[512,128]{1,0:T(8,128)(2,1)}, bf16[512,128]{1,0:T(8,128)(2,1)S(1)}, u32[]{:S(2)}, u32[]{:S(2)}) collective-permute-start(bf16[512,128]{1,0:T(8,128)(2,1)} %refs_0_.1), channel_id=1, source_target_pairs={{0,16},{16,0},{1,17},{17,1},{2,18},{18,2},{3,19},{19,3},{4,20},{20... | collective-permute-start | bytes 393224 | tf_op jit(solution)/shard_map/ppermute | solution.py:26
  8.0 1.5 %collective-permute-start.4 = (bf16[512,128]{1,0:T(8,128)(2,1)}, bf16[512,128]{1,0:T(8,128)(2,1)S(1)}, u32[]{:S(2)}, u32[]{:S(2)}) collective-permute-start(bf16[512,128]{1,0:T(8,128)(2,1)} %refs_0_.1), channel_id=1, source_target_pairs={{0,18},{1,19},{2,16},{3,17},{4,22},{5,23},{6,20},{7,21},{8,26},{9,... | collective-permute-start | bytes 393224 | tf_op jit(solution)/shard_map/ppermute | solution.py:36
  9.5 0.0 collective-permute-done.refs_1_
  9.5 0.7 collective-permute-start.5
  10.2 1.6 %copy-done.2 = bf16[256,4096]{1,0:T(8,128)(2,1)S(1)} copy-done((bf16[256,4096]{1,0:T(8,128)(2,1)S(1)}, bf16[256,4096]{1,0:T(8,128)(2,1)}, u32[]{:S(2)}) %copy-start.2) | copy-done | bytes 2097176
  11.8 1.5 %relayout.2.refs_2_.refs_7_.w_ref = bf16[8192,128]{1,0:T(8,128)(2,1)S(1)} custom-call(bf16[256,4096]{1,0:T(8,128)(2,1)S(1)} %copy-done.2), custom_call_target="tpu_custom_call" | custom-call | flops 536870912 | bytes 6291456 | tf_op jit(solution)/shard_map/relayout/pallas_call | solution.py:62
  13.3 3.6 %collective-permute-done.1.refs_2_ = bf16[512,128]{1,0:T(8,128)(2,1)S(1)} collective-permute-done((bf16[512,128]{1,0:T(8,128)(2,1)}, bf16[512,128]{1,0:T(8,128)(2,1)S(1)}, u32[]{:S(2)}, u32[]{:S(2)}) %collective-permute-start.1) | collective-permute-done | bytes 131104 | tf_op jit(solution)/shard_map/ppermute | solution.py:26
  16.9 0.0 collective-permute-done.4.refs_1_
  16.9 0.4 collective-permute-done.5.refs_1_
  17.3 0.7 copy-done.9
  18.0 0.1 collective-permute-start.6
  18.1 1.6 %collective-permute-start.8 = (bf16[2048,128]{1,0:T(8,128)(2,1)S(1)}, bf16[2048,128]{1,0:T(8,128)(2,1)}, u32[]{:S(2)}, u32[]{:S(2)}) collective-permute-start(bf16[2048,128]{1,0:T(8,128)(2,1)S(1)} %join_parts.3.refs_3_.refs_4_), channel_id=1, source_target_pairs={{0,16},{16,0},{1,17},{17,1},{2,18},{18,2},{3,19},{19,3},{4,20},{20... | collective-permute-start | bytes 1572872 | tf_op jit(solution)/shard_map/ppermute | solution.py:26
  19.7 1.4 %collective-permute-start.11 = (bf16[2048,128]{1,0:T(8,128)(2,1)S(1)}, bf16[2048,128]{1,0:T(8,128)(2,1)}, u32[]{:S(2)}, u32[]{:S(2)}) collective-permute-start(bf16[2048,128]{1,0:T(8,128)(2,1)S(1)} %join_parts.3.refs_3_.refs_4_), channel_id=1, source_target_pairs={{0,2},{1,3},{2,0},{3,1},{4,6},{5,7},{6,4},{7,5},{8,10},{9,11},{10,... | collective-permute-start | bytes 1572872 | tf_op jit(solution)/shard_map/ppermute | solution.py:26
  21.0 1.8 %collective-permute-start.7 = (bf16[1024,128]{1,0:T(8,128)(2,1)S(1)}, bf16[1024,128]{1,0:T(8,128)(2,1)}, u32[]{:S(2)}, u32[]{:S(2)}) collective-permute-start(bf16[1024,128]{1,0:T(8,128)(2,1)S(1)} %join_parts.4.refs_8_), channel_id=1, source_target_pairs={{0,4},{1,5},{2,6},{3,7},{4,0},{5,1},{6,2},{7,3},{8,12},{9,13},{10,... | collective-permute-start | bytes 786440 | tf_op jit(solution)/shard_map/ppermute | solution.py:26
  22.8 2.3 %collective-permute-start.9 = (bf16[512,128]{1,0:T(8,128)(2,1)S(1)}, bf16[512,128]{1,0:T(8,128)(2,1)}, u32[]{:S(2)}, u32[]{:S(2)}) collective-permute-start(bf16[512,128]{1,0:T(8,128)(2,1)S(1)} %copy-done.8), channel_id=1, source_target_pairs={{0,8},{1,9},{2,10},{3,11},{4,12},{5,13},{6,14},{7,15},{8,0},{9,1},... | collective-permute-start | bytes 393224 | tf_op jit(solution)/shard_map/ppermute | solution.py:26
  25.1 0.4 collective-permute-start.10
  25.5 3.0 %hidden.1.refs_5_ = f32[1024,128]{1,0:T(8,128)S(1)} custom-call(s32[1]{0:T(128)} %bitcast.refs_0_.me_ref.refs_3_, s32[256]{0:T(256)S(1)} %copy-done.11, bf16[8192,128]{1,0:T(8,128)(2,1)S(1)} %relayout.2.refs_2_.refs_7_.w_ref, bf16[2048,128]{1,0:T(8,128)(2,1)S(1)} %join_parts.3.refs_3_.refs_4_, bf16[2048,128]{1,0:T(8,128)(2,1)S(1)} %collective-permute-done.6.refs_4_.refs_6_), custom_call_target="tpu_custom_call" | custom-call | flops 536870912 | bytes 6291456 | tf_op jit(solution)/shard_map/hidden/pallas_call | solution.py:203
  28.5 0.0 copy-start.4
  28.5 0.8 copy-done.4
  29.3 1.5 %relayout.3.refs_2_ = bf16[8192,128]{1,0:T(8,128)(2,1)S(1)} custom-call(bf16[256,4096]{1,0:T(8,128)(2,1)S(1)} %copy-done.3), custom_call_target="tpu_custom_call" | custom-call | flops 536870912 | bytes 6291456 | tf_op jit(solution)/shard_map/relayout/pallas_call | solution.py:62
  30.7 1.3 %copy-done = bf16[8192,128]{1,0:T(8,128)(2,1)} copy-done((bf16[8192,128]{1,0:T(8,128)(2,1)}, bf16[8192,128]{1,0:T(8,128)(2,1)S(1)}, u32[]{:S(2)}) %copy-start) | copy-done | bytes 2097176
  32.1 2.5 %slots.1 = (s32[264]{0:T(512)}, s32[264]{0:T(512)}, s32[2]{0:T(128)}) custom-call(s32[1]{0:T(128)} %bitcast.1.me_ref, s32[256]{0:T(256)} %bitcast.4, s32[256]{0:T(256)} %bitcast.5), custom_call_target="tpu_custom_call" | custom-call | flops 536870912 | bytes 6291456 | tf_op jit(solution)/shard_map/slots/pallas_call | solution.py:97
  34.5 2.6 %collective-permute-done.10.refs_3_ = bf16[512,128]{1,0:T(8,128)(2,1)} collective-permute-done((bf16[512,128]{1,0:T(8,128)(2,1)S(1)}, bf16[512,128]{1,0:T(8,128)(2,1)}, u32[]{:S(2)}, u32[]{:S(2)}) %collective-permute-start.10) | collective-permute-done | bytes 131104 | tf_op jit(solution)/shard_map/ppermute | solution.py:26
  37.2 0.1 collective-permute-start.12
  37.3 0.0 copy-start.10
  37.3 0.9 copy-done.10
  38.2 1.0 %join_parts.5.refs_3_.refs_4_ = bf16[2048,128]{1,0:T(8,128)(2,1)S(1)} custom-call(bf16[512,128]{1,0:T(8,128)(2,1)S(1)} %copy-done.8, bf16[512,128]{1,0:T(8,128)(2,1)S(1)} %copy-done.10, bf16[512,128]{1,0:T(8,128)(2,1)} %collective-permute-done.9.refs_2_, bf16[512,128]{1,0:T(8,128)(2,1)} %collective-permute-done.10.refs_3_), custom_call_target="tpu_custom_call" | custom-call | flops 1000 | bytes 1048576 | tf_op jit(solution)/shard_map/join_parts/pallas_call | solution.py:256
  39.2 0.6 collective-permute-start.14
  39.8 0.5 collective-permute-start.13
  40.3 1.5 %collective-permute-start.15 = (bf16[2048,128]{1,0:T(8,128)(2,1)}, bf16[2048,128]{1,0:T(8,128)(2,1)S(1)}, u32[]{:S(2)}, u32[]{:S(2)}) collective-permute-start(bf16[2048,128]{1,0:T(8,128)(2,1)} %collective-permute-done.11.refs_3_.refs_5_), channel_id=1, source_target_pairs={{0,16},{16,0},{1,17},{17,1},{2,18},{18,2},{3,19},{19,3},{4,20},{20... | collective-permute-start | bytes 1572872 | tf_op jit(solution)/shard_map/ppermute | solution.py:26
  41.8 1.7 %collective-permute-start.16 = (bf16[1024,128]{1,0:T(8,128)(2,1)S(1)}, bf16[1024,128]{1,0:T(8,128)(2,1)S(1)}, u32[]{:S(2)}, u32[]{:S(2)}) collective-permute-start(bf16[1024,128]{1,0:T(8,128)(2,1)S(1)} %join_parts.4.refs_8_), channel_id=1, source_target_pairs={{0,8},{1,9},{2,10},{3,11},{4,12},{5,13},{6,14},{7,15},{8,0},{9,1},... | collective-permute-start | bytes 786440 | tf_op jit(solution)/shard_map/ppermute | solution.py:26
  43.5 1.0 %copy-done.5 = f32[1024,128]{1,0:T(8,128)S(1)} copy-done((f32[1024,128]{1,0:T(8,128)S(1)}, f32[1024,128]{1,0:T(8,128)}, u32[]{:S(2)}) %copy-start.5) | copy-done | bytes 524312
  44.5 4.6 %hidden_last.1 = (bf16[1024,128]{1,0:T(8,128)(2,1)}, f32[1024,128]{1,0:T(8,128)S(1)}) custom-call(s32[1]{0:T(128)} %bitcast.refs_0_.me_ref.refs_3_, s32[256]{0:T(256)S(1)} %copy-done.11, bf16[8192,128]{1,0:T(8,128)(2,1)S(1)} %relayout.2.refs_2_.refs_7_.w_ref, bf16[2048,128]{1,0:T(8,128)(2,1)} %collective-permute-done.11.refs_3_.refs_5_, ...), custom_call_target="tpu_custom_call" | custom-call | flops 536870912 | bytes 6291456 | tf_op jit(solution)/shard_map/hidden_last/pallas_call | solution.py:203
  49.2 2.6 %upper.2.refs_4_ = f32[1024,128]{1,0:T(8,128)S(1)} custom-call(s32[1]{0:T(128)} %bitcast.refs_0_.me_ref.refs_3_, s32[256]{0:T(256)S(1)} %copy-done.12, bf16[8192,128]{1,0:T(8,128)(2,1)S(1)} %copy-done.1, bf16[2048,128]{1,0:T(8,128)(2,1)S(1)} %join_parts.5.refs_3_.refs_4_, bf16[2048,128]{1,0:T(8,128)(2,1)S(1)} %collective-permute-done.14.refs_4_.refs_6_), custom_call_target="tpu_custom_call" | custom-call | flops 536870912 | bytes 6291456 | tf_op jit(solution)/shard_map/upper/pallas_call | solution.py:203
  51.7 4.3 %collective-permute-done.16.refs_10_ = bf16[1024,128]{1,0:T(8,128)(2,1)S(1)} collective-permute-done((bf16[1024,128]{1,0:T(8,128)(2,1)S(1)}, bf16[1024,128]{1,0:T(8,128)(2,1)S(1)}, u32[]{:S(2)}, u32[]{:S(2)}) %collective-permute-start.16) | collective-permute-done | bytes 262176 | tf_op jit(solution)/shard_map/ppermute | solution.py:26
  56.0 1.6 %upper.3.refs_4_ = f32[1024,128]{1,0:T(8,128)S(1)} custom-call(s32[1]{0:T(128)} %bitcast.refs_0_.me_ref.refs_3_, s32[256]{0:T(256)S(1)} %copy-done.12, bf16[8192,128]{1,0:T(8,128)(2,1)S(1)} %copy-done.1, bf16[2048,128]{1,0:T(8,128)(2,1)S(1)} %collective-permute-done.13.refs_3_.refs_5_, f32[1024,128]{1,0:T(8,128)S(1)} %upper.2.refs_4_), custom_call_target="tpu_custom_call" | custom-call | flops 536870912 | bytes 6291456 | tf_op jit(solution)/shard_map/upper/pallas_call | solution.py:203
  57.6 0.3 collective-permute-done.17.refs_3_.refs_7_
  57.9 2.5 %upper_last.1 = (bf16[1024,128]{1,0:T(8,128)(2,1)S(1)}, bf16[2048,128]{1,0:T(8,128)(2,1)S(1)}) custom-call(s32[1]{0:T(128)} %bitcast.refs_0_.me_ref.refs_3_, s32[256]{0:T(256)S(1)} %copy-done.12, bf16[8192,128]{1,0:T(8,128)(2,1)S(1)} %copy-done.1, bf16[2048,128]{1,0:T(8,128)(2,1)S(1)} %collective-permute-done.17.refs_3_.refs_7_, ...), custom_call_target="tpu_custom_call" | custom-call | flops 536870912 | bytes 6291456 | tf_op jit(solution)/shard_map/upper_last/pallas_call | solution.py:203
  60.5 0.3 collective-permute-start.18
  60.7 1.3 %collective-permute-start.20 = (bf16[1024,128]{1,0:T(8,128)(2,1)S(1)}, bf16[1024,128]{1,0:T(8,128)(2,1)S(1)}, u32[]{:S(2)}, u32[]{:S(2)}) collective-permute-start(bf16[1024,128]{1,0:T(8,128)(2,1)S(1)} %join_parts.4.refs_8_), channel_id=1, source_target_pairs={{0,12},{1,13},{2,14},{3,15},{4,8},{5,9},{6,10},{7,11},{8,4},{9,5},... | collective-permute-start | bytes 786440 | tf_op jit(solution)/shard_map/ppermute | solution.py:26
  62.1 1.4 %input_grad_part.2.terms_ref = f32[2048,128]{1,0:T(8,128)S(1)} custom-call(s32[1]{0:T(128)} %bitcast.refs_0_.me_ref.refs_3_, s32[256]{0:T(256)S(1)} %copy-done.11, bf16[8192,128]{1,0:T(8,128)(2,1)S(1)} %relayout.2.refs_2_.refs_7_.w_ref, bf16[1024,128]{1,0:T(8,128)(2,1)S(1)} %get-tuple-element.92.s_ref.refs_12_), custom_call_target="tpu_custom_call" | custom-call | flops 536870912 | bytes 6291456 | tf_op jit(solution)/shard_map/input_grad_part/pallas_call | solution.py:243
  63.5 0.0 copy-start.6
  63.5 0.1 add_stage.2
  63.6 0.6 collective-permute-start.19
  64.2 1.5 %collective-permute-start.21 = (bf16[1024,128]{1,0:T(8,128)(2,1)S(1)}, bf16[1024,128]{1,0:T(8,128)(2,1)S(1)}, u32[]{:S(2)}, u32[]{:S(2)}) collective-permute-start(bf16[1024,128]{1,0:T(8,128)(2,1)S(1)} %get-tuple-element.92.s_ref.refs_12_), channel_id=1, source_target_pairs={{0,16},{16,0},{1,17},{17,1},{2,18},{18,2},{3,19},{19,3},{4,20},{20... | collective-permute-start | bytes 786440 | tf_op jit(solution)/shard_map/ppermute | solution.py:26
  65.7 1.6 %input_grad_part.3 = (bf16[2048,128]{1,0:T(8,128)(2,1)S(1)}, f32[2048,128]{1,0:T(8,128)S(1)}) custom-call(s32[1]{0:T(128)} %bitcast.refs_0_.me_ref.refs_3_, s32[256]{0:T(256)S(1)} %copy-done.11, bf16[8192,128]{1,0:T(8,128)(2,1)S(1)} %relayout.2.refs_2_.refs_7_.w_ref, bf16[1024,128]{1,0:T(8,128)(2,1)S(1)} %get-tuple-element.92.s_ref.refs_12_), custom_call_target="tpu_custom_call" | custom-call | flops 536870912 | bytes 6291456 | tf_op jit(solution)/shard_map/input_grad_part/pallas_call | solution.py:243
  67.4 0.3 collective-permute-start.22
  67.7 3.5 %collective-permute-done.20.refs_11_ = bf16[1024,128]{1,0:T(8,128)(2,1)S(1)} collective-permute-done((bf16[1024,128]{1,0:T(8,128)(2,1)S(1)}, bf16[1024,128]{1,0:T(8,128)(2,1)S(1)}, u32[]{:S(2)}, u32[]{:S(2)}) %collective-permute-start.20) | collective-permute-done | bytes 262176 | tf_op jit(solution)/shard_map/ppermute | solution.py:26
  71.2 0.5 collective-permute-start.27
  71.7 1.3 %collective-permute-done.21.refs_13_ = bf16[1024,128]{1,0:T(8,128)(2,1)S(1)} collective-permute-done((bf16[1024,128]{1,0:T(8,128)(2,1)S(1)}, bf16[1024,128]{1,0:T(8,128)(2,1)S(1)}, u32[]{:S(2)}, u32[]{:S(2)}) %collective-permute-start.21) | collective-permute-done | bytes 262176 | tf_op jit(solution)/shard_map/ppermute | solution.py:26
  73.0 4.6 %collective-permute-done.19.refs_0_ = bf16[2048,128]{1,0:T(8,128)(2,1)S(1)} collective-permute-done((bf16[2048,128]{1,0:T(8,128)(2,1)S(1)}, bf16[2048,128]{1,0:T(8,128)(2,1)S(1)}, u32[]{:S(2)}, u32[]{:S(2)}) %collective-permute-start.19) | collective-permute-done | bytes 524320 | tf_op jit(solution)/shard_map/ppermute | solution.py:26
  77.5 0.6 collective-permute-start.32
  78.2 0.2 collective-permute-start.31
  78.3 0.2 add_stage.3
  78.5 0.2 collective-permute-start.23
  78.7 0.4 collective-permute-done.30.refs_14_
  79.1 2.6 %collective-permute-start.24 = (bf16[512,128]{1,0:T(8,128)(2,1)S(1)}, bf16[512,128]{1,0:T(8,128)(2,1)S(1)}, u32[]{:S(2)}, u32[]{:S(2)}) collective-permute-start(bf16[512,128]{1,0:T(8,128)(2,1)S(1)} %get-tuple-element.99), channel_id=1, source_target_pairs={{0,8},{1,9},{2,10},{3,11},{4,12},{5,13},{6,14},{7,15},{8,0},{9,1},... | collective-permute-start | bytes 393224 | tf_op jit(solution)/shard_map/ppermute | solution.py:26
  81.6 1.3 %collective-permute-start.25 = (bf16[512,128]{1,0:T(8,128)(2,1)S(1)}, bf16[512,128]{1,0:T(8,128)(2,1)S(1)}, u32[]{:S(2)}, u32[]{:S(2)}) collective-permute-start(bf16[512,128]{1,0:T(8,128)(2,1)S(1)} %get-tuple-element.100), channel_id=1, source_target_pairs={{0,12},{1,13},{2,14},{3,15},{4,8},{5,9},{6,10},{7,11},{8,4},{9,5},... | collective-permute-start | bytes 393224 | tf_op jit(solution)/shard_map/ppermute | solution.py:26
  83.0 5.3 %grads_up.1 = bf16[160,4096]{1,0:T(8,128)(2,1)} custom-call(s32[264]{0:T(512)S(1)} %copy-done.14, s32[2]{0:T(128)S(1)} %copy-done.15, s32[256]{0:T(256)S(1)} %copy-done.11, s32[1]{0:T(128)} %bitcast.refs_0_.me_ref.refs_3_, bf16[2048,128]{1,0:T(8,128)(2,1)S(1)} %join_parts.3.refs_3_.refs_4_, bf16[2048,128]{1,0:T(8,128)(2,1)} %collective-permute-done.11.refs_3_.refs_5_, ...), custom_call_target="tpu_custom_call" | custom-call | flops 536870912 | bytes 6291456 | tf_op jit(solution)/shard_map/grads_up/pallas_call | solution.py:404
  88.3 5.3 %grads_down.1 = bf16[160,4096]{1,0:T(8,128)(2,1)} custom-call(s32[264]{0:T(512)S(1)} %copy-done.13, s32[2]{0:T(128)S(1)} %copy-done.15, s32[256]{0:T(256)S(1)} %copy-done.12, s32[1]{0:T(128)} %bitcast.refs_0_.me_ref.refs_3_, bf16[2048,128]{1,0:T(8,128)(2,1)S(1)} %join_parts.5.refs_3_.refs_4_, bf16[2048,128]{1,0:T(8,128)(2,1)S(1)} %collective-permute-done.13.refs_3_.refs_5_, ...), custom_call_target="tpu_custom_call" | custom-call | flops 536870912 | bytes 6291456 | tf_op jit(solution)/shard_map/grads_down/pallas_call | solution.py:404
  93.6 0.7 add_last.1
  (52 shorter events, 0.2 us)
Async XLA Ops:
  0.6 8.9 %collective-permute-start = (bf16[512,128]{1,0:T(8,128)(2,1)}, bf16[512,128]{1,0:T(8,128)(2,1)S(1)}, u32[]{:S(2)}, u32[]{:S(2)}) collective-permute-start(bf16[512,128]{1,0:T(8,128)(2,1)} %refs_0_), channel_id=1, source_target_pairs={{0,4},{1,5},{2,6},{3,7},{4,0},{5,1},{6,2},{7,3},{8,12},{9,13},{10,... | collective-permute-start | bytes 393224 | tf_op jit(solution)/shard_map/ppermute | solution.py:26
  3.7 13.2 %collective-permute-start.1 = (bf16[512,128]{1,0:T(8,128)(2,1)}, bf16[512,128]{1,0:T(8,128)(2,1)S(1)}, u32[]{:S(2)}, u32[]{:S(2)}) collective-permute-start(bf16[512,128]{1,0:T(8,128)(2,1)} %refs_0_), channel_id=1, source_target_pairs={{0,8},{1,9},{2,10},{3,11},{4,12},{5,13},{6,14},{7,15},{8,0},{9,1},... | collective-permute-start | bytes 393224 | tf_op jit(solution)/shard_map/ppermute | solution.py:26
  6.3 10.6 %collective-permute-start.2 = (bf16[512,128]{1,0:T(8,128)(2,1)}, bf16[512,128]{1,0:T(8,128)(2,1)S(1)}, u32[]{:S(2)}, u32[]{:S(2)}) collective-permute-start(bf16[512,128]{1,0:T(8,128)(2,1)} %refs_0_), channel_id=1, source_target_pairs={{0,12},{1,13},{2,14},{3,15},{4,8},{5,9},{6,10},{7,11},{8,4},{9,5},... | collective-permute-start | bytes 393224 | tf_op jit(solution)/shard_map/ppermute | solution.py:26
  6.3 10.6 %collective-permute-start.3 = (bf16[512,128]{1,0:T(8,128)(2,1)}, bf16[512,128]{1,0:T(8,128)(2,1)S(1)}, u32[]{:S(2)}, u32[]{:S(2)}) collective-permute-start(bf16[512,128]{1,0:T(8,128)(2,1)} %refs_0_.1), channel_id=1, source_target_pairs={{0,16},{16,0},{1,17},{17,1},{2,18},{18,2},{3,19},{19,3},{4,20},{20... | collective-permute-start | bytes 393224 | tf_op jit(solution)/shard_map/ppermute | solution.py:26
  8.0 8.9 %collective-permute-start.4 = (bf16[512,128]{1,0:T(8,128)(2,1)}, bf16[512,128]{1,0:T(8,128)(2,1)S(1)}, u32[]{:S(2)}, u32[]{:S(2)}) collective-permute-start(bf16[512,128]{1,0:T(8,128)(2,1)} %refs_0_.1), channel_id=1, source_target_pairs={{0,18},{1,19},{2,16},{3,17},{4,22},{5,23},{6,20},{7,21},{8,26},{9,... | collective-permute-start | bytes 393224 | tf_op jit(solution)/shard_map/ppermute | solution.py:36
  9.5 7.8 %collective-permute-start.5 = (bf16[512,128]{1,0:T(8,128)(2,1)}, bf16[512,128]{1,0:T(8,128)(2,1)S(1)}, u32[]{:S(2)}, u32[]{:S(2)}) collective-permute-start(bf16[512,128]{1,0:T(8,128)(2,1)} %refs_0_.1), channel_id=1, source_target_pairs={{0,4},{1,5},{2,6},{3,7},{4,0},{5,1},{6,2},{7,3},{8,12},{9,13},{10,... | collective-permute-start | bytes 393224 | tf_op jit(solution)/shard_map/ppermute | solution.py:26
  10.2 1.6 %copy-start.2 = (bf16[256,4096]{1,0:T(8,128)(2,1)S(1)}, bf16[256,4096]{1,0:T(8,128)(2,1)}, u32[]{:S(2)}) copy-start(bf16[256,4096]{1,0:T(8,128)(2,1)} %src.1) | copy-start | bytes 6291460
  11.8 6.2 %copy-start.7 = (bf16[512,128]{1,0:T(8,128)(2,1)S(1)}, bf16[512,128]{1,0:T(8,128)(2,1)}, u32[]{:S(2)}) copy-start(bf16[512,128]{1,0:T(8,128)(2,1)} %refs_0_) | copy-start | bytes 393220
  11.8 11.0 %copy-start.8 = (bf16[512,128]{1,0:T(8,128)(2,1)S(1)}, bf16[512,128]{1,0:T(8,128)(2,1)}, u32[]{:S(2)}) copy-start(bf16[512,128]{1,0:T(8,128)(2,1)} %refs_0_.1) | copy-start | bytes 393220
  11.8 13.7 %copy-start.11 = (s32[256]{0:T(256)S(1)}, s32[256]{0:T(256)}, u32[]{:S(2)}) copy-start(s32[256]{0:T(256)} %refs_2_.2) | copy-start | bytes 3076
  17.3 0.7 copy-start.9
  18.0 3.0 %collective-permute-start.6 = (bf16[2048,128]{1,0:T(8,128)(2,1)S(1)}, bf16[2048,128]{1,0:T(8,128)(2,1)S(1)}, u32[]{:S(2)}, u32[]{:S(2)}) collective-permute-start(bf16[2048,128]{1,0:T(8,128)(2,1)S(1)} %join_parts.3.refs_3_.refs_4_), channel_id=1, source_target_pairs={{0,1},{1,0},{2,3},{3,2},{4,5},{5,4},{6,7},{7,6},{8,9},{9,8},{10,11... | collective-permute-start | bytes 1572872 | tf_op jit(solution)/shard_map/ppermute | solution.py:26
  18.1 19.1 %collective-permute-start.8 = (bf16[2048,128]{1,0:T(8,128)(2,1)S(1)}, bf16[2048,128]{1,0:T(8,128)(2,1)}, u32[]{:S(2)}, u32[]{:S(2)}) collective-permute-start(bf16[2048,128]{1,0:T(8,128)(2,1)S(1)} %join_parts.3.refs_3_.refs_4_), channel_id=1, source_target_pairs={{0,16},{16,0},{1,17},{17,1},{2,18},{18,2},{3,19},{19,3},{4,20},{20... | collective-permute-start | bytes 1572872 | tf_op jit(solution)/shard_map/ppermute | solution.py:26
  19.7 17.5 %collective-permute-start.11 = (bf16[2048,128]{1,0:T(8,128)(2,1)S(1)}, bf16[2048,128]{1,0:T(8,128)(2,1)}, u32[]{:S(2)}, u32[]{:S(2)}) collective-permute-start(bf16[2048,128]{1,0:T(8,128)(2,1)S(1)} %join_parts.3.refs_3_.refs_4_), channel_id=1, source_target_pairs={{0,2},{1,3},{2,0},{3,1},{4,6},{5,7},{6,4},{7,5},{8,10},{9,11},{10,... | collective-permute-start | bytes 1572872 | tf_op jit(solution)/shard_map/ppermute | solution.py:26
  21.0 16.2 %collective-permute-start.7 = (bf16[1024,128]{1,0:T(8,128)(2,1)S(1)}, bf16[1024,128]{1,0:T(8,128)(2,1)}, u32[]{:S(2)}, u32[]{:S(2)}) collective-permute-start(bf16[1024,128]{1,0:T(8,128)(2,1)S(1)} %join_parts.4.refs_8_), channel_id=1, source_target_pairs={{0,4},{1,5},{2,6},{3,7},{4,0},{5,1},{6,2},{7,3},{8,12},{9,13},{10,... | collective-permute-start | bytes 786440 | tf_op jit(solution)/shard_map/ppermute | solution.py:26
  22.8 6.5 %copy-start.3 = (bf16[256,4096]{1,0:T(8,128)(2,1)S(1)}, bf16[256,4096]{1,0:T(8,128)(2,1)}, u32[]{:S(2)}) copy-start(bf16[256,4096]{1,0:T(8,128)(2,1)} %src.2) | copy-start | bytes 6291460
  22.8 11.7 %collective-permute-start.9 = (bf16[512,128]{1,0:T(8,128)(2,1)S(1)}, bf16[512,128]{1,0:T(8,128)(2,1)}, u32[]{:S(2)}, u32[]{:S(2)}) collective-permute-start(bf16[512,128]{1,0:T(8,128)(2,1)S(1)} %copy-done.8), channel_id=1, source_target_pairs={{0,8},{1,9},{2,10},{3,11},{4,12},{5,13},{6,14},{7,15},{8,0},{9,1},... | collective-permute-start | bytes 393224 | tf_op jit(solution)/shard_map/ppermute | solution.py:26
  25.1 12.1 %collective-permute-start.10 = (bf16[512,128]{1,0:T(8,128)(2,1)S(1)}, bf16[512,128]{1,0:T(8,128)(2,1)}, u32[]{:S(2)}, u32[]{:S(2)}) collective-permute-start(bf16[512,128]{1,0:T(8,128)(2,1)S(1)} %copy-done.8), channel_id=1, source_target_pairs={{0,12},{1,13},{2,14},{3,15},{4,8},{5,9},{6,10},{7,11},{8,4},{9,5},... | collective-permute-start | bytes 393224 | tf_op jit(solution)/shard_map/ppermute | solution.py:26
  28.5 0.8 copy-start.4
  30.7 1.3 %copy-start = (bf16[8192,128]{1,0:T(8,128)(2,1)}, bf16[8192,128]{1,0:T(8,128)(2,1)S(1)}, u32[]{:S(2)}) copy-start(bf16[8192,128]{1,0:T(8,128)(2,1)S(1)} %relayout.3.refs_2_) | copy-start | bytes 6291460
  37.2 6.3 %collective-permute-start.12 = (bf16[2048,128]{1,0:T(8,128)(2,1)}, bf16[2048,128]{1,0:T(8,128)(2,1)S(1)}, u32[]{:S(2)}, u32[]{:S(2)}) collective-permute-start(bf16[2048,128]{1,0:T(8,128)(2,1)} %collective-permute-done.11.refs_3_.refs_5_), channel_id=1, source_target_pairs={{0,1},{1,0},{2,3},{3,2},{4,5},{5,4},{6,7},{7,6},{8,9},{9,8},{10,11... | collective-permute-start | bytes 1572872 | tf_op jit(solution)/shard_map/ppermute | solution.py:26
  37.3 0.9 copy-start.10
  38.2 11.0 %copy-start.12 = (s32[256]{0:T(256)S(1)}, s32[256]{0:T(256)}, u32[]{:S(2)}) copy-start(s32[256]{0:T(256)} %refs_2_.3) | copy-start | bytes 3076
  39.2 9.9 %copy-start.1 = (bf16[8192,128]{1,0:T(8,128)(2,1)S(1)}, bf16[8192,128]{1,0:T(8,128)(2,1)}, u32[]{:S(2)}) copy-start(bf16[8192,128]{1,0:T(8,128)(2,1)} %copy-done) | copy-start | bytes 6291460
  39.2 9.9 %collective-permute-start.14 = (bf16[2048,128]{1,0:T(8,128)(2,1)S(1)}, bf16[2048,128]{1,0:T(8,128)(2,1)S(1)}, u32[]{:S(2)}, u32[]{:S(2)}) collective-permute-start(bf16[2048,128]{1,0:T(8,128)(2,1)S(1)} %join_parts.5.refs_3_.refs_4_), channel_id=1, source_target_pairs={{0,1},{1,0},{2,3},{3,2},{4,5},{5,4},{6,7},{7,6},{8,9},{9,8},{10,11... | collective-permute-start | bytes 1572872 | tf_op jit(solution)/shard_map/ppermute | solution.py:26
  39.8 16.2 %collective-permute-start.13 = (bf16[2048,128]{1,0:T(8,128)(2,1)S(1)}, bf16[2048,128]{1,0:T(8,128)(2,1)S(1)}, u32[]{:S(2)}, u32[]{:S(2)}) collective-permute-start(bf16[2048,128]{1,0:T(8,128)(2,1)S(1)} %join_parts.5.refs_3_.refs_4_), channel_id=1, source_target_pairs={{0,2},{1,3},{2,0},{3,1},{4,6},{5,7},{6,4},{7,5},{8,10},{9,11},{10,... | collective-permute-start | bytes 1572872 | tf_op jit(solution)/shard_map/ppermute | solution.py:26
  40.3 15.7 %collective-permute-start.15 = (bf16[2048,128]{1,0:T(8,128)(2,1)}, bf16[2048,128]{1,0:T(8,128)(2,1)S(1)}, u32[]{:S(2)}, u32[]{:S(2)}) collective-permute-start(bf16[2048,128]{1,0:T(8,128)(2,1)} %collective-permute-done.11.refs_3_.refs_5_), channel_id=1, source_target_pairs={{0,16},{16,0},{1,17},{17,1},{2,18},{18,2},{3,19},{19,3},{4,20},{20... | collective-permute-start | bytes 1572872 | tf_op jit(solution)/shard_map/ppermute | solution.py:26
  41.8 14.2 %collective-permute-start.16 = (bf16[1024,128]{1,0:T(8,128)(2,1)S(1)}, bf16[1024,128]{1,0:T(8,128)(2,1)S(1)}, u32[]{:S(2)}, u32[]{:S(2)}) collective-permute-start(bf16[1024,128]{1,0:T(8,128)(2,1)S(1)} %join_parts.4.refs_8_), channel_id=1, source_target_pairs={{0,8},{1,9},{2,10},{3,11},{4,12},{5,13},{6,14},{7,15},{8,0},{9,1},... | collective-permute-start | bytes 786440 | tf_op jit(solution)/shard_map/ppermute | solution.py:26
  43.5 1.0 %copy-start.5 = (f32[1024,128]{1,0:T(8,128)S(1)}, f32[1024,128]{1,0:T(8,128)}, u32[]{:S(2)}) copy-start(f32[1024,128]{1,0:T(8,128)} %copy-done.4) | copy-start | bytes 1572868
  56.0 1.9 %collective-permute-start.17 = (bf16[2048,128]{1,0:T(8,128)(2,1)S(1)}, bf16[2048,128]{1,0:T(8,128)(2,1)S(1)}, u32[]{:S(2)}, u32[]{:S(2)}) collective-permute-start(bf16[2048,128]{1,0:T(8,128)(2,1)S(1)} %collective-permute-done.13.refs_3_.refs_5_), channel_id=1, source_target_pairs={{0,1},{1,0},{2,3},{3,2},{4,5},{5,4},{6,7},{7,6},{8,9},{9,8},{10,11... | collective-permute-start | bytes 1572872 | tf_op jit(solution)/shard_map/ppermute | solution.py:26
  60.5 3.0 %collective-permute-start.18 = (bf16[2048,128]{1,0:T(8,128)(2,1)S(1)}, bf16[2048,128]{1,0:T(8,128)(2,1)S(1)}, u32[]{:S(2)}, u32[]{:S(2)}) collective-permute-start(bf16[2048,128]{1,0:T(8,128)(2,1)S(1)} %get-tuple-element.91), channel_id=1, source_target_pairs={{0,1},{1,0},{2,3},{3,2},{4,5},{5,4},{6,7},{7,6},{8,9},{9,8},{10,11... | collective-permute-start | bytes 1572872 | tf_op jit(solution)/shard_map/ppermute | solution.py:26
  60.7 10.4 %collective-permute-start.20 = (bf16[1024,128]{1,0:T(8,128)(2,1)S(1)}, bf16[1024,128]{1,0:T(8,128)(2,1)S(1)}, u32[]{:S(2)}, u32[]{:S(2)}) collective-permute-start(bf16[1024,128]{1,0:T(8,128)(2,1)S(1)} %join_parts.4.refs_8_), channel_id=1, source_target_pairs={{0,12},{1,13},{2,14},{3,15},{4,8},{5,9},{6,10},{7,11},{8,4},{9,5},... | collective-permute-start | bytes 786440 | tf_op jit(solution)/shard_map/ppermute | solution.py:26
  63.5 14.1 %copy-start.6 = (bf16[1024,128]{1,0:T(8,128)(2,1)S(1)}, bf16[1024,128]{1,0:T(8,128)(2,1)}, u32[]{:S(2)}) copy-start(bf16[1024,128]{1,0:T(8,128)(2,1)} %get-tuple-element.110.refs_16_) | copy-start | bytes 786436
  63.6 13.9 %collective-permute-start.19 = (bf16[2048,128]{1,0:T(8,128)(2,1)S(1)}, bf16[2048,128]{1,0:T(8,128)(2,1)S(1)}, u32[]{:S(2)}, u32[]{:S(2)}) collective-permute-start(bf16[2048,128]{1,0:T(8,128)(2,1)S(1)} %add_stage.2), channel_id=1, source_target_pairs={{0,2},{1,3},{2,0},{3,1},{4,6},{5,7},{6,4},{7,5},{8,10},{9,11},{10,... | collective-permute-start | bytes 1572872 | tf_op jit(solution)/shard_map/ppermute | solution.py:26
  64.2 6.9 %collective-permute-start.28 = (bf16[1024,128]{1,0:T(8,128)(2,1)S(1)}, bf16[1024,128]{1,0:T(8,128)(2,1)S(1)}, u32[]{:S(2)}, u32[]{:S(2)}) collective-permute-start(bf16[1024,128]{1,0:T(8,128)(2,1)S(1)} %join_parts.4.refs_8_), channel_id=1, source_target_pairs={{0,1},{1,0},{2,3},{3,2},{4,5},{5,4},{6,7},{7,6},{8,9},{9,8},{10,11... | collective-permute-start | bytes 786440 | tf_op jit(solution)/shard_map/ppermute | solution.py:26
  64.2 8.7 %collective-permute-start.21 = (bf16[1024,128]{1,0:T(8,128)(2,1)S(1)}, bf16[1024,128]{1,0:T(8,128)(2,1)S(1)}, u32[]{:S(2)}, u32[]{:S(2)}) collective-permute-start(bf16[1024,128]{1,0:T(8,128)(2,1)S(1)} %get-tuple-element.92.s_ref.refs_12_), channel_id=1, source_target_pairs={{0,16},{16,0},{1,17},{17,1},{2,18},{18,2},{3,19},{19,3},{4,20},{20... | collective-permute-start | bytes 786440 | tf_op jit(solution)/shard_map/ppermute | solution.py:26
  65.7 17.2 %copy-start.14 = (s32[264]{0:T(512)S(1)}, s32[264]{0:T(512)}, u32[]{:S(2)}) copy-start(s32[264]{0:T(512)} %get-tuple-element.101.refs_0_) | copy-start | bytes 3172
  65.7 17.2 %copy-start.15 = (s32[2]{0:T(128)S(1)}, s32[2]{0:T(128)}, u32[]{:S(2)}) copy-start(s32[2]{0:T(128)} %get-tuple-element.102.refs_1_) | copy-start | bytes 28
  67.4 10.8 %collective-permute-start.22 = (bf16[2048,128]{1,0:T(8,128)(2,1)S(1)}, bf16[2048,128]{1,0:T(8,128)(2,1)S(1)}, u32[]{:S(2)}, u32[]{:S(2)}) collective-permute-start(bf16[2048,128]{1,0:T(8,128)(2,1)S(1)} %get-tuple-element.96), channel_id=1, source_target_pairs={{0,1},{1,0},{2,3},{3,2},{4,5},{5,4},{6,7},{7,6},{8,9},{9,8},{10,11... | collective-permute-start | bytes 1572872 | tf_op jit(solution)/shard_map/ppermute | solution.py:26
  71.2 7.3 %collective-permute-start.26 = (bf16[2048,128]{1,0:T(8,128)(2,1)}, bf16[2048,128]{1,0:T(8,128)(2,1)S(1)}, u32[]{:S(2)}, u32[]{:S(2)}) collective-permute-start(bf16[2048,128]{1,0:T(8,128)(2,1)} %collective-permute-done.8.refs_8_), channel_id=1, source_target_pairs={{0,1},{1,0},{2,3},{3,2},{4,5},{5,4},{6,7},{7,6},{8,9},{9,8},{10,11... | collective-permute-start | bytes 1572872 | tf_op jit(solution)/shard_map/ppermute | solution.py:26
  71.2 10.4 %collective-permute-start.27 = (bf16[2048,128]{1,0:T(8,128)(2,1)S(1)}, bf16[2048,128]{1,0:T(8,128)(2,1)S(1)}, u32[]{:S(2)}, u32[]{:S(2)}) collective-permute-start(bf16[2048,128]{1,0:T(8,128)(2,1)S(1)} %collective-permute-done.15.refs_9_), channel_id=1, source_target_pairs={{0,1},{1,0},{2,3},{3,2},{4,5},{5,4},{6,7},{7,6},{8,9},{9,8},{10,11... | collective-permute-start | bytes 1572872 | tf_op jit(solution)/shard_map/ppermute | solution.py:26
  73.0 4.6 %collective-permute-start.29 = (bf16[1024,128]{1,0:T(8,128)(2,1)}, bf16[1024,128]{1,0:T(8,128)(2,1)S(1)}, u32[]{:S(2)}, u32[]{:S(2)}) collective-permute-start(bf16[1024,128]{1,0:T(8,128)(2,1)} %collective-permute-done.7.refs_9_), channel_id=1, source_target_pairs={{0,1},{1,0},{2,3},{3,2},{4,5},{5,4},{6,7},{7,6},{8,9},{9,8},{10,11... | collective-permute-start | bytes 786440 | tf_op jit(solution)/shard_map/ppermute | solution.py:26
  77.5 1.5 %collective-permute-start.30 = (bf16[1024,128]{1,0:T(8,128)(2,1)S(1)}, bf16[1024,128]{1,0:T(8,128)(2,1)S(1)}, u32[]{:S(2)}, u32[]{:S(2)}) collective-permute-start(bf16[1024,128]{1,0:T(8,128)(2,1)S(1)} %collective-permute-done.16.refs_10_), channel_id=1, source_target_pairs={{0,1},{1,0},{2,3},{3,2},{4,5},{5,4},{6,7},{7,6},{8,9},{9,8},{10,11... | collective-permute-start | bytes 786440 | tf_op jit(solution)/shard_map/ppermute | solution.py:26
  77.5 10.7 %collective-permute-start.32 = (bf16[1024,128]{1,0:T(8,128)(2,1)S(1)}, bf16[1024,128]{1,0:T(8,128)(2,1)S(1)}, u32[]{:S(2)}, u32[]{:S(2)}) collective-permute-start(bf16[1024,128]{1,0:T(8,128)(2,1)S(1)} %copy-done.6), channel_id=1, source_target_pairs={{0,16},{16,0},{1,17},{17,1},{2,18},{18,2},{3,19},{19,3},{4,20},{20... | collective-permute-start | bytes 786440 | tf_op jit(solution)/shard_map/ppermute | solution.py:26
  78.2 10.1 %collective-permute-start.31 = (bf16[1024,128]{1,0:T(8,128)(2,1)S(1)}, bf16[1024,128]{1,0:T(8,128)(2,1)S(1)}, u32[]{:S(2)}, u32[]{:S(2)}) collective-permute-start(bf16[1024,128]{1,0:T(8,128)(2,1)S(1)} %collective-permute-done.20.refs_11_), channel_id=1, source_target_pairs={{0,1},{1,0},{2,3},{3,2},{4,5},{5,4},{6,7},{7,6},{8,9},{9,8},{10,11... | collective-permute-start | bytes 786440 | tf_op jit(solution)/shard_map/ppermute | solution.py:26
  78.5 15.1 %collective-permute-start.23 = (bf16[512,128]{1,0:T(8,128)(2,1)S(1)}, bf16[512,128]{1,0:T(8,128)(2,1)S(1)}, u32[]{:S(2)}, u32[]{:S(2)}) collective-permute-start(bf16[512,128]{1,0:T(8,128)(2,1)S(1)} %get-tuple-element.98), channel_id=1, source_target_pairs={{0,4},{1,5},{2,6},{3,7},{4,0},{5,1},{6,2},{7,3},{8,12},{9,13},{10,... | collective-permute-start | bytes 393224 | tf_op jit(solution)/shard_map/ppermute | solution.py:26
  79.1 14.5 %collective-permute-start.24 = (bf16[512,128]{1,0:T(8,128)(2,1)S(1)}, bf16[512,128]{1,0:T(8,128)(2,1)S(1)}, u32[]{:S(2)}, u32[]{:S(2)}) collective-permute-start(bf16[512,128]{1,0:T(8,128)(2,1)S(1)} %get-tuple-element.99), channel_id=1, source_target_pairs={{0,8},{1,9},{2,10},{3,11},{4,12},{5,13},{6,14},{7,15},{8,0},{9,1},... | collective-permute-start | bytes 393224 | tf_op jit(solution)/shard_map/ppermute | solution.py:26
  81.6 12.0 %collective-permute-start.25 = (bf16[512,128]{1,0:T(8,128)(2,1)S(1)}, bf16[512,128]{1,0:T(8,128)(2,1)S(1)}, u32[]{:S(2)}, u32[]{:S(2)}) collective-permute-start(bf16[512,128]{1,0:T(8,128)(2,1)S(1)} %get-tuple-element.100), channel_id=1, source_target_pairs={{0,12},{1,13},{2,14},{3,15},{4,8},{5,9},{6,10},{7,11},{8,4},{9,5},... | collective-permute-start | bytes 393224 | tf_op jit(solution)/shard_map/ppermute | solution.py:26
  83.0 5.3 %copy-start.13 = (s32[264]{0:T(512)S(1)}, s32[264]{0:T(512)}, u32[]{:S(2)}) copy-start(s32[264]{0:T(512)} %get-tuple-element.106.refs_0_) | copy-start | bytes 3172

commit v4 on v3

--- a/solution.py
+++ b/solution.py
@@ -438,7 +438,6 @@
     in_near_b = swap(in_near, "mp", 1)
     cot_parts += [swap(cotangent, "mp", 4 * z) for z in range(2, far)]
     cot_o = [join([x, xy]) for x, xy in zip(cot_x, cot_xy)]
-    in_near_b, cot_o = after((in_near_b, cot_o))
     cot_o_1 = [swap(x, "mp", 4) for x in cot_o]
     (hidden,) = hidden_sum(
         rows, True, me, col_up, up_w, [in_near, in_near_b], [(0, 0), (1, 0)]
@@ -456,14 +455,13 @@
     cot_near_b = swap(cot_near, "mp", 1)
     in_far_b = swap(in_far, "mp", 1)
     in_far_o = [swap(in_far, "dp", d) for d in others]
-    cot_o_z = [[swap(x, "mp", 4 * z) for z in range(2, far)] for x in cot_o]
+    early = [[swap(x, "mp", 4 * z) for z in range(2, far - 1)] for x in cot_o]
     (upper,) = hidden_sum(
         rows, False, me, row_down, down_w, [cot_near, cot_near_b], [(0, 0), (1, 0)]
     )
     active, slope = hidden_sum(
         rows, True, me, col_up, up_w, [in_far, in_far_b], [(0, far), (1, far)], hidden, True
     )
-    early = [x[: far // 2 - 1] for x in cot_o_z]
     cot_far, slope, upper, in_far_o, early = after((cot_far, slope, upper, in_far_o, early))
     cot_far_b = swap(cot_far, "mp", 1)
     (upper,) = hidden_sum(rows, False, me, row_down, down_w, [cot_far], [(0, far)], upper)
@@ -478,7 +476,8 @@
     (terms,) = part(far, (0,), me, col_up, up_w, slope_grad)
     (sent,) = add_and_split(terms, [arrived], 0)
     arrived = swap(sent, "mp", 2)
-    sent, near_slope_grad, near_active = after((sent, slope_grad, active))
+    sent, near_slope_grad, near_active, near_cot_o = after((sent, slope_grad, active, cot_o))
+    late = [[swap(x, "mp", 4 * (far - 1))] for x in near_cot_o]
     active_o = [swap(near_active, "dp", d) for d in others]
     sent_b, terms = part(0, (1, 0), me, col_up, up_w, near_slope_grad)
     arrived_b = swap(sent_b, "mp", 1)
@@ -486,7 +485,6 @@
     in_far_o_b = [swap(x, "mp", 1) for x in in_far_o]
     in_all = [[in_near, in_far, in_near_b, in_far_b]]
     in_all += [list(x) for x in zip(in_near_o, in_far_o, in_near_o_b, in_far_o_b)]
-    late = [x[far // 2 - 1 :] for x in cot_o_z]
     arrived, late, slope_grad_o, terms = after((arrived, late, slope_grad_o, terms))
     cot_o = [
         [x, x_1] + near + rest for x, x_1, near, rest in zip(cot_o, cot_o_1, early, late)

time: 94.7 us -> 95 us (level)
  starting transfers between devices: 30.7 us -> 32.8 us
  waiting for transfers between devices: 21.1 us -> 19.2 us
    ppermute x32, starting transfers between devices: 29.2 us -> 31.3 us  [swap(): return lax.ppermute(value, axis, [(i, i ^ mask) for i in range(size)])]
    ppermute x32, waiting for transfers between devices: 21.1 us -> 19.2 us  [swap(): return lax.ppermute(value, axis, [(i, i ^ mask) for i in range(size)])]
where the time goes in v4:
time: 95 us; the launch traced here: 94.6 us
  Pallas kernels  35.4 us (37%)
  starting transfers between devices  32.8 us (35%)
  waiting for transfers between devices  19.2 us (20%)
  local copies, waits for them, and re-layouts  6.34 us (7%)
    ppermute x32, starting transfers between devices, swap(): return lax.ppermute(value, axis, [(i, i ^ mask) for i in range(size)])  31.3 us
    ppermute x32, waiting for transfers between devices, swap(): return lax.ppermute(value, axis, [(i, i ^ mask) for i in range(size)])  19.2 us
    pallas_call x5, Pallas kernels, hidden_sum(): pl.pallas_call(functools.partial(hidden_kernel, rows, is_up, tuple(starts...  14.3 us
    pallas_call x2, Pallas kernels, owned_grads(): pl.pallas_call(functools.partial(grads_kernel, groups, pieces, capacity,...  10.6 us
    unnamed x32, local copies, waits for them, and re-layouts  6.34 us
    pallas_call x2, Pallas kernels, input_grad_part(): pl.pallas_call(functools.partial(input_grad_kernel, rows, skip, bits), in...  3.03 us
    pallas_call x2, Pallas kernels, relayout(): pl.pallas_call(functools.partial(relayout_kernel, RELAYOUT), in_specs=[vm...  2.93 us
    pallas_call x1, Pallas kernels, slots(): pl.pallas_call(slots_kernel, in_specs=[spec] * 3, out_specs=[spec] * 3, o...  2.46 us
  transfers between devices with their start and end apart: 33, of which 9 were waited for; matrix products, arithmetic and copies ran while one was open for 0% of the time, Pallas kernels for 34%

profile of v4, /device:TPU:0, one launch (start us, length us, event | category | flops | bytes accessed | tf_op | source)
XLA Modules:
  0.0 94.6 jit_solution(6383637591269637829)
XLA Ops:
  0.6 3.1 %collective-permute-start = (bf16[512,128]{1,0:T(8,128)(2,1)}, bf16[512,128]{1,0:T(8,128)(2,1)S(1)}, u32[]{:S(2)}, u32[]{:S(2)}) collective-permute-start(bf16[512,128]{1,0:T(8,128)(2,1)} %refs_0_), channel_id=1, source_target_pairs={{0,4},{1,5},{2,6},{3,7},{4,0},{5,1},{6,2},{7,3},{8,12},{9,13},{10,... | collective-permute-start | bytes 393224 | tf_op jit(solution)/shard_map/ppermute | solution.py:26
  3.7 2.6 %collective-permute-start.1 = (bf16[512,128]{1,0:T(8,128)(2,1)}, bf16[512,128]{1,0:T(8,128)(2,1)S(1)}, u32[]{:S(2)}, u32[]{:S(2)}) collective-permute-start(bf16[512,128]{1,0:T(8,128)(2,1)} %refs_0_), channel_id=1, source_target_pairs={{0,8},{1,9},{2,10},{3,11},{4,12},{5,13},{6,14},{7,15},{8,0},{9,1},... | collective-permute-start | bytes 393224 | tf_op jit(solution)/shard_map/ppermute | solution.py:26
  6.3 1.7 %collective-permute-start.3 = (bf16[512,128]{1,0:T(8,128)(2,1)}, bf16[512,128]{1,0:T(8,128)(2,1)S(1)}, u32[]{:S(2)}, u32[]{:S(2)}) collective-permute-start(bf16[512,128]{1,0:T(8,128)(2,1)} %refs_0_.1), channel_id=1, source_target_pairs={{0,16},{16,0},{1,17},{17,1},{2,18},{18,2},{3,19},{19,3},{4,20},{20... | collective-permute-start | bytes 393224 | tf_op jit(solution)/shard_map/ppermute | solution.py:26
  8.0 1.5 %collective-permute-start.4 = (bf16[512,128]{1,0:T(8,128)(2,1)}, bf16[512,128]{1,0:T(8,128)(2,1)S(1)}, u32[]{:S(2)}, u32[]{:S(2)}) collective-permute-start(bf16[512,128]{1,0:T(8,128)(2,1)} %refs_0_.1), channel_id=1, source_target_pairs={{0,18},{1,19},{2,16},{3,17},{4,22},{5,23},{6,20},{7,21},{8,26},{9,... | collective-permute-start | bytes 393224 | tf_op jit(solution)/shard_map/ppermute | solution.py:36
  9.5 0.0 collective-permute-done.refs_1_
  9.5 0.7 collective-permute-start.5
  10.2 1.6 %copy-done.2 = bf16[256,4096]{1,0:T(8,128)(2,1)S(1)} copy-done((bf16[256,4096]{1,0:T(8,128)(2,1)S(1)}, bf16[256,4096]{1,0:T(8,128)(2,1)}, u32[]{:S(2)}) %copy-start.2) | copy-done | bytes 2097176
  11.8 1.5 %relayout.2.refs_2_.refs_7_.w_ref = bf16[8192,128]{1,0:T(8,128)(2,1)S(1)} custom-call(bf16[256,4096]{1,0:T(8,128)(2,1)S(1)} %copy-done.2), custom_call_target="tpu_custom_call" | custom-call | flops 536870912 | bytes 6291456 | tf_op jit(solution)/shard_map/relayout/pallas_call | solution.py:62
  13.3 3.6 %collective-permute-done.1.refs_2_ = bf16[512,128]{1,0:T(8,128)(2,1)S(1)} collective-permute-done((bf16[512,128]{1,0:T(8,128)(2,1)}, bf16[512,128]{1,0:T(8,128)(2,1)S(1)}, u32[]{:S(2)}, u32[]{:S(2)}) %collective-permute-start.1) | collective-permute-done | bytes 131104 | tf_op jit(solution)/shard_map/ppermute | solution.py:26
  16.9 0.4 collective-permute-done.5.refs_1_
  17.3 0.7 copy-done.9
  18.0 0.1 collective-permute-start.11
  18.1 1.6 %collective-permute-start.7 = (bf16[2048,128]{1,0:T(8,128)(2,1)S(1)}, bf16[2048,128]{1,0:T(8,128)(2,1)}, u32[]{:S(2)}, u32[]{:S(2)}) collective-permute-start(bf16[2048,128]{1,0:T(8,128)(2,1)S(1)} %join_parts.4.refs_3_.refs_4_), channel_id=1, source_target_pairs={{0,16},{16,0},{1,17},{17,1},{2,18},{18,2},{3,19},{19,3},{4,20},{20... | collective-permute-start | bytes 1572872 | tf_op jit(solution)/shard_map/ppermute | solution.py:26
  19.7 1.4 %collective-permute-start.10 = (bf16[2048,128]{1,0:T(8,128)(2,1)S(1)}, bf16[2048,128]{1,0:T(8,128)(2,1)}, u32[]{:S(2)}, u32[]{:S(2)}) collective-permute-start(bf16[2048,128]{1,0:T(8,128)(2,1)S(1)} %join_parts.4.refs_3_.refs_4_), channel_id=1, source_target_pairs={{0,2},{1,3},{2,0},{3,1},{4,6},{5,7},{6,4},{7,5},{8,10},{9,11},{10,... | collective-permute-start | bytes 1572872 | tf_op jit(solution)/shard_map/ppermute | solution.py:26
  21.0 1.8 %collective-permute-start.6 = (bf16[1024,128]{1,0:T(8,128)(2,1)S(1)}, bf16[1024,128]{1,0:T(8,128)(2,1)}, u32[]{:S(2)}, u32[]{:S(2)}) collective-permute-start(bf16[1024,128]{1,0:T(8,128)(2,1)S(1)} %join_parts.3.refs_8_), channel_id=1, source_target_pairs={{0,4},{1,5},{2,6},{3,7},{4,0},{5,1},{6,2},{7,3},{8,12},{9,13},{10,... | collective-permute-start | bytes 786440 | tf_op jit(solution)/shard_map/ppermute | solution.py:26
  22.8 2.3 %collective-permute-start.8 = (bf16[512,128]{1,0:T(8,128)(2,1)S(1)}, bf16[512,128]{1,0:T(8,128)(2,1)}, u32[]{:S(2)}, u32[]{:S(2)}) collective-permute-start(bf16[512,128]{1,0:T(8,128)(2,1)S(1)} %copy-done.8), channel_id=1, source_target_pairs={{0,8},{1,9},{2,10},{3,11},{4,12},{5,13},{6,14},{7,15},{8,0},{9,1},... | collective-permute-start | bytes 393224 | tf_op jit(solution)/shard_map/ppermute | solution.py:26
  25.1 0.4 collective-permute-start.9
  25.5 3.0 %hidden.1.refs_5_ = f32[1024,128]{1,0:T(8,128)S(1)} custom-call(s32[1]{0:T(128)} %bitcast.refs_0_.me_ref.refs_3_, s32[256]{0:T(256)S(1)} %copy-done.11, bf16[8192,128]{1,0:T(8,128)(2,1)S(1)} %relayout.2.refs_2_.refs_7_.w_ref, bf16[2048,128]{1,0:T(8,128)(2,1)S(1)} %join_parts.4.refs_3_.refs_4_, bf16[2048,128]{1,0:T(8,128)(2,1)S(1)} %collective-permute-done.11.refs_4_.refs_6_), custom_call_target="tpu_custom_call" | custom-call | flops 536870912 | bytes 6291456 | tf_op jit(solution)/shard_map/hidden/pallas_call | solution.py:203
  28.5 0.0 copy-start.4
  28.5 0.8 copy-done.4
  29.3 1.5 %relayout.3.refs_2_ = bf16[8192,128]{1,0:T(8,128)(2,1)S(1)} custom-call(bf16[256,4096]{1,0:T(8,128)(2,1)S(1)} %copy-done.3), custom_call_target="tpu_custom_call" | custom-call | flops 536870912 | bytes 6291456 | tf_op jit(solution)/shard_map/relayout/pallas_call | solution.py:62
  30.8 1.3 %copy-done = bf16[8192,128]{1,0:T(8,128)(2,1)} copy-done((bf16[8192,128]{1,0:T(8,128)(2,1)}, bf16[8192,128]{1,0:T(8,128)(2,1)S(1)}, u32[]{:S(2)}) %copy-start) | copy-done | bytes 2097176
  32.1 2.5 %slots.1 = (s32[264]{0:T(512)}, s32[264]{0:T(512)}, s32[2]{0:T(128)}) custom-call(s32[1]{0:T(128)} %bitcast.1.me_ref, s32[256]{0:T(256)} %bitcast.4, s32[256]{0:T(256)} %bitcast.5), custom_call_target="tpu_custom_call" | custom-call | flops 536870912 | bytes 6291456 | tf_op jit(solution)/shard_map/slots/pallas_call | solution.py:97
  34.6 2.6 %collective-permute-done.9.refs_3_ = bf16[512,128]{1,0:T(8,128)(2,1)} collective-permute-done((bf16[512,128]{1,0:T(8,128)(2,1)S(1)}, bf16[512,128]{1,0:T(8,128)(2,1)}, u32[]{:S(2)}, u32[]{:S(2)}) %collective-permute-start.9) | collective-permute-done | bytes 131104 | tf_op jit(solution)/shard_map/ppermute | solution.py:26
  37.2 0.1 collective-permute-start.12
  37.3 0.0 copy-start.10
  37.3 0.9 copy-done.10
  38.2 1.0 %join_parts.5.refs_3_.refs_4_ = bf16[2048,128]{1,0:T(8,128)(2,1)S(1)} custom-call(bf16[512,128]{1,0:T(8,128)(2,1)S(1)} %copy-done.8, bf16[512,128]{1,0:T(8,128)(2,1)S(1)} %copy-done.10, bf16[512,128]{1,0:T(8,128)(2,1)} %collective-permute-done.8.refs_2_, bf16[512,128]{1,0:T(8,128)(2,1)} %collective-permute-done.9.refs_3_), custom_call_target="tpu_custom_call" | custom-call | flops 1000 | bytes 1048576 | tf_op jit(solution)/shard_map/join_parts/pallas_call | solution.py:256
  39.2 0.6 collective-permute-start.14
  39.8 0.5 collective-permute-start.13
  40.3 0.5 collective-permute-start.15
  40.8 1.7 %collective-permute-start.16 = (bf16[1024,128]{1,0:T(8,128)(2,1)S(1)}, bf16[1024,128]{1,0:T(8,128)(2,1)S(1)}, u32[]{:S(2)}, u32[]{:S(2)}) collective-permute-start(bf16[1024,128]{1,0:T(8,128)(2,1)S(1)} %join_parts.3.refs_8_), channel_id=1, source_target_pairs={{0,8},{1,9},{2,10},{3,11},{4,12},{5,13},{6,14},{7,15},{8,0},{9,1},... | collective-permute-start | bytes 786440 | tf_op jit(solution)/shard_map/ppermute | solution.py:26
  42.5 1.0 %copy-done.5 = f32[1024,128]{1,0:T(8,128)S(1)} copy-done((f32[1024,128]{1,0:T(8,128)S(1)}, f32[1024,128]{1,0:T(8,128)}, u32[]{:S(2)}) %copy-start.5) | copy-done | bytes 524312
  43.6 4.6 %hidden_last.1 = (bf16[1024,128]{1,0:T(8,128)(2,1)}, f32[1024,128]{1,0:T(8,128)S(1)}) custom-call(s32[1]{0:T(128)} %bitcast.refs_0_.me_ref.refs_3_, s32[256]{0:T(256)S(1)} %copy-done.11, bf16[8192,128]{1,0:T(8,128)(2,1)S(1)} %relayout.2.refs_2_.refs_7_.w_ref, bf16[2048,128]{1,0:T(8,128)(2,1)} %collective-permute-done.10.refs_3_.refs_5_, ...), custom_call_target="tpu_custom_call" | custom-call | flops 536870912 | bytes 6291456 | tf_op jit(solution)/shard_map/hidden_last/pallas_call | solution.py:203
  48.2 2.6 %upper.2.refs_4_ = f32[1024,128]{1,0:T(8,128)S(1)} custom-call(s32[1]{0:T(128)} %bitcast.refs_0_.me_ref.refs_3_, s32[256]{0:T(256)S(1)} %copy-done.12, bf16[8192,128]{1,0:T(8,128)(2,1)S(1)} %copy-done.1, bf16[2048,128]{1,0:T(8,128)(2,1)S(1)} %join_parts.5.refs_3_.refs_4_, bf16[2048,128]{1,0:T(8,128)(2,1)S(1)} %collective-permute-done.14.refs_4_.refs_6_), custom_call_target="tpu_custom_call" | custom-call | flops 536870912 | bytes 6291456 | tf_op jit(solution)/shard_map/upper/pallas_call | solution.py:203
  50.8 4.3 %collective-permute-done.16.refs_10_ = bf16[1024,128]{1,0:T(8,128)(2,1)S(1)} collective-permute-done((bf16[1024,128]{1,0:T(8,128)(2,1)S(1)}, bf16[1024,128]{1,0:T(8,128)(2,1)S(1)}, u32[]{:S(2)}, u32[]{:S(2)}) %collective-permute-start.16) | collective-permute-done | bytes 262176 | tf_op jit(solution)/shard_map/ppermute | solution.py:26
  55.1 1.6 %upper.3.refs_4_ = f32[1024,128]{1,0:T(8,128)S(1)} custom-call(s32[1]{0:T(128)} %bitcast.refs_0_.me_ref.refs_3_, s32[256]{0:T(256)S(1)} %copy-done.12, bf16[8192,128]{1,0:T(8,128)(2,1)S(1)} %copy-done.1, bf16[2048,128]{1,0:T(8,128)(2,1)S(1)} %collective-permute-done.13.refs_3_.refs_5_, f32[1024,128]{1,0:T(8,128)S(1)} %upper.2.refs_4_), custom_call_target="tpu_custom_call" | custom-call | flops 536870912 | bytes 6291456 | tf_op jit(solution)/shard_map/upper/pallas_call | solution.py:203
  56.7 0.3 collective-permute-done.17.refs_3_.refs_7_
  57.0 2.5 %upper_last.1 = (bf16[1024,128]{1,0:T(8,128)(2,1)S(1)}, bf16[2048,128]{1,0:T(8,128)(2,1)S(1)}) custom-call(s32[1]{0:T(128)} %bitcast.refs_0_.me_ref.refs_3_, s32[256]{0:T(256)S(1)} %copy-done.12, bf16[8192,128]{1,0:T(8,128)(2,1)S(1)} %copy-done.1, bf16[2048,128]{1,0:T(8,128)(2,1)S(1)} %collective-permute-done.17.refs_3_.refs_7_, ...), custom_call_target="tpu_custom_call" | custom-call | flops 536870912 | bytes 6291456 | tf_op jit(solution)/shard_map/upper_last/pallas_call | solution.py:203
  59.5 0.3 collective-permute-start.18
  59.8 0.3 collective-permute-start.28
  60.1 1.4 %input_grad_part.2.terms_ref = f32[2048,128]{1,0:T(8,128)S(1)} custom-call(s32[1]{0:T(128)} %bitcast.refs_0_.me_ref.refs_3_, s32[256]{0:T(256)S(1)} %copy-done.11, bf16[8192,128]{1,0:T(8,128)(2,1)S(1)} %relayout.2.refs_2_.refs_7_.w_ref, bf16[1024,128]{1,0:T(8,128)(2,1)S(1)} %get-tuple-element.90.s_ref.refs_12_), custom_call_target="tpu_custom_call" | custom-call | flops 536870912 | bytes 6291456 | tf_op jit(solution)/shard_map/input_grad_part/pallas_call | solution.py:243
  61.5 0.0 copy-start.6
  61.5 0.0 collective-permute-done.18.refs_0_
  61.5 0.1 add_stage.2
  61.6 1.6 %collective-permute-start.19 = (bf16[2048,128]{1,0:T(8,128)(2,1)S(1)}, bf16[2048,128]{1,0:T(8,128)(2,1)S(1)}, u32[]{:S(2)}, u32[]{:S(2)}) collective-permute-start(bf16[2048,128]{1,0:T(8,128)(2,1)S(1)} %add_stage.2), channel_id=1, source_target_pairs={{0,2},{1,3},{2,0},{3,1},{4,6},{5,7},{6,4},{7,5},{8,10},{9,11},{10,... | collective-permute-start | bytes 1572872 | tf_op jit(solution)/shard_map/ppermute | solution.py:26
  63.2 1.5 %collective-permute-start.21 = (bf16[1024,128]{1,0:T(8,128)(2,1)S(1)}, bf16[1024,128]{1,0:T(8,128)(2,1)S(1)}, u32[]{:S(2)}, u32[]{:S(2)}) collective-permute-start(bf16[1024,128]{1,0:T(8,128)(2,1)S(1)} %get-tuple-element.90.s_ref.refs_12_), channel_id=1, source_target_pairs={{0,16},{16,0},{1,17},{17,1},{2,18},{18,2},{3,19},{19,3},{4,20},{20... | collective-permute-start | bytes 786440 | tf_op jit(solution)/shard_map/ppermute | solution.py:26
  64.7 1.3 %collective-permute-start.20 = (bf16[1024,128]{1,0:T(8,128)(2,1)S(1)}, bf16[1024,128]{1,0:T(8,128)(2,1)S(1)}, u32[]{:S(2)}, u32[]{:S(2)}) collective-permute-start(bf16[1024,128]{1,0:T(8,128)(2,1)S(1)} %join_parts.3.refs_8_), channel_id=1, source_target_pairs={{0,12},{1,13},{2,14},{3,15},{4,8},{5,9},{6,10},{7,11},{8,4},{9,5},... | collective-permute-start | bytes 786440 | tf_op jit(solution)/shard_map/ppermute | solution.py:26
  66.0 1.6 %input_grad_part.3 = (bf16[2048,128]{1,0:T(8,128)(2,1)S(1)}, f32[2048,128]{1,0:T(8,128)S(1)}) custom-call(s32[1]{0:T(128)} %bitcast.refs_0_.me_ref.refs_3_, s32[256]{0:T(256)S(1)} %copy-done.11, bf16[8192,128]{1,0:T(8,128)(2,1)S(1)} %relayout.2.refs_2_.refs_7_.w_ref, bf16[1024,128]{1,0:T(8,128)(2,1)S(1)} %get-tuple-element.90.s_ref.refs_12_), custom_call_target="tpu_custom_call" | custom-call | flops 536870912 | bytes 6291456 | tf_op jit(solution)/shard_map/input_grad_part/pallas_call | solution.py:243
  67.7 0.1 collective-permute-start.22
  67.8 0.5 collective-permute-start.26
  68.3 3.1 %collective-permute-done.21.refs_13_ = bf16[1024,128]{1,0:T(8,128)(2,1)S(1)} collective-permute-done((bf16[1024,128]{1,0:T(8,128)(2,1)S(1)}, bf16[1024,128]{1,0:T(8,128)(2,1)S(1)}, u32[]{:S(2)}, u32[]{:S(2)}) %collective-permute-start.21) | collective-permute-done | bytes 262176 | tf_op jit(solution)/shard_map/ppermute | solution.py:26
  71.3 3.1 %collective-permute-done.20.refs_11_ = bf16[1024,128]{1,0:T(8,128)(2,1)S(1)} collective-permute-done((bf16[1024,128]{1,0:T(8,128)(2,1)S(1)}, bf16[1024,128]{1,0:T(8,128)(2,1)S(1)}, u32[]{:S(2)}, u32[]{:S(2)}) %collective-permute-start.20) | collective-permute-done | bytes 262176 | tf_op jit(solution)/shard_map/ppermute | solution.py:26
  74.4 1.3 %collective-permute-done.19.refs_0_ = bf16[2048,128]{1,0:T(8,128)(2,1)S(1)} collective-permute-done((bf16[2048,128]{1,0:T(8,128)(2,1)S(1)}, bf16[2048,128]{1,0:T(8,128)(2,1)S(1)}, u32[]{:S(2)}, u32[]{:S(2)}) %collective-permute-start.19) | collective-permute-done | bytes 524320 | tf_op jit(solution)/shard_map/ppermute | solution.py:26
  75.7 0.5 collective-permute-done.29.refs_13_
  76.2 1.1 %collective-permute-start.32 = (bf16[1024,128]{1,0:T(8,128)(2,1)S(1)}, bf16[1024,128]{1,0:T(8,128)(2,1)S(1)}, u32[]{:S(2)}, u32[]{:S(2)}) collective-permute-start(bf16[1024,128]{1,0:T(8,128)(2,1)S(1)} %copy-done.6), channel_id=1, source_target_pairs={{0,16},{16,0},{1,17},{17,1},{2,18},{18,2},{3,19},{19,3},{4,20},{20... | collective-permute-start | bytes 786440 | tf_op jit(solution)/shard_map/ppermute | solution.py:26
  77.3 0.2 collective-permute-start.31
  77.4 0.2 add_stage.3
  77.6 3.1 %collective-permute-start.23 = (bf16[512,128]{1,0:T(8,128)(2,1)S(1)}, bf16[512,128]{1,0:T(8,128)(2,1)S(1)}, u32[]{:S(2)}, u32[]{:S(2)}) collective-permute-start(bf16[512,128]{1,0:T(8,128)(2,1)S(1)} %get-tuple-element.96), channel_id=1, source_target_pairs={{0,4},{1,5},{2,6},{3,7},{4,0},{5,1},{6,2},{7,3},{8,12},{9,13},{10,... | collective-permute-start | bytes 393224 | tf_op jit(solution)/shard_map/ppermute | solution.py:26
  80.7 1.1 %collective-permute-start.24 = (bf16[512,128]{1,0:T(8,128)(2,1)S(1)}, bf16[512,128]{1,0:T(8,128)(2,1)S(1)}, u32[]{:S(2)}, u32[]{:S(2)}) collective-permute-start(bf16[512,128]{1,0:T(8,128)(2,1)S(1)} %get-tuple-element.97), channel_id=1, source_target_pairs={{0,8},{1,9},{2,10},{3,11},{4,12},{5,13},{6,14},{7,15},{8,0},{9,1},... | collective-permute-start | bytes 393224 | tf_op jit(solution)/shard_map/ppermute | solution.py:26
  81.9 1.4 %collective-permute-start.25 = (bf16[512,128]{1,0:T(8,128)(2,1)S(1)}, bf16[512,128]{1,0:T(8,128)(2,1)S(1)}, u32[]{:S(2)}, u32[]{:S(2)}) collective-permute-start(bf16[512,128]{1,0:T(8,128)(2,1)S(1)} %get-tuple-element.98), channel_id=1, source_target_pairs={{0,12},{1,13},{2,14},{3,15},{4,8},{5,9},{6,10},{7,11},{8,4},{9,5},... | collective-permute-start | bytes 393224 | tf_op jit(solution)/shard_map/ppermute | solution.py:26
  83.3 5.3 %grads_up.1 = bf16[160,4096]{1,0:T(8,128)(2,1)} custom-call(s32[264]{0:T(512)S(1)} %copy-done.14, s32[2]{0:T(128)S(1)} %copy-done.15, s32[256]{0:T(256)S(1)} %copy-done.11, s32[1]{0:T(128)} %bitcast.refs_0_.me_ref.refs_3_, bf16[2048,128]{1,0:T(8,128)(2,1)S(1)} %join_parts.4.refs_3_.refs_4_, bf16[2048,128]{1,0:T(8,128)(2,1)} %collective-permute-done.10.refs_3_.refs_5_, ...), custom_call_target="tpu_custom_call" | custom-call | flops 536870912 | bytes 6291456 | tf_op jit(solution)/shard_map/grads_up/pallas_call | solution.py:404
  88.6 5.3 %grads_down.1 = bf16[160,4096]{1,0:T(8,128)(2,1)} custom-call(s32[264]{0:T(512)S(1)} %copy-done.13, s32[2]{0:T(128)S(1)} %copy-done.15, s32[256]{0:T(256)S(1)} %copy-done.12, s32[1]{0:T(128)} %bitcast.refs_0_.me_ref.refs_3_, bf16[2048,128]{1,0:T(8,128)(2,1)S(1)} %join_parts.5.refs_3_.refs_4_, bf16[2048,128]{1,0:T(8,128)(2,1)S(1)} %collective-permute-done.13.refs_3_.refs_5_, ...), custom_call_target="tpu_custom_call" | custom-call | flops 536870912 | bytes 6291456 | tf_op jit(solution)/shard_map/grads_down/pallas_call | solution.py:404
  93.9 0.7 add_last.1
  (52 shorter events, 0.2 us)
Async XLA Ops:
  0.6 8.9 %collective-permute-start = (bf16[512,128]{1,0:T(8,128)(2,1)}, bf16[512,128]{1,0:T(8,128)(2,1)S(1)}, u32[]{:S(2)}, u32[]{:S(2)}) collective-permute-start(bf16[512,128]{1,0:T(8,128)(2,1)} %refs_0_), channel_id=1, source_target_pairs={{0,4},{1,5},{2,6},{3,7},{4,0},{5,1},{6,2},{7,3},{8,12},{9,13},{10,... | collective-permute-start | bytes 393224 | tf_op jit(solution)/shard_map/ppermute | solution.py:26
  3.7 13.2 %collective-permute-start.1 = (bf16[512,128]{1,0:T(8,128)(2,1)}, bf16[512,128]{1,0:T(8,128)(2,1)S(1)}, u32[]{:S(2)}, u32[]{:S(2)}) collective-permute-start(bf16[512,128]{1,0:T(8,128)(2,1)} %refs_0_), channel_id=1, source_target_pairs={{0,8},{1,9},{2,10},{3,11},{4,12},{5,13},{6,14},{7,15},{8,0},{9,1},... | collective-permute-start | bytes 393224 | tf_op jit(solution)/shard_map/ppermute | solution.py:26
  6.3 10.6 %collective-permute-start.2 = (bf16[512,128]{1,0:T(8,128)(2,1)}, bf16[512,128]{1,0:T(8,128)(2,1)S(1)}, u32[]{:S(2)}, u32[]{:S(2)}) collective-permute-start(bf16[512,128]{1,0:T(8,128)(2,1)} %refs_0_), channel_id=1, source_target_pairs={{0,12},{1,13},{2,14},{3,15},{4,8},{5,9},{6,10},{7,11},{8,4},{9,5},... | collective-permute-start | bytes 393224 | tf_op jit(solution)/shard_map/ppermute | solution.py:26
  6.3 10.6 %collective-permute-start.3 = (bf16[512,128]{1,0:T(8,128)(2,1)}, bf16[512,128]{1,0:T(8,128)(2,1)S(1)}, u32[]{:S(2)}, u32[]{:S(2)}) collective-permute-start(bf16[512,128]{1,0:T(8,128)(2,1)} %refs_0_.1), channel_id=1, source_target_pairs={{0,16},{16,0},{1,17},{17,1},{2,18},{18,2},{3,19},{19,3},{4,20},{20... | collective-permute-start | bytes 393224 | tf_op jit(solution)/shard_map/ppermute | solution.py:26
  8.0 8.9 %collective-permute-start.4 = (bf16[512,128]{1,0:T(8,128)(2,1)}, bf16[512,128]{1,0:T(8,128)(2,1)S(1)}, u32[]{:S(2)}, u32[]{:S(2)}) collective-permute-start(bf16[512,128]{1,0:T(8,128)(2,1)} %refs_0_.1), channel_id=1, source_target_pairs={{0,18},{1,19},{2,16},{3,17},{4,22},{5,23},{6,20},{7,21},{8,26},{9,... | collective-permute-start | bytes 393224 | tf_op jit(solution)/shard_map/ppermute | solution.py:36
  9.5 7.8 %collective-permute-start.5 = (bf16[512,128]{1,0:T(8,128)(2,1)}, bf16[512,128]{1,0:T(8,128)(2,1)S(1)}, u32[]{:S(2)}, u32[]{:S(2)}) collective-permute-start(bf16[512,128]{1,0:T(8,128)(2,1)} %refs_0_.1), channel_id=1, source_target_pairs={{0,4},{1,5},{2,6},{3,7},{4,0},{5,1},{6,2},{7,3},{8,12},{9,13},{10,... | collective-permute-start | bytes 393224 | tf_op jit(solution)/shard_map/ppermute | solution.py:26
  10.2 1.6 %copy-start.2 = (bf16[256,4096]{1,0:T(8,128)(2,1)S(1)}, bf16[256,4096]{1,0:T(8,128)(2,1)}, u32[]{:S(2)}) copy-start(bf16[256,4096]{1,0:T(8,128)(2,1)} %src.1) | copy-start | bytes 6291460
  11.8 6.2 %copy-start.7 = (bf16[512,128]{1,0:T(8,128)(2,1)S(1)}, bf16[512,128]{1,0:T(8,128)(2,1)}, u32[]{:S(2)}) copy-start(bf16[512,128]{1,0:T(8,128)(2,1)} %refs_0_) | copy-start | bytes 393220
  11.8 11.0 %copy-start.8 = (bf16[512,128]{1,0:T(8,128)(2,1)S(1)}, bf16[512,128]{1,0:T(8,128)(2,1)}, u32[]{:S(2)}) copy-start(bf16[512,128]{1,0:T(8,128)(2,1)} %refs_0_.1) | copy-start | bytes 393220
  11.8 13.7 %copy-start.11 = (s32[256]{0:T(256)S(1)}, s32[256]{0:T(256)}, u32[]{:S(2)}) copy-start(s32[256]{0:T(256)} %refs_2_.2) | copy-start | bytes 3076
  17.3 0.7 copy-start.9
  18.0 7.1 %collective-permute-start.11 = (bf16[2048,128]{1,0:T(8,128)(2,1)S(1)}, bf16[2048,128]{1,0:T(8,128)(2,1)S(1)}, u32[]{:S(2)}, u32[]{:S(2)}) collective-permute-start(bf16[2048,128]{1,0:T(8,128)(2,1)S(1)} %join_parts.4.refs_3_.refs_4_), channel_id=1, source_target_pairs={{0,1},{1,0},{2,3},{3,2},{4,5},{5,4},{6,7},{7,6},{8,9},{9,8},{10,11... | collective-permute-start | bytes 1572872 | tf_op jit(solution)/shard_map/ppermute | solution.py:26
  18.1 19.1 %collective-permute-start.7 = (bf16[2048,128]{1,0:T(8,128)(2,1)S(1)}, bf16[2048,128]{1,0:T(8,128)(2,1)}, u32[]{:S(2)}, u32[]{:S(2)}) collective-permute-start(bf16[2048,128]{1,0:T(8,128)(2,1)S(1)} %join_parts.4.refs_3_.refs_4_), channel_id=1, source_target_pairs={{0,16},{16,0},{1,17},{17,1},{2,18},{18,2},{3,19},{19,3},{4,20},{20... | collective-permute-start | bytes 1572872 | tf_op jit(solution)/shard_map/ppermute | solution.py:26
  19.7 17.5 %collective-permute-start.10 = (bf16[2048,128]{1,0:T(8,128)(2,1)S(1)}, bf16[2048,128]{1,0:T(8,128)(2,1)}, u32[]{:S(2)}, u32[]{:S(2)}) collective-permute-start(bf16[2048,128]{1,0:T(8,128)(2,1)S(1)} %join_parts.4.refs_3_.refs_4_), channel_id=1, source_target_pairs={{0,2},{1,3},{2,0},{3,1},{4,6},{5,7},{6,4},{7,5},{8,10},{9,11},{10,... | collective-permute-start | bytes 1572872 | tf_op jit(solution)/shard_map/ppermute | solution.py:26
  21.0 16.2 %collective-permute-start.6 = (bf16[1024,128]{1,0:T(8,128)(2,1)S(1)}, bf16[1024,128]{1,0:T(8,128)(2,1)}, u32[]{:S(2)}, u32[]{:S(2)}) collective-permute-start(bf16[1024,128]{1,0:T(8,128)(2,1)S(1)} %join_parts.3.refs_8_), channel_id=1, source_target_pairs={{0,4},{1,5},{2,6},{3,7},{4,0},{5,1},{6,2},{7,3},{8,12},{9,13},{10,... | collective-permute-start | bytes 786440 | tf_op jit(solution)/shard_map/ppermute | solution.py:26
  22.8 6.5 %copy-start.3 = (bf16[256,4096]{1,0:T(8,128)(2,1)S(1)}, bf16[256,4096]{1,0:T(8,128)(2,1)}, u32[]{:S(2)}) copy-start(bf16[256,4096]{1,0:T(8,128)(2,1)} %src.2) | copy-start | bytes 6291460
  22.8 11.8 %collective-permute-start.8 = (bf16[512,128]{1,0:T(8,128)(2,1)S(1)}, bf16[512,128]{1,0:T(8,128)(2,1)}, u32[]{:S(2)}, u32[]{:S(2)}) collective-permute-start(bf16[512,128]{1,0:T(8,128)(2,1)S(1)} %copy-done.8), channel_id=1, source_target_pairs={{0,8},{1,9},{2,10},{3,11},{4,12},{5,13},{6,14},{7,15},{8,0},{9,1},... | collective-permute-start | bytes 393224 | tf_op jit(solution)/shard_map/ppermute | solution.py:26
  25.1 12.1 %collective-permute-start.9 = (bf16[512,128]{1,0:T(8,128)(2,1)S(1)}, bf16[512,128]{1,0:T(8,128)(2,1)}, u32[]{:S(2)}, u32[]{:S(2)}) collective-permute-start(bf16[512,128]{1,0:T(8,128)(2,1)S(1)} %copy-done.8), channel_id=1, source_target_pairs={{0,12},{1,13},{2,14},{3,15},{4,8},{5,9},{6,10},{7,11},{8,4},{9,5},... | collective-permute-start | bytes 393224 | tf_op jit(solution)/shard_map/ppermute | solution.py:26
  28.5 0.8 copy-start.4
  30.8 1.3 %copy-start = (bf16[8192,128]{1,0:T(8,128)(2,1)}, bf16[8192,128]{1,0:T(8,128)(2,1)S(1)}, u32[]{:S(2)}) copy-start(bf16[8192,128]{1,0:T(8,128)(2,1)S(1)} %relayout.3.refs_2_) | copy-start | bytes 6291460
  37.2 5.3 %collective-permute-start.12 = (bf16[2048,128]{1,0:T(8,128)(2,1)}, bf16[2048,128]{1,0:T(8,128)(2,1)S(1)}, u32[]{:S(2)}, u32[]{:S(2)}) collective-permute-start(bf16[2048,128]{1,0:T(8,128)(2,1)} %collective-permute-done.10.refs_3_.refs_5_), channel_id=1, source_target_pairs={{0,1},{1,0},{2,3},{3,2},{4,5},{5,4},{6,7},{7,6},{8,9},{9,8},{10,11... | collective-permute-start | bytes 1572872 | tf_op jit(solution)/shard_map/ppermute | solution.py:26
  37.3 0.9 copy-start.10
  38.2 10.0 %copy-start.12 = (s32[256]{0:T(256)S(1)}, s32[256]{0:T(256)}, u32[]{:S(2)}) copy-start(s32[256]{0:T(256)} %refs_2_.3) | copy-start | bytes 3076
  39.2 9.0 %copy-start.1 = (bf16[8192,128]{1,0:T(8,128)(2,1)S(1)}, bf16[8192,128]{1,0:T(8,128)(2,1)}, u32[]{:S(2)}) copy-start(bf16[8192,128]{1,0:T(8,128)(2,1)} %copy-done) | copy-start | bytes 6291460
  39.2 9.0 %collective-permute-start.14 = (bf16[2048,128]{1,0:T(8,128)(2,1)S(1)}, bf16[2048,128]{1,0:T(8,128)(2,1)S(1)}, u32[]{:S(2)}, u32[]{:S(2)}) collective-permute-start(bf16[2048,128]{1,0:T(8,128)(2,1)S(1)} %join_parts.5.refs_3_.refs_4_), channel_id=1, source_target_pairs={{0,1},{1,0},{2,3},{3,2},{4,5},{5,4},{6,7},{7,6},{8,9},{9,8},{10,11... | collective-permute-start | bytes 1572872 | tf_op jit(solution)/shard_map/ppermute | solution.py:26
  39.8 15.3 %collective-permute-start.13 = (bf16[2048,128]{1,0:T(8,128)(2,1)S(1)}, bf16[2048,128]{1,0:T(8,128)(2,1)S(1)}, u32[]{:S(2)}, u32[]{:S(2)}) collective-permute-start(bf16[2048,128]{1,0:T(8,128)(2,1)S(1)} %join_parts.5.refs_3_.refs_4_), channel_id=1, source_target_pairs={{0,2},{1,3},{2,0},{3,1},{4,6},{5,7},{6,4},{7,5},{8,10},{9,11},{10,... | collective-permute-start | bytes 1572872 | tf_op jit(solution)/shard_map/ppermute | solution.py:26
  40.3 14.8 %collective-permute-start.15 = (bf16[2048,128]{1,0:T(8,128)(2,1)}, bf16[2048,128]{1,0:T(8,128)(2,1)S(1)}, u32[]{:S(2)}, u32[]{:S(2)}) collective-permute-start(bf16[2048,128]{1,0:T(8,128)(2,1)} %collective-permute-done.10.refs_3_.refs_5_), channel_id=1, source_target_pairs={{0,16},{16,0},{1,17},{17,1},{2,18},{18,2},{3,19},{19,3},{4,20},{20... | collective-permute-start | bytes 1572872 | tf_op jit(solution)/shard_map/ppermute | solution.py:26
  40.8 14.2 %collective-permute-start.16 = (bf16[1024,128]{1,0:T(8,128)(2,1)S(1)}, bf16[1024,128]{1,0:T(8,128)(2,1)S(1)}, u32[]{:S(2)}, u32[]{:S(2)}) collective-permute-start(bf16[1024,128]{1,0:T(8,128)(2,1)S(1)} %join_parts.3.refs_8_), channel_id=1, source_target_pairs={{0,8},{1,9},{2,10},{3,11},{4,12},{5,13},{6,14},{7,15},{8,0},{9,1},... | collective-permute-start | bytes 786440 | tf_op jit(solution)/shard_map/ppermute | solution.py:26
  42.5 1.0 %copy-start.5 = (f32[1024,128]{1,0:T(8,128)S(1)}, f32[1024,128]{1,0:T(8,128)}, u32[]{:S(2)}) copy-start(f32[1024,128]{1,0:T(8,128)} %copy-done.4) | copy-start | bytes 1572868
  55.1 1.9 %collective-permute-start.17 = (bf16[2048,128]{1,0:T(8,128)(2,1)S(1)}, bf16[2048,128]{1,0:T(8,128)(2,1)S(1)}, u32[]{:S(2)}, u32[]{:S(2)}) collective-permute-start(bf16[2048,128]{1,0:T(8,128)(2,1)S(1)} %collective-permute-done.13.refs_3_.refs_5_), channel_id=1, source_target_pairs={{0,1},{1,0},{2,3},{3,2},{4,5},{5,4},{6,7},{7,6},{8,9},{9,8},{10,11... | collective-permute-start | bytes 1572872 | tf_op jit(solution)/shard_map/ppermute | solution.py:26
  59.5 2.0 %collective-permute-start.18 = (bf16[2048,128]{1,0:T(8,128)(2,1)S(1)}, bf16[2048,128]{1,0:T(8,128)(2,1)S(1)}, u32[]{:S(2)}, u32[]{:S(2)}) collective-permute-start(bf16[2048,128]{1,0:T(8,128)(2,1)S(1)} %get-tuple-element.88), channel_id=1, source_target_pairs={{0,1},{1,0},{2,3},{3,2},{4,5},{5,4},{6,7},{7,6},{8,9},{9,8},{10,11... | collective-permute-start | bytes 1572872 | tf_op jit(solution)/shard_map/ppermute | solution.py:26
  59.8 8.0 %collective-permute-start.28 = (bf16[1024,128]{1,0:T(8,128)(2,1)S(1)}, bf16[1024,128]{1,0:T(8,128)(2,1)S(1)}, u32[]{:S(2)}, u32[]{:S(2)}) collective-permute-start(bf16[1024,128]{1,0:T(8,128)(2,1)S(1)} %join_parts.3.refs_8_), channel_id=1, source_target_pairs={{0,1},{1,0},{2,3},{3,2},{4,5},{5,4},{6,7},{7,6},{8,9},{9,8},{10,11... | collective-permute-start | bytes 786440 | tf_op jit(solution)/shard_map/ppermute | solution.py:26
  61.5 14.7 %copy-start.6 = (bf16[1024,128]{1,0:T(8,128)(2,1)S(1)}, bf16[1024,128]{1,0:T(8,128)(2,1)}, u32[]{:S(2)}) copy-start(bf16[1024,128]{1,0:T(8,128)(2,1)} %get-tuple-element.108.refs_16_) | copy-start | bytes 786436
  61.6 14.1 %collective-permute-start.19 = (bf16[2048,128]{1,0:T(8,128)(2,1)S(1)}, bf16[2048,128]{1,0:T(8,128)(2,1)S(1)}, u32[]{:S(2)}, u32[]{:S(2)}) collective-permute-start(bf16[2048,128]{1,0:T(8,128)(2,1)S(1)} %add_stage.2), channel_id=1, source_target_pairs={{0,2},{1,3},{2,0},{3,1},{4,6},{5,7},{6,4},{7,5},{8,10},{9,11},{10,... | collective-permute-start | bytes 1572872 | tf_op jit(solution)/shard_map/ppermute | solution.py:26
  63.2 8.1 %collective-permute-start.21 = (bf16[1024,128]{1,0:T(8,128)(2,1)S(1)}, bf16[1024,128]{1,0:T(8,128)(2,1)S(1)}, u32[]{:S(2)}, u32[]{:S(2)}) collective-permute-start(bf16[1024,128]{1,0:T(8,128)(2,1)S(1)} %get-tuple-element.90.s_ref.refs_12_), channel_id=1, source_target_pairs={{0,16},{16,0},{1,17},{17,1},{2,18},{18,2},{3,19},{19,3},{4,20},{20... | collective-permute-start | bytes 786440 | tf_op jit(solution)/shard_map/ppermute | solution.py:26
  64.7 18.6 %copy-start.14 = (s32[264]{0:T(512)S(1)}, s32[264]{0:T(512)}, u32[]{:S(2)}) copy-start(s32[264]{0:T(512)} %get-tuple-element.99.refs_0_) | copy-start | bytes 3172
  64.7 18.6 %copy-start.15 = (s32[2]{0:T(128)S(1)}, s32[2]{0:T(128)}, u32[]{:S(2)}) copy-start(s32[2]{0:T(128)} %get-tuple-element.100.refs_1_) | copy-start | bytes 28
  64.7 9.7 %collective-permute-start.20 = (bf16[1024,128]{1,0:T(8,128)(2,1)S(1)}, bf16[1024,128]{1,0:T(8,128)(2,1)S(1)}, u32[]{:S(2)}, u32[]{:S(2)}) collective-permute-start(bf16[1024,128]{1,0:T(8,128)(2,1)S(1)} %join_parts.3.refs_8_), channel_id=1, source_target_pairs={{0,12},{1,13},{2,14},{3,15},{4,8},{5,9},{6,10},{7,11},{8,4},{9,5},... | collective-permute-start | bytes 786440 | tf_op jit(solution)/shard_map/ppermute | solution.py:26
  67.7 9.6 %collective-permute-start.22 = (bf16[2048,128]{1,0:T(8,128)(2,1)S(1)}, bf16[2048,128]{1,0:T(8,128)(2,1)S(1)}, u32[]{:S(2)}, u32[]{:S(2)}) collective-permute-start(bf16[2048,128]{1,0:T(8,128)(2,1)S(1)} %get-tuple-element.94), channel_id=1, source_target_pairs={{0,1},{1,0},{2,3},{3,2},{4,5},{5,4},{6,7},{7,6},{8,9},{9,8},{10,11... | collective-permute-start | bytes 1572872 | tf_op jit(solution)/shard_map/ppermute | solution.py:26
  67.8 9.8 %collective-permute-start.26 = (bf16[2048,128]{1,0:T(8,128)(2,1)}, bf16[2048,128]{1,0:T(8,128)(2,1)S(1)}, u32[]{:S(2)}, u32[]{:S(2)}) collective-permute-start(bf16[2048,128]{1,0:T(8,128)(2,1)} %collective-permute-done.7.refs_8_), channel_id=1, source_target_pairs={{0,1},{1,0},{2,3},{3,2},{4,5},{5,4},{6,7},{7,6},{8,9},{9,8},{10,11... | collective-permute-start | bytes 1572872 | tf_op jit(solution)/shard_map/ppermute | solution.py:26
  71.3 10.5 %collective-permute-start.27 = (bf16[2048,128]{1,0:T(8,128)(2,1)S(1)}, bf16[2048,128]{1,0:T(8,128)(2,1)S(1)}, u32[]{:S(2)}, u32[]{:S(2)}) collective-permute-start(bf16[2048,128]{1,0:T(8,128)(2,1)S(1)} %collective-permute-done.15.refs_9_), channel_id=1, source_target_pairs={{0,1},{1,0},{2,3},{3,2},{4,5},{5,4},{6,7},{7,6},{8,9},{9,8},{10,11... | collective-permute-start | bytes 1572872 | tf_op jit(solution)/shard_map/ppermute | solution.py:26
  74.4 1.7 %collective-permute-start.29 = (bf16[1024,128]{1,0:T(8,128)(2,1)}, bf16[1024,128]{1,0:T(8,128)(2,1)S(1)}, u32[]{:S(2)}, u32[]{:S(2)}) collective-permute-start(bf16[1024,128]{1,0:T(8,128)(2,1)} %collective-permute-done.6.refs_9_), channel_id=1, source_target_pairs={{0,1},{1,0},{2,3},{3,2},{4,5},{5,4},{6,7},{7,6},{8,9},{9,8},{10,11... | collective-permute-start | bytes 786440 | tf_op jit(solution)/shard_map/ppermute | solution.py:26
  75.7 5.0 %collective-permute-start.30 = (bf16[1024,128]{1,0:T(8,128)(2,1)S(1)}, bf16[1024,128]{1,0:T(8,128)(2,1)S(1)}, u32[]{:S(2)}, u32[]{:S(2)}) collective-permute-start(bf16[1024,128]{1,0:T(8,128)(2,1)S(1)} %collective-permute-done.16.refs_10_), channel_id=1, source_target_pairs={{0,1},{1,0},{2,3},{3,2},{4,5},{5,4},{6,7},{7,6},{8,9},{9,8},{10,11... | collective-permute-start | bytes 786440 | tf_op jit(solution)/shard_map/ppermute | solution.py:26
  76.2 12.4 %collective-permute-start.32 = (bf16[1024,128]{1,0:T(8,128)(2,1)S(1)}, bf16[1024,128]{1,0:T(8,128)(2,1)S(1)}, u32[]{:S(2)}, u32[]{:S(2)}) collective-permute-start(bf16[1024,128]{1,0:T(8,128)(2,1)S(1)} %copy-done.6), channel_id=1, source_target_pairs={{0,16},{16,0},{1,17},{17,1},{2,18},{18,2},{3,19},{19,3},{4,20},{20... | collective-permute-start | bytes 786440 | tf_op jit(solution)/shard_map/ppermute | solution.py:26
  77.3 11.3 %collective-permute-start.31 = (bf16[1024,128]{1,0:T(8,128)(2,1)S(1)}, bf16[1024,128]{1,0:T(8,128)(2,1)S(1)}, u32[]{:S(2)}, u32[]{:S(2)}) collective-permute-start(bf16[1024,128]{1,0:T(8,128)(2,1)S(1)} %collective-permute-done.20.refs_11_), channel_id=1, source_target_pairs={{0,1},{1,0},{2,3},{3,2},{4,5},{5,4},{6,7},{7,6},{8,9},{9,8},{10,11... | collective-permute-start | bytes 786440 | tf_op jit(solution)/shard_map/ppermute | solution.py:26
  77.6 16.3 %collective-permute-start.23 = (bf16[512,128]{1,0:T(8,128)(2,1)S(1)}, bf16[512,128]{1,0:T(8,128)(2,1)S(1)}, u32[]{:S(2)}, u32[]{:S(2)}) collective-permute-start(bf16[512,128]{1,0:T(8,128)(2,1)S(1)} %get-tuple-element.96), channel_id=1, source_target_pairs={{0,4},{1,5},{2,6},{3,7},{4,0},{5,1},{6,2},{7,3},{8,12},{9,13},{10,... | collective-permute-start | bytes 393224 | tf_op jit(solution)/shard_map/ppermute | solution.py:26
  80.7 13.2 %collective-permute-start.24 = (bf16[512,128]{1,0:T(8,128)(2,1)S(1)}, bf16[512,128]{1,0:T(8,128)(2,1)S(1)}, u32[]{:S(2)}, u32[]{:S(2)}) collective-permute-start(bf16[512,128]{1,0:T(8,128)(2,1)S(1)} %get-tuple-element.97), channel_id=1, source_target_pairs={{0,8},{1,9},{2,10},{3,11},{4,12},{5,13},{6,14},{7,15},{8,0},{9,1},... | collective-permute-start | bytes 393224 | tf_op jit(solution)/shard_map/ppermute | solution.py:26
  81.9 12.1 %collective-permute-start.25 = (bf16[512,128]{1,0:T(8,128)(2,1)S(1)}, bf16[512,128]{1,0:T(8,128)(2,1)S(1)}, u32[]{:S(2)}, u32[]{:S(2)}) collective-permute-start(bf16[512,128]{1,0:T(8,128)(2,1)S(1)} %get-tuple-element.98), channel_id=1, source_target_pairs={{0,12},{1,13},{2,14},{3,15},{4,8},{5,9},{6,10},{7,11},{8,4},{9,5},... | collective-permute-start | bytes 393224 | tf_op jit(solution)/shard_map/ppermute | solution.py:26
  83.3 5.3 %copy-start.13 = (s32[264]{0:T(512)S(1)}, s32[264]{0:T(512)}, u32[]{:S(2)}) copy-start(s32[264]{0:T(512)} %get-tuple-element.104.refs_0_) | copy-start | bytes 3172
